TPU v7x, 32 devices: a whole 2x2x4 slice. The times are simulated.
32 devices in a mesh: gx: 4 (over z), gy: 2 (over x), gz: 4 (over y, core).
Axes of the slice: x: 2, y: 2, z: 4, core: 2. Of those that a mesh axis runs over, the one named last changes fastest.
Arguments:
- adj_final: float32 [4, 5, 64, 2048], P('gx', None, None, ('gy', 'gz')), may hold values from -6 to 6
- new_states: float32 [4, 3, 5, 64, 2048], P('gx', None, None, None, ('gy', 'gz')), may hold values from -1 to 4, as said below
- old_states: float32 [4, 3, 5, 64, 2048], P('gx', None, None, None, ('gy', 'gz')), may hold values from -1 to 4, as said below
- owner_device_index: int32 [4, 4096, 1], P('gx', ('gy', 'gz')), may hold values from 0 to 7; in each aligned block of 512 rows (0 to 511, 512 to 1023, ..., all dimensions but the last counted through in order) at most 128 rows name the same one
- owner_element_index: int32 [4, 4096], P('gx', ('gy', 'gz')), may hold values from 0 to 255
- proj_blocks: float32 [4, 64, 64, 4096], P('gx', None, None, ('gy', 'gz')), may hold values from -0.2 to 0.6
Outputs:
- adj_new: float32 [4, 5, 64, 2048], P('gx', None, None, ('gy', 'gz'))
- adj_old: float32 [4, 5, 64, 2048], P('gx', None, None, ('gy', 'gz'))
Inputs may be any that keep to these rules, and one draw needn't show every extreme that they name: `owner_device_index`: in each aligned block of 512 slots (the slots of one device) no owner is named more than 128 times, a bound that some block reaches. `new_states`: variable 0 lies in 0.8 to 1.6, variables 1 to 3 in -1 to 1, variable 4 in 2.5 to 4. `old_states`: variable 0 lies in 0.8 to 1.6, variables 1 to 3 in -1 to 1, variable 4 in 2.5 to 4.
All inputs are finite; a program needn't handle non-finite values.
Results may differ from a plain program's by a relative error of at most 0.0003.
Values sent between devices are 32-bit elements; how exact they have to be, the bound alone decides.
No kernel may reach another device: no remote copies, remote signals or barrier semaphores. Data moves between devices by JAX's collectives and lax.ppermute only.
A program may use at most 128 MiB of HBM per device.

v0:
```python
import functools

import jax
import jax.numpy as jnp
import numpy as np
from jax import lax
from jax.experimental import pallas as pl
from jax.experimental.pallas import tpu as pltpu
from jax.sharding import PartitionSpec as P

ELEMENTS_Z = 64

step_rate = 0.01
lift_scale = 6.0
half_lift = 3.0
vmem_limit = 40 * 1024 * 1024
VARS = 5
LANES = 128


def shifted(value, axis, steps):
    count = lax.axis_size(axis)
    pairs = [(source, (source + steps) % count) for source in range(count)]
    return lax.ppermute(value, axis, pairs)


def lgl_matrix():
    points = np.array([-1.0, -1.0 / np.sqrt(5.0), 1.0 / np.sqrt(5.0), 1.0])
    factors = np.array(
        [np.prod([points[i] - points[j] for j in range(4) if j != i]) for i in range(4)]
    )
    deriv_table = np.zeros((4, 4))
    for i in range(4):
        for j in range(4):
            if i != j:
                deriv_table[i, j] = factors[i] / (factors[j] * (points[i] - points[j]))
    for i in range(4):
        deriv_table[i, i] = -np.sum(deriv_table[i])
    return deriv_table


face_table = lgl_matrix()
face_table[0, 0] += half_lift
face_table[3, 3] -= half_lift
assert np.max(np.abs(np.diag(face_table))) < 1e-12


def iotas():
    row = lax.broadcasted_iota(jnp.int32, (8, LANES), 0)
    lane = lax.broadcasted_iota(jnp.int32, (8, LANES), 1)
    return row, lane


def by_sublane(row, values):
    out = jnp.full((8, LANES), np.float32(values[7]))
    for s in range(6, -1, -1):
        out = jnp.where(row == s, np.float32(values[s]), out)
    return out


def tile_of(ref, v, i, j):
    return ref[v, 8 * i : 8 * i + 8, LANES * j : LANES * (j + 1)]


def primitive_state(get):
    inverse = 1.0 / get(0)
    speeds = [get(1 + d) * inverse for d in range(3)]
    kinetic = (
        get(1) * speeds[0] + get(2) * speeds[1] + get(3) * speeds[2]
    )
    energy = get(4)
    pressure = 0.4 * (energy - 0.5 * kinetic)
    return speeds, (energy + pressure) * inverse


def pull_full(speeds, enthalpy, v):
    total = v[0][4] * speeds[0] + v[1][4] * speeds[1] + v[2][4] * speeds[2]
    weight = v[0][1] + v[1][2] + v[2][3] + total
    fifth = 0.2 * weight
    pulled = []
    for d in range(3):
        part = (
            v[d][1] * speeds[0]
            + v[d][2] * speeds[1]
            + v[d][3] * speeds[2]
            + v[d][4] * enthalpy
        )
        pulled.append(part - fifth * speeds[d])
    out = [-(pulled[0] * speeds[0] + pulled[1] * speeds[1] + pulled[2] * speeds[2])]
    for j in range(3):
        moved = (
            v[0][1 + j] * speeds[0] + v[1][1 + j] * speeds[1] + v[2][1 + j] * speeds[2]
        )
        out.append(v[j][0] + moved - fifth * speeds[j] + pulled[j])
    out.append(total + 2.0 * fifth)
    return out


def pull_one(direction, speeds, enthalpy, v):
    own = speeds[direction]
    total = v[4] * own
    fifth = 0.2 * (v[1 + direction] + total)
    pulled = [-fifth * speeds[d] for d in range(3)]
    pulled[direction] = (
        v[1] * speeds[0]
        + v[2] * speeds[1]
        + v[3] * speeds[2]
        + v[4] * enthalpy
        + pulled[direction]
    )
    out = [-(pulled[0] * speeds[0] + pulled[1] * speeds[1] + pulled[2] * speeds[2])]
    for j in range(3):
        moved = v[1 + j] * own - fifth * speeds[j] + pulled[j]
        out.append(v[0] + moved if j == direction else moved)
    out.append(total + 2.0 * fifth)
    return out


def local_kernel(scale, extras, halves, *refs):
    state_ref, w_ref = refs[0], refs[1]
    extra_refs = refs[2 : 2 + len(extras)]
    out_ref = refs[2 + len(extras)]
    row, lane = iotas()
    low_half_rows = row < 4
    low_half_lanes = lane < 64
    within = row % 4
    z_first = lane % ELEMENTS_Z == 0
    z_last = lane % ELEMENTS_Z == ELEMENTS_Z - 1
    z_shift = {}
    for k in (1, 2, 3, -1, -2, -3):
        column = [
            face_table[s % 4 - k, s % 4] if 0 <= s % 4 - k <= 3 else 0.0 for s in range(8)
        ]
        z_shift[k] = by_sublane(row, column)
    z_low = by_sublane(row, [half_lift if s % 4 == 0 else 0.0 for s in range(8)])
    z_high = by_sublane(row, [-half_lift if s % 4 == 3 else 0.0 for s in range(8)])
    zero = jnp.zeros((8, LANES), jnp.float32)

    for j in range(halves):
        for i in range(8):
            a, t = i // 2, i % 2
            other = 2 * a + 1 - t
            bs = [2 * t + s // 4 for s in range(8)]
            y_same = by_sublane(row, [face_table[2 * (1 - t) + s // 4, bs[s]] for s in range(8)])
            y_swap = by_sublane(row, [face_table[2 * t + 1 - s // 4, bs[s]] for s in range(8)])
            y_both = by_sublane(
                row, [face_table[2 * (1 - t) + 1 - s // 4, bs[s]] for s in range(8)]
            )
            y_face_rows = low_half_rows if t == 0 else jnp.logical_not(low_half_rows)
            y_sign = half_lift if t == 0 else -half_lift
            y_face = jnp.where(y_face_rows, np.float32(y_sign), 0.0)
            count = by_sublane(
                row,
                [
                    lift_scale
                    * ((a in (0, 3)) + (bs[s] in (0, 3)) + (s % 4 in (0, 3)))
                    for s in range(8)
                ],
            )
            v = [[], [], []]
            penalties = []
            for var in range(VARS):
                w = tile_of(w_ref, var, i, j)
                acc = None
                for source in range(4):
                    if source == a:
                        continue
                    term = np.float32(face_table[source, a]) * tile_of(
                        w_ref, var, 2 * source + t, j
                    )
                    acc = term if acc is None else acc + term
                v[0].append(acc)
                pair = tile_of(w_ref, var, other, j)
                pair_swapped = pltpu.roll(pair, 4, 0)
                acc = (
                    y_same * pair
                    + y_swap * pltpu.roll(w, 4, 0)
                    + y_both * pair_swapped
                )
                here = pltpu.roll(pair_swapped, 64, 1)
                if t == 0:
                    before = (
                        pltpu.roll(pltpu.roll(tile_of(w_ref, var, other, j - 1), 4, 0), 64, 1)
                        if j > 0
                        else zero
                    )
                    y_in = jnp.where(low_half_lanes, before, here)
                else:
                    after = (
                        pltpu.roll(pltpu.roll(tile_of(w_ref, var, other, j + 1), 4, 0), 64, 1)
                        if j < halves - 1
                        else zero
                    )
                    y_in = jnp.where(low_half_lanes, here, after)
                y_term = y_face * y_in
                v[1].append(acc + y_term)
                acc = None
                moved = {}
                for k in (1, 2, 3, -1, -2, -3):
                    moved[k] = pltpu.roll(w, k % 8, 0)
                    term = z_shift[k] * moved[k]
                    acc = term if acc is None else acc + term
                below = jnp.where(
                    z_first, pltpu.roll(moved[-3], 65, 1), pltpu.roll(moved[-3], 1, 1)
                )
                above = jnp.where(
                    z_last, pltpu.roll(moved[3], 63, 1), pltpu.roll(moved[3], 127, 1)
                )
                low_term = z_low * below
                high_term = z_high * above
                v[2].append(acc + low_term + high_term)
                y_jump = y_term if t == 0 else -y_term
                penalties.append(
                    count * w - 2.0 * (y_jump + (low_term - high_term))
                )
            speeds, enthalpy = primitive_state(lambda q: tile_of(state_ref, q, i, j))
            pulled = pull_full(speeds, enthalpy, v)
            for var in range(VARS):
                change = (-step_rate * scale) * (pulled[var] + penalties[var])
                base = scale * tile_of(w_ref, var, i, j)
                for ref, factor in zip(extra_refs, extras):
                    base = base + np.float32(factor) * tile_of(ref, var, i, j)
                out_ref[var, 8 * i : 8 * i + 8, LANES * j : LANES * (j + 1)] = base + change


def pack_faces(w_ref, halves, xl_ref, xu_ref, yl_ref, yu_ref):
    row, lane = iotas()
    low_rows = row < 4
    low_lanes = lane < 64
    for var in range(VARS):
        xl_ref[var] = w_ref[var, 0:16, :]
        xu_ref[var] = w_ref[var, 48:64, :]
        low = [tile_of(w_ref, var, 2 * a, 0) for a in range(4)]
        left = jnp.where(low_rows, low[0], pltpu.roll(low[1], 4, 0))
        right = jnp.where(low_rows, low[2], pltpu.roll(low[3], 4, 0))
        yl_ref[var] = jnp.where(low_lanes, left, pltpu.roll(right, 64, 1))
        high = [tile_of(w_ref, var, 2 * a + 1, halves - 1) for a in range(4)]
        left = jnp.where(low_rows, pltpu.roll(high[0], 4, 0), high[1])
        right = jnp.where(low_rows, pltpu.roll(high[2], 4, 0), high[3])
        yu_ref[var] = jnp.where(low_lanes, pltpu.roll(left, 64, 1), right)


def face_kernel(halves, w_ref, *out_refs):
    pack_faces(w_ref, halves, *out_refs)


def finish_kernel(
    scale, with_faces, halves, state_ref, base_ref, xlow_ref, xhigh_ref, ylow_ref, yhigh_ref, *outs
):
    out_ref = outs[0]
    row, lane = iotas()
    rate = np.float32(-step_rate * scale)
    y_low_mask = jnp.where(jnp.logical_and(row < 4, lane < 64), np.float32(half_lift), 0.0)
    y_high_mask = jnp.where(jnp.logical_and(row >= 4, lane >= 64), np.float32(-half_lift), 0.0)
    for j in range(halves):
        for i in range(8):
            a, t = i // 2, i % 2
            has_x = a in (0, 3)
            has_y = (t == 0 and j == 0) or (t == 1 and j == halves - 1)
            place = (slice(8 * i, 8 * i + 8), slice(LANES * j, LANES * (j + 1)))
            values = [base_ref[(var,) + place] for var in range(VARS)]
            if has_x or has_y:
                speeds, enthalpy = primitive_state(lambda q: tile_of(state_ref, q, i, j))
            if has_x:
                source = xlow_ref if a == 0 else xhigh_ref
                sign = half_lift if a == 0 else -half_lift
                got = [np.float32(sign) * tile_of(source, var, t, j) for var in range(VARS)]
                pulled = pull_one(0, speeds, enthalpy, got)
                jump = 2.0 if a == 0 else -2.0
                values = [
                    x + rate * (g - jump * q) for x, g, q in zip(values, pulled, got)
                ]
            if has_y:
                got = []
                for var in range(VARS):
                    packed = (ylow_ref if t == 0 else yhigh_ref)[var]
                    if t == 0:
                        if a >= 2:
                            packed = pltpu.roll(packed, 64, 1)
                        if a % 2 == 1:
                            packed = pltpu.roll(packed, 4, 0)
                        got.append(y_low_mask * packed)
                    else:
                        if a < 2:
                            packed = pltpu.roll(packed, 64, 1)
                        if a % 2 == 0:
                            packed = pltpu.roll(packed, 4, 0)
                        got.append(y_high_mask * packed)
                pulled = pull_one(1, speeds, enthalpy, got)
                jump = 2.0 if t == 0 else -2.0
                values = [
                    x + rate * (g - jump * q) for x, g, q in zip(values, pulled, got)
                ]
            for var in range(VARS):
                out_ref[(var,) + place] = values[var]
    if with_faces:
        pack_faces(out_ref, halves, *outs[1:])


def vmem_spec():
    return pl.BlockSpec(memory_space=pltpu.VMEM)


def params():
    return pltpu.CompilerParams(vmem_limit_bytes=vmem_limit)


def face_shapes(columns):
    return [
        jax.ShapeDtypeStruct((VARS, 16, columns), jnp.float32),
        jax.ShapeDtypeStruct((VARS, 16, columns), jnp.float32),
        jax.ShapeDtypeStruct((VARS, 8, LANES), jnp.float32),
        jax.ShapeDtypeStruct((VARS, 8, LANES), jnp.float32),
    ]


def get_faces(w):
    columns = w.shape[2]
    return pl.pallas_call(
        functools.partial(face_kernel, columns // LANES),
        out_shape=face_shapes(columns),
        in_specs=[vmem_spec()],
        out_specs=[vmem_spec()] * 4,
        compiler_params=params(),
        name="faces",
    )(w)


def exchange(faces):
    xl, xu, yl, yu = faces
    x_low = shifted(xu, "gx", 1)
    x_high = shifted(xl, "gx", -1)
    y_low = shifted(yu, ("gy", "gz"), 1)
    y_high = shifted(yl, ("gy", "gz"), -1)
    return x_low, x_high, y_low, y_high


def section(states, index, w, faces, scale, extras, with_faces):
    columns = w.shape[2]
    halves = columns // LANES
    shape = jax.ShapeDtypeStruct(w.shape, jnp.float32)
    received = exchange(faces)
    state = states[index]
    base = pl.pallas_call(
        functools.partial(local_kernel, scale, tuple(f for _, f in extras), halves),
        out_shape=shape,
        in_specs=[vmem_spec()] * (2 + len(extras)),
        out_specs=vmem_spec(),
        compiler_params=params(),
        cost_estimate=pl.CostEstimate(
            flops=400 * 64 * columns, bytes_accessed=12 * VARS * 64 * columns, transcendentals=0
        ),
        name="local_part",
    )(state, w, *[x for x, _ in extras])
    out_shape = [shape] + (face_shapes(columns) if with_faces else [])
    return pl.pallas_call(
        functools.partial(finish_kernel, scale, with_faces, halves),
        out_shape=out_shape,
        in_specs=[vmem_spec()] * 6,
        out_specs=[vmem_spec()] * len(out_shape),
        compiler_params=params(),
        name="finish",
    )(state, base, *received)


def reverse_step(states, begin, faces):
    second, *faces = section(states, 2, begin, faces, 2.0 / 3.0, [], True)
    first, *faces = section(states, 1, second, faces, 0.25, [], True)
    (result,) = section(
        states, 0, first, faces, 1.0, [(begin, 1.0 / 3.0), (second, 0.75)], False
    )
    return result


def split_three(x):
    high = x.astype(jnp.bfloat16)
    rest = x - high.astype(jnp.float32)
    middle = rest.astype(jnp.bfloat16)
    low = (rest - middle.astype(jnp.float32)).astype(jnp.bfloat16)
    return high, middle, low


def project_kernel(m_tiles, w_ref, block_ref, placing_ref, extra_ref, out_ref, held):
    step = pl.program_id(0)

    def body(n, sums):
        sums = list(sums)
        rows = [
            jnp.broadcast_to(w_ref[var, pl.ds(n, 1), :], (8, LANES)) for var in range(VARS)
        ]
        for m in range(m_tiles):
            block = block_ref[n, 8 * m : 8 * m + 8, :]
            for var in range(VARS):
                q = m * VARS + var
                sums[q] = sums[q] + block * rows[var]
        return tuple(sums)

    start = tuple(jnp.zeros((8, LANES), jnp.float32) for _ in range(m_tiles * VARS))
    sums = lax.fori_loop(0, 64, body, start, unroll=8)
    for q in range(m_tiles * VARS):
        held[step, 8 * q : 8 * q + 8, :] = sums[q]

    @pl.when(step == pl.num_programs(0) - 1)
    def _():
        total = m_tiles * VARS * 8
        result = jnp.zeros((total + 8, placing_ref.shape[1]), jnp.float32)
        for s in range(held.shape[0]):
            values = jnp.concatenate([held[s], extra_ref[:, LANES * s : LANES * (s + 1)]], axis=0)
            spot = placing_ref[LANES * s : LANES * (s + 1), :]
            for piece in split_three(values):
                result = result + jnp.dot(piece, spot, preferred_element_type=jnp.float32)
        for g in range(out_ref.shape[0]):
            out_ref[g] = result[:, LANES * g : LANES * (g + 1)]


def project(w, blocks, placing, extra, first, m_tiles):
    halves = w.shape[2] // LANES
    slots = blocks.shape[3]
    steps = slots // LANES
    rows = m_tiles * VARS * 8
    places = placing.shape[1]
    return pl.pallas_call(
        functools.partial(project_kernel, m_tiles),
        out_shape=jax.ShapeDtypeStruct((places // LANES, rows + 8, LANES), jnp.float32),
        grid=(steps,),
        in_specs=[
            pl.BlockSpec((VARS, 64, LANES), lambda s: (0, 0, lax.rem(s, halves))),
            pl.BlockSpec((None, 64, 8 * m_tiles, LANES), lambda s: (0, 0, first, s)),
            vmem_spec(),
            vmem_spec(),
        ],
        out_specs=vmem_spec(),
        scratch_shapes=[pltpu.VMEM((steps, rows, LANES), jnp.float32)],
        compiler_params=params(),
        name="project",
    )(w, blocks, placing, extra)


def receive_kernel(count, m_tiles, halves, *refs):
    incoming = refs[:count]
    out_ref = refs[count]
    columns = out_ref.shape[2]
    spots = []
    for g in range(incoming[0].shape[0]):
        rows = m_tiles * VARS * 8
        local = incoming[0][g, rows : rows + 1, :].astype(jnp.int32)
        index = lax.broadcasted_iota(jnp.int32, (columns, LANES), 0)
        spots.append((index == local).astype(jnp.float32).astype(jnp.bfloat16))
    for piece_index in range(count):
        rows = m_tiles * VARS * 8
        result = jnp.zeros((rows, columns), jnp.float32)
        for g, spot in enumerate(spots):
            for piece in split_three(incoming[piece_index][g, 0:rows, :]):
                result = result + lax.dot_general(
                    piece, spot, (((1,), (1,)), ((), ())), preferred_element_type=jnp.float32
                )
        for m in range(m_tiles):
            node = 8 * (piece_index * m_tiles + m)
            for var in range(VARS):
                q = m * VARS + var
                out_ref[var, node : node + 8, :] = result[8 * q : 8 * q + 8, :]
    pack_faces(out_ref, halves, *refs[count + 1 :])


def receive(incoming, columns, m_tiles):
    shapes = [jax.ShapeDtypeStruct((VARS, 64, columns), jnp.float32)] + face_shapes(columns)
    return pl.pallas_call(
        functools.partial(receive_kernel, len(incoming), m_tiles, columns // LANES),
        out_shape=shapes,
        in_specs=[vmem_spec()] * len(incoming),
        out_specs=[vmem_spec()] * len(shapes),
        compiler_params=params(),
        name="receive",
    )(*incoming)


def send_to_owners(values, group, capacity):
    blocks, rows, lanes = values.shape
    if capacity == lanes:
        return lax.all_to_all(values, ("gy", "gz"), split_axis=0, concat_axis=0, tiled=True)
    per = lanes // capacity
    values = values.reshape(blocks, rows, per, capacity).transpose(0, 2, 1, 3)
    values = values.reshape(group, rows, capacity)
    values = lax.all_to_all(values, ("gy", "gz"), split_axis=0, concat_axis=0, tiled=True)
    values = values.reshape(blocks, per, rows, capacity).transpose(0, 2, 1, 3)
    return values.reshape(blocks, rows, lanes)


CHUNKS = 1


def per_device(
    adj_final, new_states, old_states, owner_device_index, owner_element_index, proj_blocks
):
    columns = adj_final.shape[3]
    slots = proj_blocks.shape[3]
    group = lax.axis_size("gy") * lax.axis_size("gz")
    capacity = max(2, (2 * slots + group - 1) // group)
    target = owner_device_index[0, :, 0]
    order = jnp.arange(slots)
    earlier_same = (target[:, None] == target[None, :]) & (order[None, :] < order[:, None])
    rank_in = jnp.sum(earlier_same.astype(jnp.int32), axis=1)
    place = target * capacity + rank_in
    placing = (place[:, None] == jnp.arange(group * capacity)[None, :]).astype(jnp.bfloat16)
    extra = jnp.broadcast_to(owner_element_index.astype(jnp.float32), (8, slots))

    begin = adj_final[0]
    adj_new = reverse_step(new_states[0], begin, get_faces(begin))

    m_tiles = 8 // CHUNKS
    incoming = []
    for chunk in range(CHUNKS):
        outgoing = project(adj_new, proj_blocks, placing, extra, chunk, m_tiles)
        incoming.append(send_to_owners(outgoing, group, capacity))
    adj_proj, *faces = receive(incoming, columns, m_tiles)
    adj_old = reverse_step(old_states[0], adj_proj, faces)
    return (adj_new.reshape(adj_final.shape), adj_old.reshape(adj_final.shape))


def solution(mesh):
    in_specs = (
        P("gx", None, None, ("gy", "gz")),
        P("gx", None, None, None, ("gy", "gz")),
        P("gx", None, None, None, ("gy", "gz")),
        P("gx", ("gy", "gz"), None),
        P("gx", ("gy", "gz")),
        P("gx", None, None, ("gy", "gz")),
    )
    out_specs = (P("gx", None, None, ("gy", "gz")), P("gx", None, None, ("gy", "gz")))
    return jax.shard_map(
        per_device, mesh=mesh, in_specs=in_specs, out_specs=out_specs, check_vma=False
    )
```

profile of v0, /device:TPU:0, one launch (start us, length us, event | category | flops | bytes accessed | tf_op | source)
XLA Modules:
  0.0 86.2 jit_solution(4631073455142381452)
XLA Ops:
  0.6 1.0 %copy-done.1 = f32[1,5,64,256]{3,2,1,0:T(8,128)S(1)} copy-done((f32[1,5,64,256]{3,2,1,0:T(8,128)S(1)}, f32[1,5,64,256]{3,2,1,0:T(8,128)}, u32[]{:S(2)}) %copy-start.1) | copy-done | bytes 327704
  1.6 0.1 faces.1
  1.7 3.1 %collective-permute-start = (f32[5,16,256]{2,1,0:T(8,128)S(1)}, f32[5,16,256]{2,1,0:T(8,128)S(1)}, u32[]{:S(2)}, u32[]{:S(2)}) collective-permute-start(f32[5,16,256]{2,1,0:T(8,128)S(1)} %get-tuple-element.31), channel_id=1, source_target_pairs={{0,8},{8,16},{16,24},{24,0},{1,9},{9,17},{17,25},{25,1},{2,10},{10... | collective-permute-start | bytes 245768 | tf_op jit(solution)/shard_map/ppermute | solution.py:24
  4.8 2.1 %collective-permute-start.1 = (f32[5,16,256]{2,1,0:T(8,128)S(1)}, f32[5,16,256]{2,1,0:T(8,128)S(1)}, u32[]{:S(2)}, u32[]{:S(2)}) collective-permute-start(f32[5,16,256]{2,1,0:T(8,128)S(1)} %get-tuple-element.32), channel_id=1, source_target_pairs={{0,24},{8,0},{16,8},{24,16},{1,25},{9,1},{17,9},{25,17},{2,26},{10... | collective-permute-start | bytes 245768 | tf_op jit(solution)/shard_map/ppermute | solution.py:24
  6.9 2.6 %collective-permute-start.3 = (f32[5,8,128]{2,1,0:T(8,128)S(1)}, f32[5,8,128]{2,1,0:T(8,128)S(1)}, u32[]{:S(2)}, u32[]{:S(2)}) collective-permute-start(f32[5,8,128]{2,1,0:T(8,128)S(1)} %get-tuple-element.34), channel_id=1, source_target_pairs={{0,7},{1,0},{2,1},{3,2},{4,3},{5,4},{6,5},{7,6},{8,15},{9,8},{10,9... | collective-permute-start | bytes 61448 | tf_op jit(solution)/shard_map/ppermute | solution.py:24
  9.5 1.4 %slice_bitcast_fusion.3 = (f32[5,64,256]{2,1,0:T(8,128)S(1)}, f32[5,64,256]{2,1,0:T(8,128)S(1)}, f32[5,64,256]{2,1,0:T(8,128)S(1)}) fusion(f32[1,3,5,64,256]{4,3,2,1,0:T(8,128)} %param.7), kind=kLoop, calls=%fused_computation.8 | loop fusion | bytes 1966080 | tf_op jit(solution)/shard_map/squeeze | solution.py:343
  10.9 0.2 convert_reduce_fusion
  11.2 0.7 local_part.6.base_ref
  12.0 0.2 finish.6
  12.2 0.1 collective-permute-start.4
  12.2 3.8 %collective-permute-start.5 = (f32[5,16,256]{2,1,0:T(8,128)S(1)}, f32[5,16,256]{2,1,0:T(8,128)S(1)}, u32[]{:S(2)}, u32[]{:S(2)}) collective-permute-start(f32[5,16,256]{2,1,0:T(8,128)S(1)} %get-tuple-element.37), channel_id=1, source_target_pairs={{0,24},{8,0},{16,8},{24,16},{1,25},{9,1},{17,9},{25,17},{2,26},{10... | collective-permute-start | bytes 245768 | tf_op jit(solution)/shard_map/ppermute | solution.py:24
  16.0 2.6 %collective-permute-start.7 = (f32[5,8,128]{2,1,0:T(8,128)S(1)}, f32[5,8,128]{2,1,0:T(8,128)S(1)}, u32[]{:S(2)}, u32[]{:S(2)}) collective-permute-start(f32[5,8,128]{2,1,0:T(8,128)S(1)} %get-tuple-element.39), channel_id=1, source_target_pairs={{0,7},{1,0},{2,1},{3,2},{4,3},{5,4},{6,5},{7,6},{8,15},{9,8},{10,9... | collective-permute-start | bytes 61448 | tf_op jit(solution)/shard_map/ppermute | solution.py:24
  18.7 0.7 local_part.7.base_ref
  19.4 0.7 collective-permute-done.6.ylow_ref
  20.1 0.0 collective-permute-done.7.yhigh_ref
  20.2 0.2 finish.7
  20.4 0.1 collective-permute-start.8
  20.4 3.8 %collective-permute-start.9 = (f32[5,16,256]{2,1,0:T(8,128)S(1)}, f32[5,16,256]{2,1,0:T(8,128)S(1)}, u32[]{:S(2)}, u32[]{:S(2)}) collective-permute-start(f32[5,16,256]{2,1,0:T(8,128)S(1)} %get-tuple-element.42), channel_id=1, source_target_pairs={{0,24},{8,0},{16,8},{24,16},{1,25},{9,1},{17,9},{25,17},{2,26},{10... | collective-permute-start | bytes 245768 | tf_op jit(solution)/shard_map/ppermute | solution.py:24
  24.2 2.6 %collective-permute-start.11 = (f32[5,8,128]{2,1,0:T(8,128)S(1)}, f32[5,8,128]{2,1,0:T(8,128)S(1)}, u32[]{:S(2)}, u32[]{:S(2)}) collective-permute-start(f32[5,8,128]{2,1,0:T(8,128)S(1)} %get-tuple-element.44), channel_id=1, source_target_pairs={{0,7},{1,0},{2,1},{3,2},{4,3},{5,4},{6,5},{7,6},{8,15},{9,8},{10,9... | collective-permute-start | bytes 61448 | tf_op jit(solution)/shard_map/ppermute | solution.py:24
  26.9 0.2 fusion.placing_ref
  27.1 0.8 local_part.8.base_ref
  27.9 0.4 collective-permute-done.10.ylow_ref
  28.3 0.0 collective-permute-done.11.yhigh_ref
  28.4 0.9 %finish.8.w_ref = f32[5,64,256]{2,1,0:T(8,128)} custom-call(f32[5,64,256]{2,1,0:T(8,128)S(1)} %get-tuple-element.64.refs_0_.state_ref, f32[5,64,256]{2,1,0:T(8,128)S(1)} %local_part.8.base_ref, f32[5,16,256]{2,1,0:T(8,128)S(1)} %collective-permute-done.8.xlow_ref, f32[5,16,256]{2,1,0:T(8,128)S(1)} %collective-permute-done.9.xhigh_ref, ...), custom_call_target="tpu_custom_call" | custom-call | tf_op jit(solution)/shard_map/finish/pallas_call | solution.py:356
  29.3 1.0 %copy-done.3 = f32[5,64,256]{2,1,0:T(8,128)S(1)} copy-done((f32[5,64,256]{2,1,0:T(8,128)S(1)}, f32[5,64,256]{2,1,0:T(8,128)}, u32[]{:S(2)}) %copy-start.3) | copy-done | bytes 327704
  30.3 6.7 %project.1 = f32[8,328,128]{2,1,0:T(8,128)S(1)} custom-call(f32[5,64,256]{2,1,0:T(8,128)S(1)} %copy-done.3, f32[1,64,64,512]{3,2,1,0:T(8,128)S(1)} %copy-done, bf16[512,1024]{1,0:T(8,128)(2,1)S(1)} %fusion.placing_ref, f32[8,512]{1,0:T(8,128)S(1)} %broadcast_in_dim.5.extra_ref), custom_call_target="tpu_custom_call" | custom-call | tf_op jit(solution)/shard_map/project/pallas_call | solution.py:422
  36.9 22.7 %all_to_all.5.refs_0_ = f32[8,328,128]{2,1,0:T(8,128)S(1)} all-to-all(f32[8,328,128]{2,1,0:T(8,128)S(1)} %project.1), channel_id=1, replica_groups=mesh['gx'=4,'gy'=2,'gz'=4] {'gy','gz'}, dimensions={0} | all-to-all | bytes 2686976 | tf_op jit(solution)/shard_map/all_to_all | solution.py:480
  59.6 1.2 %receive.1 = (f32[5,64,256]{2,1,0:T(8,128)S(1)}, f32[5,16,256]{2,1,0:T(8,128)S(1)}, f32[5,16,256]{2,1,0:T(8,128)S(1)}, f32[5,8,128]{2,1,0:T(8,128)S(1)}, f32[5,8,128]{2,1,0:T(8,128)S(1)}) custom-call(f32[8,328,128]{2,1,0:T(8,128)S(1)} %all_to_all.5.refs_0_), custom_call_target="tpu_custom_call" | custom-call | tf_op jit(solution)/shard_map/receive/pallas_call | solution.py:467
  60.9 0.0 collective-permute-start.12
  60.9 3.8 %collective-permute-start.13 = (f32[5,16,256]{2,1,0:T(8,128)S(1)}, f32[5,16,256]{2,1,0:T(8,128)S(1)}, u32[]{:S(2)}, u32[]{:S(2)}) collective-permute-start(f32[5,16,256]{2,1,0:T(8,128)S(1)} %get-tuple-element.47), channel_id=1, source_target_pairs={{0,24},{8,0},{16,8},{24,16},{1,25},{9,1},{17,9},{25,17},{2,26},{10... | collective-permute-start | bytes 245768 | tf_op jit(solution)/shard_map/ppermute | solution.py:24
  64.7 2.6 %collective-permute-start.15 = (f32[5,8,128]{2,1,0:T(8,128)S(1)}, f32[5,8,128]{2,1,0:T(8,128)S(1)}, u32[]{:S(2)}, u32[]{:S(2)}) collective-permute-start(f32[5,8,128]{2,1,0:T(8,128)S(1)} %get-tuple-element.49), channel_id=1, source_target_pairs={{0,7},{1,0},{2,1},{3,2},{4,3},{5,4},{6,5},{7,6},{8,15},{9,8},{10,9... | collective-permute-start | bytes 61448 | tf_op jit(solution)/shard_map/ppermute | solution.py:24
  67.4 0.1 slice_bitcast_fusion
  67.5 0.7 local_part.9.base_ref
  68.2 0.7 collective-permute-done.14.ylow_ref
  68.9 0.2 finish.9
  69.1 0.1 collective-permute-start.16
  69.1 3.8 %collective-permute-start.17 = (f32[5,16,256]{2,1,0:T(8,128)S(1)}, f32[5,16,256]{2,1,0:T(8,128)S(1)}, u32[]{:S(2)}, u32[]{:S(2)}) collective-permute-start(f32[5,16,256]{2,1,0:T(8,128)S(1)} %get-tuple-element.52), channel_id=1, source_target_pairs={{0,24},{8,0},{16,8},{24,16},{1,25},{9,1},{17,9},{25,17},{2,26},{10... | collective-permute-start | bytes 245768 | tf_op jit(solution)/shard_map/ppermute | solution.py:24
  72.9 2.6 %collective-permute-start.19 = (f32[5,8,128]{2,1,0:T(8,128)S(1)}, f32[5,8,128]{2,1,0:T(8,128)S(1)}, u32[]{:S(2)}, u32[]{:S(2)}) collective-permute-start(f32[5,8,128]{2,1,0:T(8,128)S(1)} %get-tuple-element.54), channel_id=1, source_target_pairs={{0,7},{1,0},{2,1},{3,2},{4,3},{5,4},{6,5},{7,6},{8,15},{9,8},{10,9... | collective-permute-start | bytes 61448 | tf_op jit(solution)/shard_map/ppermute | solution.py:24
  75.6 0.7 local_part.10.base_ref
  76.3 0.7 collective-permute-done.18.ylow_ref
  77.0 0.0 collective-permute-done.19.yhigh_ref
  77.1 0.2 finish.10
  77.3 0.1 collective-permute-start.20
  77.3 3.8 %collective-permute-start.21 = (f32[5,16,256]{2,1,0:T(8,128)S(1)}, f32[5,16,256]{2,1,0:T(8,128)S(1)}, u32[]{:S(2)}, u32[]{:S(2)}) collective-permute-start(f32[5,16,256]{2,1,0:T(8,128)S(1)} %get-tuple-element.57), channel_id=1, source_target_pairs={{0,24},{8,0},{16,8},{24,16},{1,25},{9,1},{17,9},{25,17},{2,26},{10... | collective-permute-start | bytes 245768 | tf_op jit(solution)/shard_map/ppermute | solution.py:24
  81.2 2.6 %collective-permute-start.23 = (f32[5,8,128]{2,1,0:T(8,128)S(1)}, f32[5,8,128]{2,1,0:T(8,128)S(1)}, u32[]{:S(2)}, u32[]{:S(2)}) collective-permute-start(f32[5,8,128]{2,1,0:T(8,128)S(1)} %get-tuple-element.59), channel_id=1, source_target_pairs={{0,7},{1,0},{2,1},{3,2},{4,3},{5,4},{6,5},{7,6},{8,15},{9,8},{10,9... | collective-permute-start | bytes 61448 | tf_op jit(solution)/shard_map/ppermute | solution.py:24
  83.8 0.7 local_part.11.base_ref
  84.5 0.7 collective-permute-done.22.ylow_ref
  85.3 0.9 %finish.11 = f32[5,64,256]{2,1,0:T(8,128)} custom-call(f32[5,64,256]{2,1,0:T(8,128)S(1)} %get-tuple-element.61.refs_0_.state_ref, f32[5,64,256]{2,1,0:T(8,128)S(1)} %local_part.11.base_ref, f32[5,16,256]{2,1,0:T(8,128)S(1)} %collective-permute-done.20.xlow_ref, f32[5,16,256]{2,1,0:T(8,128)S(1)} %collective-permute-done.21.xhigh_ref, ...), custom_call_target="tpu_custom_call" | custom-call | tf_op jit(solution)/shard_map/finish/pallas_call | solution.py:356
  (37 shorter events, 0.1 us)
Async XLA Ops:
  0.6 1.0 %copy-start.1 = (f32[1,5,64,256]{3,2,1,0:T(8,128)S(1)}, f32[1,5,64,256]{3,2,1,0:T(8,128)}, u32[]{:S(2)}) copy-start(f32[1,5,64,256]{3,2,1,0:T(8,128)} %param.6) | copy-start | bytes 983044
  1.6 9.3 %copy-start.5 = (s32[1,512,1]{1,2,0:T(1,128)S(1)}, s32[1,512,1]{1,2,0:T(1,128)}, u32[]{:S(2)}) copy-start(s32[1,512,1]{1,2,0:T(1,128)} %param.9) | copy-start | bytes 6148
  1.6 9.6 %copy-start.2 = (f32[1,5,64,256]{3,2,1,0:T(8,128)S(1)}, f32[1,5,64,256]{3,2,1,0:T(8,128)}, u32[]{:S(2)}) copy-start(f32[1,5,64,256]{3,2,1,0:T(8,128)} %param.6) | copy-start | bytes 983044
  1.7 10.2 %collective-permute-start = (f32[5,16,256]{2,1,0:T(8,128)S(1)}, f32[5,16,256]{2,1,0:T(8,128)S(1)}, u32[]{:S(2)}, u32[]{:S(2)}) collective-permute-start(f32[5,16,256]{2,1,0:T(8,128)S(1)} %get-tuple-element.31), channel_id=1, source_target_pairs={{0,8},{8,16},{16,24},{24,0},{1,9},{9,17},{17,25},{25,1},{2,10},{10... | collective-permute-start | bytes 245768 | tf_op jit(solution)/shard_map/ppermute | solution.py:24
  4.8 7.2 %collective-permute-start.1 = (f32[5,16,256]{2,1,0:T(8,128)S(1)}, f32[5,16,256]{2,1,0:T(8,128)S(1)}, u32[]{:S(2)}, u32[]{:S(2)}) collective-permute-start(f32[5,16,256]{2,1,0:T(8,128)S(1)} %get-tuple-element.32), channel_id=1, source_target_pairs={{0,24},{8,0},{16,8},{24,16},{1,25},{9,1},{17,9},{25,17},{2,26},{10... | collective-permute-start | bytes 245768 | tf_op jit(solution)/shard_map/ppermute | solution.py:24
  6.9 5.1 %collective-permute-start.2 = (f32[5,8,128]{2,1,0:T(8,128)S(1)}, f32[5,8,128]{2,1,0:T(8,128)S(1)}, u32[]{:S(2)}, u32[]{:S(2)}) collective-permute-start(f32[5,8,128]{2,1,0:T(8,128)S(1)} %get-tuple-element.33), channel_id=1, source_target_pairs={{0,1},{1,2},{2,3},{3,4},{4,5},{5,6},{6,7},{7,0},{8,9},{9,10},{10,1... | collective-permute-start | bytes 61448 | tf_op jit(solution)/shard_map/ppermute | solution.py:24
  6.9 20.3 %copy-start.6 = (s32[1,512]{1,0:T(1,128)S(1)}, s32[1,512]{1,0:T(1,128)}, u32[]{:S(2)}) copy-start(s32[1,512]{1,0:T(1,128)} %param.10) | copy-start | bytes 6148
  6.9 5.1 %collective-permute-start.3 = (f32[5,8,128]{2,1,0:T(8,128)S(1)}, f32[5,8,128]{2,1,0:T(8,128)S(1)}, u32[]{:S(2)}, u32[]{:S(2)}) collective-permute-start(f32[5,8,128]{2,1,0:T(8,128)S(1)} %get-tuple-element.34), channel_id=1, source_target_pairs={{0,7},{1,0},{2,1},{3,2},{4,3},{5,4},{6,5},{7,6},{8,15},{9,8},{10,9... | collective-permute-start | bytes 61448 | tf_op jit(solution)/shard_map/ppermute | solution.py:24
  9.5 19.8 %copy-start = (f32[1,64,64,512]{3,2,1,0:T(8,128)S(1)}, f32[1,64,64,512]{3,2,1,0:T(8,128)}, u32[]{:S(2)}) copy-start(f32[1,64,64,512]{3,2,1,0:T(8,128)} %block_ref.1) | copy-start | bytes 25165828
  12.2 8.0 %collective-permute-start.4 = (f32[5,16,256]{2,1,0:T(8,128)S(1)}, f32[5,16,256]{2,1,0:T(8,128)S(1)}, u32[]{:S(2)}, u32[]{:S(2)}) collective-permute-start(f32[5,16,256]{2,1,0:T(8,128)S(1)} %get-tuple-element.36), channel_id=1, source_target_pairs={{0,8},{8,16},{16,24},{24,0},{1,9},{9,17},{17,25},{25,1},{2,10},{10... | collective-permute-start | bytes 245768 | tf_op jit(solution)/shard_map/ppermute | solution.py:24
  12.2 7.9 %collective-permute-start.5 = (f32[5,16,256]{2,1,0:T(8,128)S(1)}, f32[5,16,256]{2,1,0:T(8,128)S(1)}, u32[]{:S(2)}, u32[]{:S(2)}) collective-permute-start(f32[5,16,256]{2,1,0:T(8,128)S(1)} %get-tuple-element.37), channel_id=1, source_target_pairs={{0,24},{8,0},{16,8},{24,16},{1,25},{9,1},{17,9},{25,17},{2,26},{10... | collective-permute-start | bytes 245768 | tf_op jit(solution)/shard_map/ppermute | solution.py:24
  16.0 4.1 %collective-permute-start.6 = (f32[5,8,128]{2,1,0:T(8,128)S(1)}, f32[5,8,128]{2,1,0:T(8,128)S(1)}, u32[]{:S(2)}, u32[]{:S(2)}) collective-permute-start(f32[5,8,128]{2,1,0:T(8,128)S(1)} %get-tuple-element.38), channel_id=1, source_target_pairs={{0,1},{1,2},{2,3},{3,4},{4,5},{5,6},{6,7},{7,0},{8,9},{9,10},{10,1... | collective-permute-start | bytes 61448 | tf_op jit(solution)/shard_map/ppermute | solution.py:24
  16.0 4.1 %collective-permute-start.7 = (f32[5,8,128]{2,1,0:T(8,128)S(1)}, f32[5,8,128]{2,1,0:T(8,128)S(1)}, u32[]{:S(2)}, u32[]{:S(2)}) collective-permute-start(f32[5,8,128]{2,1,0:T(8,128)S(1)} %get-tuple-element.39), channel_id=1, source_target_pairs={{0,7},{1,0},{2,1},{3,2},{4,3},{5,4},{6,5},{7,6},{8,15},{9,8},{10,9... | collective-permute-start | bytes 61448 | tf_op jit(solution)/shard_map/ppermute | solution.py:24
  20.4 8.0 %collective-permute-start.8 = (f32[5,16,256]{2,1,0:T(8,128)S(1)}, f32[5,16,256]{2,1,0:T(8,128)S(1)}, u32[]{:S(2)}, u32[]{:S(2)}) collective-permute-start(f32[5,16,256]{2,1,0:T(8,128)S(1)} %get-tuple-element.41), channel_id=1, source_target_pairs={{0,8},{8,16},{16,24},{24,0},{1,9},{9,17},{17,25},{25,1},{2,10},{10... | collective-permute-start | bytes 245768 | tf_op jit(solution)/shard_map/ppermute | solution.py:24
  20.4 7.9 %collective-permute-start.9 = (f32[5,16,256]{2,1,0:T(8,128)S(1)}, f32[5,16,256]{2,1,0:T(8,128)S(1)}, u32[]{:S(2)}, u32[]{:S(2)}) collective-permute-start(f32[5,16,256]{2,1,0:T(8,128)S(1)} %get-tuple-element.42), channel_id=1, source_target_pairs={{0,24},{8,0},{16,8},{24,16},{1,25},{9,1},{17,9},{25,17},{2,26},{10... | collective-permute-start | bytes 245768 | tf_op jit(solution)/shard_map/ppermute | solution.py:24
  24.2 4.1 %collective-permute-start.10 = (f32[5,8,128]{2,1,0:T(8,128)S(1)}, f32[5,8,128]{2,1,0:T(8,128)S(1)}, u32[]{:S(2)}, u32[]{:S(2)}) collective-permute-start(f32[5,8,128]{2,1,0:T(8,128)S(1)} %get-tuple-element.43), channel_id=1, source_target_pairs={{0,1},{1,2},{2,3},{3,4},{4,5},{5,6},{6,7},{7,0},{8,9},{9,10},{10,1... | collective-permute-start | bytes 61448 | tf_op jit(solution)/shard_map/ppermute | solution.py:24
  24.2 4.1 %collective-permute-start.11 = (f32[5,8,128]{2,1,0:T(8,128)S(1)}, f32[5,8,128]{2,1,0:T(8,128)S(1)}, u32[]{:S(2)}, u32[]{:S(2)}) collective-permute-start(f32[5,8,128]{2,1,0:T(8,128)S(1)} %get-tuple-element.44), channel_id=1, source_target_pairs={{0,7},{1,0},{2,1},{3,2},{4,3},{5,4},{6,5},{7,6},{8,15},{9,8},{10,9... | collective-permute-start | bytes 61448 | tf_op jit(solution)/shard_map/ppermute | solution.py:24
  29.3 1.0 %copy-start.3 = (f32[5,64,256]{2,1,0:T(8,128)S(1)}, f32[5,64,256]{2,1,0:T(8,128)}, u32[]{:S(2)}) copy-start(f32[5,64,256]{2,1,0:T(8,128)} %finish.8.w_ref) | copy-start | bytes 983044
  36.9 30.4 %copy-start.4 = (f32[1,3,5,64,256]{4,3,2,1,0:T(8,128)S(1)}, f32[1,3,5,64,256]{4,3,2,1,0:T(8,128)}, u32[]{:S(2)}) copy-start(f32[1,3,5,64,256]{4,3,2,1,0:T(8,128)} %param.8) | copy-start | bytes 2949124
  60.9 8.0 %collective-permute-start.12 = (f32[5,16,256]{2,1,0:T(8,128)S(1)}, f32[5,16,256]{2,1,0:T(8,128)S(1)}, u32[]{:S(2)}, u32[]{:S(2)}) collective-permute-start(f32[5,16,256]{2,1,0:T(8,128)S(1)} %get-tuple-element.46), channel_id=1, source_target_pairs={{0,8},{8,16},{16,24},{24,0},{1,9},{9,17},{17,25},{25,1},{2,10},{10... | collective-permute-start | bytes 245768 | tf_op jit(solution)/shard_map/ppermute | solution.py:24
  60.9 7.9 %collective-permute-start.13 = (f32[5,16,256]{2,1,0:T(8,128)S(1)}, f32[5,16,256]{2,1,0:T(8,128)S(1)}, u32[]{:S(2)}, u32[]{:S(2)}) collective-permute-start(f32[5,16,256]{2,1,0:T(8,128)S(1)} %get-tuple-element.47), channel_id=1, source_target_pairs={{0,24},{8,0},{16,8},{24,16},{1,25},{9,1},{17,9},{25,17},{2,26},{10... | collective-permute-start | bytes 245768 | tf_op jit(solution)/shard_map/ppermute | solution.py:24
  64.7 4.1 %collective-permute-start.14 = (f32[5,8,128]{2,1,0:T(8,128)S(1)}, f32[5,8,128]{2,1,0:T(8,128)S(1)}, u32[]{:S(2)}, u32[]{:S(2)}) collective-permute-start(f32[5,8,128]{2,1,0:T(8,128)S(1)} %get-tuple-element.48), channel_id=1, source_target_pairs={{0,1},{1,2},{2,3},{3,4},{4,5},{5,6},{6,7},{7,0},{8,9},{9,10},{10,1... | collective-permute-start | bytes 61448 | tf_op jit(solution)/shard_map/ppermute | solution.py:24
  64.7 4.1 %collective-permute-start.15 = (f32[5,8,128]{2,1,0:T(8,128)S(1)}, f32[5,8,128]{2,1,0:T(8,128)S(1)}, u32[]{:S(2)}, u32[]{:S(2)}) collective-permute-start(f32[5,8,128]{2,1,0:T(8,128)S(1)} %get-tuple-element.49), channel_id=1, source_target_pairs={{0,7},{1,0},{2,1},{3,2},{4,3},{5,4},{6,5},{7,6},{8,15},{9,8},{10,9... | collective-permute-start | bytes 61448 | tf_op jit(solution)/shard_map/ppermute | solution.py:24
  69.1 8.0 %collective-permute-start.16 = (f32[5,16,256]{2,1,0:T(8,128)S(1)}, f32[5,16,256]{2,1,0:T(8,128)S(1)}, u32[]{:S(2)}, u32[]{:S(2)}) collective-permute-start(f32[5,16,256]{2,1,0:T(8,128)S(1)} %get-tuple-element.51), channel_id=1, source_target_pairs={{0,8},{8,16},{16,24},{24,0},{1,9},{9,17},{17,25},{25,1},{2,10},{10... | collective-permute-start | bytes 245768 | tf_op jit(solution)/shard_map/ppermute | solution.py:24
  69.1 7.9 %collective-permute-start.17 = (f32[5,16,256]{2,1,0:T(8,128)S(1)}, f32[5,16,256]{2,1,0:T(8,128)S(1)}, u32[]{:S(2)}, u32[]{:S(2)}) collective-permute-start(f32[5,16,256]{2,1,0:T(8,128)S(1)} %get-tuple-element.52), channel_id=1, source_target_pairs={{0,24},{8,0},{16,8},{24,16},{1,25},{9,1},{17,9},{25,17},{2,26},{10... | collective-permute-start | bytes 245768 | tf_op jit(solution)/shard_map/ppermute | solution.py:24
  72.9 4.1 %collective-permute-start.18 = (f32[5,8,128]{2,1,0:T(8,128)S(1)}, f32[5,8,128]{2,1,0:T(8,128)S(1)}, u32[]{:S(2)}, u32[]{:S(2)}) collective-permute-start(f32[5,8,128]{2,1,0:T(8,128)S(1)} %get-tuple-element.53), channel_id=1, source_target_pairs={{0,1},{1,2},{2,3},{3,4},{4,5},{5,6},{6,7},{7,0},{8,9},{9,10},{10,1... | collective-permute-start | bytes 61448 | tf_op jit(solution)/shard_map/ppermute | solution.py:24
  72.9 4.1 %collective-permute-start.19 = (f32[5,8,128]{2,1,0:T(8,128)S(1)}, f32[5,8,128]{2,1,0:T(8,128)S(1)}, u32[]{:S(2)}, u32[]{:S(2)}) collective-permute-start(f32[5,8,128]{2,1,0:T(8,128)S(1)} %get-tuple-element.54), channel_id=1, source_target_pairs={{0,7},{1,0},{2,1},{3,2},{4,3},{5,4},{6,5},{7,6},{8,15},{9,8},{10,9... | collective-permute-start | bytes 61448 | tf_op jit(solution)/shard_map/ppermute | solution.py:24
  77.3 8.0 %collective-permute-start.20 = (f32[5,16,256]{2,1,0:T(8,128)S(1)}, f32[5,16,256]{2,1,0:T(8,128)S(1)}, u32[]{:S(2)}, u32[]{:S(2)}) collective-permute-start(f32[5,16,256]{2,1,0:T(8,128)S(1)} %get-tuple-element.56), channel_id=1, source_target_pairs={{0,8},{8,16},{16,24},{24,0},{1,9},{9,17},{17,25},{25,1},{2,10},{10... | collective-permute-start | bytes 245768 | tf_op jit(solution)/shard_map/ppermute | solution.py:24
  77.3 7.9 %collective-permute-start.21 = (f32[5,16,256]{2,1,0:T(8,128)S(1)}, f32[5,16,256]{2,1,0:T(8,128)S(1)}, u32[]{:S(2)}, u32[]{:S(2)}) collective-permute-start(f32[5,16,256]{2,1,0:T(8,128)S(1)} %get-tuple-element.57), channel_id=1, source_target_pairs={{0,24},{8,0},{16,8},{24,16},{1,25},{9,1},{17,9},{25,17},{2,26},{10... | collective-permute-start | bytes 245768 | tf_op jit(solution)/shard_map/ppermute | solution.py:24
  81.1 4.1 %collective-permute-start.22 = (f32[5,8,128]{2,1,0:T(8,128)S(1)}, f32[5,8,128]{2,1,0:T(8,128)S(1)}, u32[]{:S(2)}, u32[]{:S(2)}) collective-permute-start(f32[5,8,128]{2,1,0:T(8,128)S(1)} %get-tuple-element.58), channel_id=1, source_target_pairs={{0,1},{1,2},{2,3},{3,4},{4,5},{5,6},{6,7},{7,0},{8,9},{9,10},{10,1... | collective-permute-start | bytes 61448 | tf_op jit(solution)/shard_map/ppermute | solution.py:24
  81.2 4.1 %collective-permute-start.23 = (f32[5,8,128]{2,1,0:T(8,128)S(1)}, f32[5,8,128]{2,1,0:T(8,128)S(1)}, u32[]{:S(2)}, u32[]{:S(2)}) collective-permute-start(f32[5,8,128]{2,1,0:T(8,128)S(1)} %get-tuple-element.59), channel_id=1, source_target_pairs={{0,7},{1,0},{2,1},{3,2},{4,3},{5,4},{6,5},{7,6},{8,15},{9,8},{10,9... | collective-permute-start | bytes 61448 | tf_op jit(solution)/shard_map/ppermute | solution.py:24
where the time goes:
time: 86.4 us; the launch traced here: 86.2 us
  starting transfers between devices  40.4 us (47%)
  blocking collectives  22.7 us (26%)
  Pallas kernels  14.9 us (17%)
  local copies, waits for them, and re-layouts  3.45 us (4%)
  waiting for transfers between devices  3.4 us (4%)
    ppermute x24, starting transfers between devices, shifted(): return lax.ppermute(value, axis, pairs)  40.4 us
    all_to_all x1, blocking collectives, send_to_owners(): lax.all_to_all(values, ('gy', 'gz'), split_axis=0, concat_axis=0, tiled=T...  22.7 us
    pallas_call x1, Pallas kernels, project(): pl.pallas_call(functools.partial(project_kernel, m_tiles), out_shape=jax....  6.67 us
    pallas_call x6, Pallas kernels, section(): pl.pallas_call(functools.partial(local_kernel, scale, tuple((f for _, f i...  4.38 us
    ppermute x24, waiting for transfers between devices, shifted(): return lax.ppermute(value, axis, pairs)  3.4 us
    pallas_call x6, Pallas kernels, section(): pl.pallas_call(functools.partial(finish_kernel, scale, with_faces, halves...  2.57 us
    unnamed x14, local copies, waits for them, and re-layouts  1.96 us
  transfers between devices with their start and end apart: 24, of which 5 were waited for; matrix products, arithmetic and copies ran while one was open for 2% of the time, Pallas kernels for 5%

commit v1 on v0

--- a/solution.py
+++ b/solution.py
@@ -18,10 +18,19 @@
 LANES = 128
 
 
-def shifted(value, axis, steps):
+def swapped(value, axis, offset):
     count = lax.axis_size(axis)
-    pairs = [(source, (source + steps) % count) for source in range(count)]
+    pairs = []
+    for source in range(count):
+        up = source % 2 == offset
+        pairs.append((source, (source + (1 if up else -1)) % count))
     return lax.ppermute(value, axis, pairs)
+
+
+def even_places():
+    along_x = lax.axis_index("gx")
+    along_y = lax.axis_index("gy") * lax.axis_size("gz") + lax.axis_index("gz")
+    return lax.rem(along_x, 2) == 0, lax.rem(along_y, 2) == 0
 
 
 def lgl_matrix():
@@ -59,7 +68,8 @@
 
 
 def tile_of(ref, v, i, j):
-    return ref[v, 8 * i : 8 * i + 8, LANES * j : LANES * (j + 1)]
+    lead = v if isinstance(v, tuple) else (v,)
+    return ref[lead + (slice(8 * i, 8 * i + 8), slice(LANES * j, LANES * (j + 1)))]
 
 
 def primitive_state(get):
@@ -116,14 +126,13 @@
     return out
 
 
-def local_kernel(scale, extras, halves, *refs):
+def local_kernel(scale, index, extras, halves, *refs):
     state_ref, w_ref = refs[0], refs[1]
     extra_refs = refs[2 : 2 + len(extras)]
     out_ref = refs[2 + len(extras)]
     row, lane = iotas()
     low_half_rows = row < 4
     low_half_lanes = lane < 64
-    within = row % 4
     z_first = lane % ELEMENTS_Z == 0
     z_last = lane % ELEMENTS_Z == ELEMENTS_Z - 1
     z_shift = {}
@@ -213,7 +222,7 @@
                 penalties.append(
                     count * w - 2.0 * (y_jump + (low_term - high_term))
                 )
-            speeds, enthalpy = primitive_state(lambda q: tile_of(state_ref, q, i, j))
+            speeds, enthalpy = primitive_state(lambda q: tile_of(state_ref, (index, q), i, j))
             pulled = pull_full(speeds, enthalpy, v)
             for var in range(VARS):
                 change = (-step_rate * scale) * (pulled[var] + penalties[var])
@@ -223,21 +232,26 @@
                 out_ref[var, 8 * i : 8 * i + 8, LANES * j : LANES * (j + 1)] = base + change
 
 
-def pack_faces(w_ref, halves, xl_ref, xu_ref, yl_ref, yu_ref):
+def pack_faces(w_ref, halves, xa_ref, xb_ref, ya_ref, yb_ref):
+    even_x, even_y = even_places()
     row, lane = iotas()
     low_rows = row < 4
     low_lanes = lane < 64
     for var in range(VARS):
-        xl_ref[var] = w_ref[var, 0:16, :]
-        xu_ref[var] = w_ref[var, 48:64, :]
+        lower = w_ref[var, 0:16, :]
+        upper = w_ref[var, 48:64, :]
+        xa_ref[var] = jnp.where(even_x, upper, lower)
+        xb_ref[var] = jnp.where(even_x, lower, upper)
         low = [tile_of(w_ref, var, 2 * a, 0) for a in range(4)]
         left = jnp.where(low_rows, low[0], pltpu.roll(low[1], 4, 0))
         right = jnp.where(low_rows, low[2], pltpu.roll(low[3], 4, 0))
-        yl_ref[var] = jnp.where(low_lanes, left, pltpu.roll(right, 64, 1))
+        lower = jnp.where(low_lanes, left, pltpu.roll(right, 64, 1))
         high = [tile_of(w_ref, var, 2 * a + 1, halves - 1) for a in range(4)]
         left = jnp.where(low_rows, pltpu.roll(high[0], 4, 0), high[1])
         right = jnp.where(low_rows, pltpu.roll(high[2], 4, 0), high[3])
-        yu_ref[var] = jnp.where(low_lanes, pltpu.roll(left, 64, 1), right)
+        upper = jnp.where(low_lanes, pltpu.roll(left, 64, 1), right)
+        ya_ref[var] = jnp.where(even_y, upper, lower)
+        yb_ref[var] = jnp.where(even_y, lower, upper)
 
 
 def face_kernel(halves, w_ref, *out_refs):
@@ -245,9 +259,10 @@
 
 
 def finish_kernel(
-    scale, with_faces, halves, state_ref, base_ref, xlow_ref, xhigh_ref, ylow_ref, yhigh_ref, *outs
+    scale, index, with_faces, halves, state_ref, base_ref, xa_ref, xb_ref, ya_ref, yb_ref, *outs
 ):
     out_ref = outs[0]
+    even_x, even_y = even_places()
     row, lane = iotas()
     rate = np.float32(-step_rate * scale)
     y_low_mask = jnp.where(jnp.logical_and(row < 4, lane < 64), np.float32(half_lift), 0.0)
@@ -260,11 +275,15 @@
             place = (slice(8 * i, 8 * i + 8), slice(LANES * j, LANES * (j + 1)))
             values = [base_ref[(var,) + place] for var in range(VARS)]
             if has_x or has_y:
-                speeds, enthalpy = primitive_state(lambda q: tile_of(state_ref, q, i, j))
+                speeds, enthalpy = primitive_state(lambda q: tile_of(state_ref, (index, q), i, j))
             if has_x:
-                source = xlow_ref if a == 0 else xhigh_ref
+                first = jnp.logical_not(even_x) if a == 0 else even_x
                 sign = half_lift if a == 0 else -half_lift
-                got = [np.float32(sign) * tile_of(source, var, t, j) for var in range(VARS)]
+                got = [
+                    np.float32(sign)
+                    * jnp.where(first, tile_of(xa_ref, var, t, j), tile_of(xb_ref, var, t, j))
+                    for var in range(VARS)
+                ]
                 pulled = pull_one(0, speeds, enthalpy, got)
                 jump = 2.0 if a == 0 else -2.0
                 values = [
@@ -273,7 +292,8 @@
             if has_y:
                 got = []
                 for var in range(VARS):
-                    packed = (ylow_ref if t == 0 else yhigh_ref)[var]
+                    first = jnp.logical_not(even_y) if t == 0 else even_y
+                    packed = jnp.where(first, ya_ref[var], yb_ref[var])
                     if t == 0:
                         if a >= 2:
                             packed = pltpu.roll(packed, 64, 1)
@@ -327,12 +347,13 @@
 
 
 def exchange(faces):
-    xl, xu, yl, yu = faces
-    x_low = shifted(xu, "gx", 1)
-    x_high = shifted(xl, "gx", -1)
-    y_low = shifted(yu, ("gy", "gz"), 1)
-    y_high = shifted(yl, ("gy", "gz"), -1)
-    return x_low, x_high, y_low, y_high
+    xa, xb, ya, yb = faces
+    ring = ("gy", "gz")
+    xb = swapped(xb, "gx", 1)
+    xa = swapped(xa, "gx", 0)
+    yb = swapped(yb, ring, 1)
+    ya = swapped(ya, ring, 0)
+    return xa, xb, ya, yb
 
 
 def section(states, index, w, faces, scale, extras, with_faces):
@@ -340,9 +361,9 @@
     halves = columns // LANES
     shape = jax.ShapeDtypeStruct(w.shape, jnp.float32)
     received = exchange(faces)
-    state = states[index]
+    factors = tuple(f for _, f in extras)
     base = pl.pallas_call(
-        functools.partial(local_kernel, scale, tuple(f for _, f in extras), halves),
+        functools.partial(local_kernel, scale, index, factors, halves),
         out_shape=shape,
         in_specs=[vmem_spec()] * (2 + len(extras)),
         out_specs=vmem_spec(),
@@ -351,16 +372,16 @@
             flops=400 * 64 * columns, bytes_accessed=12 * VARS * 64 * columns, transcendentals=0
         ),
         name="local_part",
-    )(state, w, *[x for x, _ in extras])
+    )(states, w, *[x for x, _ in extras])
     out_shape = [shape] + (face_shapes(columns) if with_faces else [])
     return pl.pallas_call(
-        functools.partial(finish_kernel, scale, with_faces, halves),
+        functools.partial(finish_kernel, scale, index, with_faces, halves),
         out_shape=out_shape,
         in_specs=[vmem_spec()] * 6,
         out_specs=[vmem_spec()] * len(out_shape),
         compiler_params=params(),
         name="finish",
-    )(state, base, *received)
+    )(states, base, *received)
 
 
 def reverse_step(states, begin, faces):
@@ -380,113 +401,148 @@
     return high, middle, low
 
 
-def project_kernel(m_tiles, w_ref, block_ref, placing_ref, extra_ref, out_ref, held):
-    step = pl.program_id(0)
-
-    def body(n, sums):
-        sums = list(sums)
-        rows = [
-            jnp.broadcast_to(w_ref[var, pl.ds(n, 1), :], (8, LANES)) for var in range(VARS)
-        ]
-        for m in range(m_tiles):
-            block = block_ref[n, 8 * m : 8 * m + 8, :]
-            for var in range(VARS):
-                q = m * VARS + var
-                sums[q] = sums[q] + block * rows[var]
-        return tuple(sums)
-
-    start = tuple(jnp.zeros((8, LANES), jnp.float32) for _ in range(m_tiles * VARS))
-    sums = lax.fori_loop(0, 64, body, start, unroll=8)
-    for q in range(m_tiles * VARS):
-        held[step, 8 * q : 8 * q + 8, :] = sums[q]
-
-    @pl.when(step == pl.num_programs(0) - 1)
-    def _():
-        total = m_tiles * VARS * 8
-        result = jnp.zeros((total + 8, placing_ref.shape[1]), jnp.float32)
-        for s in range(held.shape[0]):
-            values = jnp.concatenate([held[s], extra_ref[:, LANES * s : LANES * (s + 1)]], axis=0)
-            spot = placing_ref[LANES * s : LANES * (s + 1), :]
-            for piece in split_three(values):
-                result = result + jnp.dot(piece, spot, preferred_element_type=jnp.float32)
-        for g in range(out_ref.shape[0]):
-            out_ref[g] = result[:, LANES * g : LANES * (g + 1)]
-
-
-def project(w, blocks, placing, extra, first, m_tiles):
-    halves = w.shape[2] // LANES
+def project_kernel(first, m_tiles, blocks, with_copy, *refs):
+    w_ref, block_ref, placing_ref, extra_ref = refs[:4]
+    out_refs = refs[4 : 4 + blocks]
+    held = refs[-2]
+    if with_copy:
+        copy = pltpu.make_async_copy(w_ref, refs[4 + blocks], refs[-1].at[0])
+        copy.start()
+    halves = w_ref.shape[2] // LANES
+    for r in range(block_ref.shape[3] // LANES):
+        lanes = slice(LANES * r, LANES * (r + 1))
+        half = r % halves
+        w_lanes = slice(LANES * half, LANES * (half + 1))
+
+        def body(tile, sums):
+            start = pl.multiple_of(8 * tile, 8)
+            groups = [w_ref[var, pl.ds(start, 8), w_lanes] for var in range(VARS)]
+            sums = list(sums)
+            for s in range(8):
+                rows = [jnp.broadcast_to(group[s : s + 1], (8, LANES)) for group in groups]
+                for m in range(m_tiles):
+                    node = 8 * (first + m)
+                    block = block_ref[0, start + s, node : node + 8, lanes]
+                    for var in range(VARS):
+                        q = m * VARS + var
+                        sums[q] = sums[q] + block * rows[var]
+            return tuple(sums)
+
+        start = tuple(jnp.zeros((8, LANES), jnp.float32) for _ in range(m_tiles * VARS))
+        sums = lax.fori_loop(0, 8, body, start)
+        for q in range(m_tiles * VARS):
+            held[8 * q : 8 * q + 8, lanes] = sums[q]
+
+    values = jnp.concatenate([held[...], extra_ref[...]], axis=0)
+    total = values.shape[0]
+    pieces = jnp.concatenate(split_three(values), axis=0)
+    result = jnp.dot(pieces, placing_ref[...], preferred_element_type=jnp.float32)
+    result = result[0:total] + result[total : 2 * total] + result[2 * total :]
+    for g in range(blocks):
+        out_refs[g][...] = result[:, LANES * g : LANES * (g + 1)]
+    if with_copy:
+        copy.wait()
+
+
+def project(w, blocks, placing, extra, first, m_tiles, with_copy):
     slots = blocks.shape[3]
-    steps = slots // LANES
     rows = m_tiles * VARS * 8
-    places = placing.shape[1]
+    count = placing.shape[1] // LANES
+    out_shape = [jax.ShapeDtypeStruct((rows + 8, LANES), jnp.float32)] * count
+    out_specs = [vmem_spec()] * count
+    if with_copy:
+        out_shape.append(jax.ShapeDtypeStruct(w.shape, jnp.float32))
+        out_specs.append(pl.BlockSpec(memory_space=pl.ANY))
     return pl.pallas_call(
-        functools.partial(project_kernel, m_tiles),
-        out_shape=jax.ShapeDtypeStruct((places // LANES, rows + 8, LANES), jnp.float32),
-        grid=(steps,),
-        in_specs=[
-            pl.BlockSpec((VARS, 64, LANES), lambda s: (0, 0, lax.rem(s, halves))),
-            pl.BlockSpec((None, 64, 8 * m_tiles, LANES), lambda s: (0, 0, first, s)),
-            vmem_spec(),
-            vmem_spec(),
+        functools.partial(project_kernel, first * m_tiles, m_tiles, count, with_copy),
+        out_shape=out_shape,
+        in_specs=[vmem_spec()] * 4,
+        out_specs=out_specs,
+        scratch_shapes=[
+            pltpu.VMEM((rows, slots), jnp.float32),
+            pltpu.SemaphoreType.DMA((1,)),
         ],
-        out_specs=vmem_spec(),
-        scratch_shapes=[pltpu.VMEM((steps, rows, LANES), jnp.float32)],
         compiler_params=params(),
+        cost_estimate=pl.CostEstimate(
+            flops=5 * 1000 * 1000 * 1000,
+            bytes_accessed=4 * rows * 64 * slots,
+            transcendentals=0,
+        ),
         name="project",
     )(w, blocks, placing, extra)
 
 
-def receive_kernel(count, m_tiles, halves, *refs):
-    incoming = refs[:count]
-    out_ref = refs[count]
+def receive_kernel(blocks, node, m_tiles, last, halves, *refs):
+    out_ref = refs[blocks + (1 if last else 0)]
     columns = out_ref.shape[2]
-    spots = []
-    for g in range(incoming[0].shape[0]):
-        rows = m_tiles * VARS * 8
-        local = incoming[0][g, rows : rows + 1, :].astype(jnp.int32)
+    rows = m_tiles * VARS * 8
+    if last:
+        done_ref = refs[blocks]
+        for var in range(VARS):
+            out_ref[var, 0:node, :] = done_ref[var]
+    result = jnp.zeros((rows, columns), jnp.float32)
+    for g in range(blocks):
+        local = refs[g][rows : rows + 1, :].astype(jnp.int32)
         index = lax.broadcasted_iota(jnp.int32, (columns, LANES), 0)
-        spots.append((index == local).astype(jnp.float32).astype(jnp.bfloat16))
-    for piece_index in range(count):
-        rows = m_tiles * VARS * 8
-        result = jnp.zeros((rows, columns), jnp.float32)
-        for g, spot in enumerate(spots):
-            for piece in split_three(incoming[piece_index][g, 0:rows, :]):
-                result = result + lax.dot_general(
-                    piece, spot, (((1,), (1,)), ((), ())), preferred_element_type=jnp.float32
-                )
-        for m in range(m_tiles):
-            node = 8 * (piece_index * m_tiles + m)
-            for var in range(VARS):
-                q = m * VARS + var
-                out_ref[var, node : node + 8, :] = result[8 * q : 8 * q + 8, :]
-    pack_faces(out_ref, halves, *refs[count + 1 :])
-
-
-def receive(incoming, columns, m_tiles):
-    shapes = [jax.ShapeDtypeStruct((VARS, 64, columns), jnp.float32)] + face_shapes(columns)
+        spot = (index == local).astype(jnp.float32).astype(jnp.bfloat16)
+        for piece in split_three(refs[g][0:rows, :]):
+            result = result + lax.dot_general(
+                piece, spot, (((1,), (1,)), ((), ())), preferred_element_type=jnp.float32
+            )
+    base = node if last else 0
+    for m in range(m_tiles):
+        for var in range(VARS):
+            q = m * VARS + var
+            out_ref[var, base + 8 * m : base + 8 * m + 8, :] = result[8 * q : 8 * q + 8, :]
+    if last:
+        pack_faces(out_ref, halves, *refs[blocks + 2 :])
+
+
+def receive(incoming, columns, node, m_tiles, done):
+    last = done is not None
+    if last:
+        shapes = [jax.ShapeDtypeStruct((VARS, 64, columns), jnp.float32)] + face_shapes(columns)
+    else:
+        shapes = [jax.ShapeDtypeStruct((VARS, 8 * m_tiles, columns), jnp.float32)]
+    operands = list(incoming) + ([done] if last else [])
     return pl.pallas_call(
-        functools.partial(receive_kernel, len(incoming), m_tiles, columns // LANES),
+        functools.partial(
+            receive_kernel, len(incoming), node, m_tiles, last, columns // LANES
+        ),
         out_shape=shapes,
-        in_specs=[vmem_spec()] * len(incoming),
+        in_specs=[vmem_spec()] * len(operands),
         out_specs=[vmem_spec()] * len(shapes),
         compiler_params=params(),
+        cost_estimate=pl.CostEstimate(
+            flops=1000 * 1000 * 1000, bytes_accessed=1000 * 1000, transcendentals=0
+        ),
         name="receive",
-    )(*incoming)
-
-
-def send_to_owners(values, group, capacity):
+    )(*operands)
+
+
+def send_direct(values):
+    ring = ("gy", "gz")
+    count = len(values)
+    received = [values[0]] * count
+    for k in (6, 7, 2, 4, 3, 5, 1):
+        if k < count:
+            received[k] = lax.ppermute(values[k], ring, [(s, s ^ k) for s in range(count)])
+    return received
+
+
+def send_all(values, group, capacity):
+    values = jnp.stack(values)
     blocks, rows, lanes = values.shape
-    if capacity == lanes:
-        return lax.all_to_all(values, ("gy", "gz"), split_axis=0, concat_axis=0, tiled=True)
     per = lanes // capacity
     values = values.reshape(blocks, rows, per, capacity).transpose(0, 2, 1, 3)
     values = values.reshape(group, rows, capacity)
     values = lax.all_to_all(values, ("gy", "gz"), split_axis=0, concat_axis=0, tiled=True)
     values = values.reshape(blocks, per, rows, capacity).transpose(0, 2, 1, 3)
-    return values.reshape(blocks, rows, lanes)
-
-
-CHUNKS = 1
+    values = values.reshape(blocks, rows, lanes)
+    return [values[g] for g in range(blocks)]
+
+
+CHUNKS = 2
 
 
 def per_device(
@@ -500,19 +556,30 @@
     order = jnp.arange(slots)
     earlier_same = (target[:, None] == target[None, :]) & (order[None, :] < order[:, None])
     rank_in = jnp.sum(earlier_same.astype(jnp.int32), axis=1)
+    direct = group in (2, 4, 8) and capacity == LANES
+    if direct:
+        here = lax.axis_index("gy") * lax.axis_size("gz") + lax.axis_index("gz")
+        target = jnp.bitwise_xor(target, here)
     place = target * capacity + rank_in
     placing = (place[:, None] == jnp.arange(group * capacity)[None, :]).astype(jnp.bfloat16)
     extra = jnp.broadcast_to(owner_element_index.astype(jnp.float32), (8, slots))
 
     begin = adj_final[0]
-    adj_new = reverse_step(new_states[0], begin, get_faces(begin))
+    result = reverse_step(new_states[0], begin, get_faces(begin))
 
     m_tiles = 8 // CHUNKS
     incoming = []
     for chunk in range(CHUNKS):
-        outgoing = project(adj_new, proj_blocks, placing, extra, chunk, m_tiles)
-        incoming.append(send_to_owners(outgoing, group, capacity))
-    adj_proj, *faces = receive(incoming, columns, m_tiles)
+        last = chunk == CHUNKS - 1
+        outgoing = project(result, proj_blocks, placing, extra, chunk, m_tiles, last)
+        if last:
+            adj_new = outgoing[-1]
+            outgoing = outgoing[:-1]
+        incoming.append(
+            send_direct(outgoing) if direct else send_all(outgoing, group, capacity)
+        )
+    (half,) = receive(incoming[0], columns, 0, m_tiles, None)
+    adj_proj, *faces = receive(incoming[1], columns, 8 * m_tiles, m_tiles, half)
     adj_old = reverse_step(old_states[0], adj_proj, faces)
     return (adj_new.reshape(adj_final.shape), adj_old.reshape(adj_final.shape))
 

time: 86.4 us -> 80.4 us (0.931)
  blocking collectives: 22.7 us -> 0 us
  waiting for transfers between devices: 3.4 us -> 17.5 us
  local copies, waits for them, and re-layouts: 3.45 us -> 6.54 us
  Pallas kernels: 14.9 us -> 12.6 us
  starting transfers between devices: 40.4 us -> 41.3 us
    all_to_all x1 -> x0, blocking collectives: 22.7 us -> none  [send_to_owners(): lax.all_to_all(values, ('gy', 'gz'), split_axis=0, concat_axis=0, tiled=T...]
    ppermute x24 -> x38, waiting for transfers between devices: 3.4 us -> 17.5 us  [the longest x24 10.5 us: swapped(): return lax.ppermute(value, axis, pairs)]
    unnamed x14 -> x16, local copies, waits for them, and re-layouts: 1.96 us -> 6.53 us
    pallas_call x14 -> x16, Pallas kernels: 14.9 us -> 12.5 us  [the longest x2 4.74 us: project(): pl.pallas_call(functools.partial(project_kernel, first * m_tiles, m_tiles...]
    squeeze x2 -> x0, local copies, waits for them, and re-layouts: 1.48 us -> none  [section(): state = states[index]]
    ppermute x24 -> x38, starting transfers between devices: 40.4 us -> 41.3 us  [the longest x24 27.8 us: swapped(): return lax.ppermute(value, axis, pairs)]
  transfers between devices with their start and end apart: 24 -> 38, of which waited for: 5 -> 15; matrix products, arithmetic and copies ran while one was open for 2% -> 2% of each run, Pallas kernels for 5% -> 9%
where the time goes in v1:
time: 80.4 us; the launch traced here: 80.1 us
  starting transfers between devices  41.3 us (51%)
  waiting for transfers between devices  17.5 us (22%)
  Pallas kernels  12.6 us (16%)
  local copies, waits for them, and re-layouts  6.54 us (8%)
  other arithmetic  1.24 us (2%)
  between operations  0.94 us (1%)
    ppermute x24, starting transfers between devices, swapped(): return lax.ppermute(value, axis, pairs)  27.8 us
    ppermute x14, starting transfers between devices, send_direct(): lax.ppermute(values[k], ring, [(s, s ^ k) for s in range(count)])  13.4 us
    ppermute x24, waiting for transfers between devices, swapped(): return lax.ppermute(value, axis, pairs)  10.5 us
    ppermute x14, waiting for transfers between devices, send_direct(): lax.ppermute(values[k], ring, [(s, s ^ k) for s in range(count)])  7.04 us
    unnamed x16, local copies, waits for them, and re-layouts  6.53 us
    pallas_call x2, Pallas kernels, project(): pl.pallas_call(functools.partial(project_kernel, first * m_tiles, m_tiles...  4.74 us
    pallas_call x6, Pallas kernels, section(): pl.pallas_call(functools.partial(local_kernel, scale, index, factors, hal...  4.41 us
    pallas_call x6, Pallas kernels, section(): pl.pallas_call(functools.partial(finish_kernel, scale, index, with_faces,...  1.92 us
  transfers between devices with their start and end apart: 38, of which 15 were waited for; matrix products, arithmetic and copies ran while one was open for 2% of the time, Pallas kernels for 9%

profile of v1, /device:TPU:0, one launch (start us, length us, event | category | flops | bytes accessed | tf_op | source)
XLA Modules:
  0.0 80.1 jit_solution(17929412849720790192)
XLA Ops:
  0.6 1.0 %copy-done.2 = f32[1,5,64,256]{3,2,1,0:T(8,128)S(1)} copy-done((f32[1,5,64,256]{3,2,1,0:T(8,128)S(1)}, f32[1,5,64,256]{3,2,1,0:T(8,128)}, u32[]{:S(2)}) %copy-start.2) | copy-done | bytes 327704
  1.7 3.1 %collective-permute-start = (f32[5,16,256]{2,1,0:T(8,128)S(1)}, f32[5,16,256]{2,1,0:T(8,128)S(1)}, u32[]{:S(2)}, u32[]{:S(2)}) collective-permute-start(f32[5,16,256]{2,1,0:T(8,128)S(1)} %get-tuple-element.48), channel_id=1, source_target_pairs={{0,8},{8,0},{16,24},{24,16},{1,9},{9,1},{17,25},{25,17},{2,10},{10... | collective-permute-start | bytes 245768 | tf_op jit(solution)/shard_map/ppermute | solution.py:27
  4.8 2.5 %collective-permute-start.1 = (f32[5,16,256]{2,1,0:T(8,128)S(1)}, f32[5,16,256]{2,1,0:T(8,128)S(1)}, u32[]{:S(2)}, u32[]{:S(2)}) collective-permute-start(f32[5,16,256]{2,1,0:T(8,128)S(1)} %get-tuple-element.49), channel_id=1, source_target_pairs={{0,24},{8,16},{16,8},{24,0},{1,25},{9,17},{17,9},{25,1},{2,26},{10... | collective-permute-start | bytes 245768 | tf_op jit(solution)/shard_map/ppermute | solution.py:27
  7.3 2.6 %collective-permute-start.3 = (f32[5,8,128]{2,1,0:T(8,128)S(1)}, f32[5,8,128]{2,1,0:T(8,128)S(1)}, u32[]{:S(2)}, u32[]{:S(2)}) collective-permute-start(f32[5,8,128]{2,1,0:T(8,128)S(1)} %get-tuple-element.51), channel_id=1, source_target_pairs={{0,7},{1,2},{2,1},{3,4},{4,3},{5,6},{6,5},{7,0},{8,15},{9,10},{10,... | collective-permute-start | bytes 61448 | tf_op jit(solution)/shard_map/ppermute | solution.py:27
  9.8 1.0 %convert_reduce_fusion = s32[512]{0:T(512)S(1)} fusion(s32[512]{0:T(512)} %bitcast.23), kind=kLoop, calls=%fused_computation.2 | loop fusion | flops 1310208 | bytes 4096 | tf_op jit(solution)/shard_map/reduce_sum | solution.py:558
  10.8 1.2 %copy-done = f32[1,3,5,64,256]{4,3,2,1,0:T(8,128)S(1)} copy-done((f32[1,3,5,64,256]{4,3,2,1,0:T(8,128)S(1)}, f32[1,3,5,64,256]{4,3,2,1,0:T(8,128)}, u32[]{:S(2)}) %copy-start) | copy-done | bytes 983064
  12.0 1.0 %copy-done.3 = f32[1,5,64,256]{3,2,1,0:T(8,128)S(1)} copy-done((f32[1,5,64,256]{3,2,1,0:T(8,128)S(1)}, f32[1,5,64,256]{3,2,1,0:T(8,128)}, u32[]{:S(2)}) %copy-start.3) | copy-done | bytes 327704
  13.0 0.7 local_part.6.base_ref
  14.0 0.7 collective-permute-start.4
  14.7 0.9 %collective-permute-start.5 = (f32[5,16,256]{2,1,0:T(8,128)S(1)}, f32[5,16,256]{2,1,0:T(8,128)S(1)}, u32[]{:S(2)}, u32[]{:S(2)}) collective-permute-start(f32[5,16,256]{2,1,0:T(8,128)S(1)} %get-tuple-element.54), channel_id=1, source_target_pairs={{0,24},{8,16},{16,8},{24,0},{1,25},{9,17},{17,9},{25,1},{2,26},{10... | collective-permute-start | bytes 245768 | tf_op jit(solution)/shard_map/ppermute | solution.py:27
  15.6 1.7 %collective-permute-start.7 = (f32[5,8,128]{2,1,0:T(8,128)S(1)}, f32[5,8,128]{2,1,0:T(8,128)S(1)}, u32[]{:S(2)}, u32[]{:S(2)}) collective-permute-start(f32[5,8,128]{2,1,0:T(8,128)S(1)} %get-tuple-element.56), channel_id=1, source_target_pairs={{0,7},{1,2},{2,1},{3,4},{4,3},{5,6},{6,5},{7,0},{8,15},{9,10},{10,... | collective-permute-start | bytes 61448 | tf_op jit(solution)/shard_map/ppermute | solution.py:27
  17.4 0.7 local_part.7.base_ref
  18.1 1.7 %collective-permute-done.7.yb_ref = f32[5,8,128]{2,1,0:T(8,128)S(1)} collective-permute-done((f32[5,8,128]{2,1,0:T(8,128)S(1)}, f32[5,8,128]{2,1,0:T(8,128)S(1)}, u32[]{:S(2)}, u32[]{:S(2)}) %collective-permute-start.7) | collective-permute-done | bytes 20512 | tf_op jit(solution)/shard_map/ppermute | solution.py:27
  19.7 1.2 %collective-permute-done.5.xb_ref = f32[5,16,256]{2,1,0:T(8,128)S(1)} collective-permute-done((f32[5,16,256]{2,1,0:T(8,128)S(1)}, f32[5,16,256]{2,1,0:T(8,128)S(1)}, u32[]{:S(2)}, u32[]{:S(2)}) %collective-permute-start.5) | collective-permute-done | bytes 81952 | tf_op jit(solution)/shard_map/ppermute | solution.py:27
  21.3 2.1 %collective-permute-start.9 = (f32[5,16,256]{2,1,0:T(8,128)S(1)}, f32[5,16,256]{2,1,0:T(8,128)S(1)}, u32[]{:S(2)}, u32[]{:S(2)}) collective-permute-start(f32[5,16,256]{2,1,0:T(8,128)S(1)} %get-tuple-element.59), channel_id=1, source_target_pairs={{0,24},{8,16},{16,8},{24,0},{1,25},{9,17},{17,9},{25,1},{2,26},{10... | collective-permute-start | bytes 245768 | tf_op jit(solution)/shard_map/ppermute | solution.py:27
  23.4 1.2 %collective-permute-start.11 = (f32[5,8,128]{2,1,0:T(8,128)S(1)}, f32[5,8,128]{2,1,0:T(8,128)S(1)}, u32[]{:S(2)}, u32[]{:S(2)}) collective-permute-start(f32[5,8,128]{2,1,0:T(8,128)S(1)} %get-tuple-element.61), channel_id=1, source_target_pairs={{0,7},{1,2},{2,1},{3,4},{4,3},{5,6},{6,5},{7,0},{8,15},{9,10},{10,... | collective-permute-start | bytes 61448 | tf_op jit(solution)/shard_map/ppermute | solution.py:27
  24.9 0.8 local_part.8.base_ref
  25.7 1.8 %collective-permute-done.11.yb_ref = f32[5,8,128]{2,1,0:T(8,128)S(1)} collective-permute-done((f32[5,8,128]{2,1,0:T(8,128)S(1)}, f32[5,8,128]{2,1,0:T(8,128)S(1)}, u32[]{:S(2)}, u32[]{:S(2)}) %collective-permute-start.11) | collective-permute-done | bytes 20512 | tf_op jit(solution)/shard_map/ppermute | solution.py:27
  27.9 3.4 %copy-done.5 = f32[1,64,64,512]{3,2,1,0:T(8,128)S(1)} copy-done((f32[1,64,64,512]{3,2,1,0:T(8,128)S(1)}, f32[1,64,64,512]{3,2,1,0:T(8,128)}, u32[]{:S(2)}) %copy-start.5) | copy-done | bytes 8388632
  31.3 2.4 %project.3 = (f32[168,128]{1,0:T(8,128)S(1)}, f32[168,128]{1,0:T(8,128)S(1)}, f32[168,128]{1,0:T(8,128)S(1)}, f32[168,128]{1,0:T(8,128)S(1)}, f32[168,128]{1,0:T...) custom-call(f32[5,64,256]{2,1,0:T(8,128)S(1)} %finish.8.refs_0_, ...), custom_call_target="tpu_custom_call" | custom-call | flops 5000000000 | bytes 20971520 | tf_op jit(solution)/shard_map/project/pallas_call | solution.py:456
  33.7 1.4 %collective-permute-start.20 = (f32[168,128]{1,0:T(8,128)S(1)}, f32[168,128]{1,0:T(8,128)S(1)}, u32[]{:S(2)}, u32[]{:S(2)}) collective-permute-start(f32[168,128]{1,0:T(8,128)S(1)} %get-tuple-element.73), channel_id=1, source_target_pairs={{0,2},{1,3},{2,0},{3,1},{4,6},{5,7},{6,4},{7,5},{8,10},{9,11},{10,... | collective-permute-start | bytes 258056 | tf_op jit(solution)/shard_map/ppermute | solution.py:529
  35.6 1.4 %collective-permute-start.22 = (f32[168,128]{1,0:T(8,128)S(1)}, f32[168,128]{1,0:T(8,128)S(1)}, u32[]{:S(2)}, u32[]{:S(2)}) collective-permute-start(f32[168,128]{1,0:T(8,128)S(1)} %get-tuple-element.75), channel_id=1, source_target_pairs={{0,4},{1,5},{2,6},{3,7},{4,0},{5,1},{6,2},{7,3},{8,12},{9,13},{10,... | collective-permute-start | bytes 258056 | tf_op jit(solution)/shard_map/ppermute | solution.py:529
  37.0 2.4 %project.2 = (f32[168,128]{1,0:T(8,128)S(1)}, f32[168,128]{1,0:T(8,128)S(1)}, f32[168,128]{1,0:T(8,128)S(1)}, f32[168,128]{1,0:T(8,128)S(1)}, f32[168,128]{1,0:T...) custom-call(f32[5,64,256]{2,1,0:T(8,128)S(1)} %finish.8.refs_0_, ...), custom_call_target="tpu_custom_call" | custom-call | flops 5000000000 | bytes 20971520 | tf_op jit(solution)/shard_map/project/pallas_call | solution.py:456
  39.7 1.6 %collective-permute-start.24 = (f32[168,128]{1,0:T(8,128)S(1)}, f32[168,128]{1,0:T(8,128)S(1)}, u32[]{:S(2)}, u32[]{:S(2)}) collective-permute-start(f32[168,128]{1,0:T(8,128)S(1)} %get-tuple-element.77), channel_id=1, source_target_pairs={{0,6},{1,7},{2,4},{3,5},{4,2},{5,3},{6,0},{7,1},{8,14},{9,15},{10,... | collective-permute-start | bytes 258056 | tf_op jit(solution)/shard_map/ppermute | solution.py:529
  41.3 1.1 %collective-permute-start.25 = (f32[168,128]{1,0:T(8,128)S(1)}, f32[168,128]{1,0:T(8,128)S(1)}, u32[]{:S(2)}, u32[]{:S(2)}) collective-permute-start(f32[168,128]{1,0:T(8,128)S(1)} %get-tuple-element.78), channel_id=1, source_target_pairs={{0,7},{1,6},{2,5},{3,4},{4,3},{5,2},{6,1},{7,0},{8,15},{9,14},{10,... | collective-permute-start | bytes 258056 | tf_op jit(solution)/shard_map/ppermute | solution.py:529
  42.8 1.4 %collective-permute-start.13 = (f32[168,128]{1,0:T(8,128)S(1)}, f32[168,128]{1,0:T(8,128)S(1)}, u32[]{:S(2)}, u32[]{:S(2)}) collective-permute-start(f32[168,128]{1,0:T(8,128)S(1)} %get-tuple-element.65), channel_id=1, source_target_pairs={{0,2},{1,3},{2,0},{3,1},{4,6},{5,7},{6,4},{7,5},{8,10},{9,11},{10,... | collective-permute-start | bytes 258056 | tf_op jit(solution)/shard_map/ppermute | solution.py:529
  44.7 2.0 %collective-permute-done.24.refs_6_ = f32[168,128]{1,0:T(8,128)S(1)} collective-permute-done((f32[168,128]{1,0:T(8,128)S(1)}, f32[168,128]{1,0:T(8,128)S(1)}, u32[]{:S(2)}, u32[]{:S(2)}) %collective-permute-start.24) | collective-permute-done | bytes 86048 | tf_op jit(solution)/shard_map/ppermute | solution.py:529
  46.6 1.2 %collective-permute-start.15 = (f32[168,128]{1,0:T(8,128)S(1)}, f32[168,128]{1,0:T(8,128)S(1)}, u32[]{:S(2)}, u32[]{:S(2)}) collective-permute-start(f32[168,128]{1,0:T(8,128)S(1)} %get-tuple-element.67), channel_id=1, source_target_pairs={{0,4},{1,5},{2,6},{3,7},{4,0},{5,1},{6,2},{7,3},{8,12},{9,13},{10,... | collective-permute-start | bytes 258056 | tf_op jit(solution)/shard_map/ppermute | solution.py:529
  48.0 0.9 %collective-permute-start.16 = (f32[168,128]{1,0:T(8,128)S(1)}, f32[168,128]{1,0:T(8,128)S(1)}, u32[]{:S(2)}, u32[]{:S(2)}) collective-permute-start(f32[168,128]{1,0:T(8,128)S(1)} %get-tuple-element.68), channel_id=1, source_target_pairs={{0,5},{1,4},{2,7},{3,6},{4,1},{5,0},{6,3},{7,2},{8,13},{9,12},{10,... | collective-permute-start | bytes 258056 | tf_op jit(solution)/shard_map/ppermute | solution.py:529
  48.9 1.5 %collective-permute-start.17 = (f32[168,128]{1,0:T(8,128)S(1)}, f32[168,128]{1,0:T(8,128)S(1)}, u32[]{:S(2)}, u32[]{:S(2)}) collective-permute-start(f32[168,128]{1,0:T(8,128)S(1)} %get-tuple-element.69), channel_id=1, source_target_pairs={{0,6},{1,7},{2,4},{3,5},{4,2},{5,3},{6,0},{7,1},{8,14},{9,15},{10,... | collective-permute-start | bytes 258056 | tf_op jit(solution)/shard_map/ppermute | solution.py:529
  50.4 1.1 %collective-permute-start.18 = (f32[168,128]{1,0:T(8,128)S(1)}, f32[168,128]{1,0:T(8,128)S(1)}, u32[]{:S(2)}, u32[]{:S(2)}) collective-permute-start(f32[168,128]{1,0:T(8,128)S(1)} %get-tuple-element.70), channel_id=1, source_target_pairs={{0,7},{1,6},{2,5},{3,4},{4,3},{5,2},{6,1},{7,0},{8,15},{9,14},{10,... | collective-permute-start | bytes 258056 | tf_op jit(solution)/shard_map/ppermute | solution.py:529
  52.8 2.9 %collective-permute-done.17.refs_6_ = f32[168,128]{1,0:T(8,128)S(1)} collective-permute-done((f32[168,128]{1,0:T(8,128)S(1)}, f32[168,128]{1,0:T(8,128)S(1)}, u32[]{:S(2)}, u32[]{:S(2)}) %collective-permute-start.17) | collective-permute-done | bytes 86048 | tf_op jit(solution)/shard_map/ppermute | solution.py:529
  55.7 1.5 %collective-permute-done.18.refs_7_ = f32[168,128]{1,0:T(8,128)S(1)} collective-permute-done((f32[168,128]{1,0:T(8,128)S(1)}, f32[168,128]{1,0:T(8,128)S(1)}, u32[]{:S(2)}, u32[]{:S(2)}) %collective-permute-start.18) | collective-permute-done | bytes 86048 | tf_op jit(solution)/shard_map/ppermute | solution.py:529
  57.2 0.7 receive.3
  58.1 2.2 %collective-permute-start.27 = (f32[5,16,256]{2,1,0:T(8,128)S(1)}, f32[5,16,256]{2,1,0:T(8,128)S(1)}, u32[]{:S(2)}, u32[]{:S(2)}) collective-permute-start(f32[5,16,256]{2,1,0:T(8,128)S(1)} %get-tuple-element.81), channel_id=1, source_target_pairs={{0,24},{8,16},{16,8},{24,0},{1,25},{9,17},{17,9},{25,1},{2,26},{10... | collective-permute-start | bytes 245768 | tf_op jit(solution)/shard_map/ppermute | solution.py:27
  60.3 1.4 %collective-permute-start.29 = (f32[5,8,128]{2,1,0:T(8,128)S(1)}, f32[5,8,128]{2,1,0:T(8,128)S(1)}, u32[]{:S(2)}, u32[]{:S(2)}) collective-permute-start(f32[5,8,128]{2,1,0:T(8,128)S(1)} %get-tuple-element.83), channel_id=1, source_target_pairs={{0,7},{1,2},{2,1},{3,4},{4,3},{5,6},{6,5},{7,0},{8,15},{9,10},{10,... | collective-permute-start | bytes 61448 | tf_op jit(solution)/shard_map/ppermute | solution.py:27
  61.7 0.7 local_part.9.base_ref
  62.4 2.0 %collective-permute-done.29.yb_ref = f32[5,8,128]{2,1,0:T(8,128)S(1)} collective-permute-done((f32[5,8,128]{2,1,0:T(8,128)S(1)}, f32[5,8,128]{2,1,0:T(8,128)S(1)}, u32[]{:S(2)}, u32[]{:S(2)}) %collective-permute-start.29) | collective-permute-done | bytes 20512 | tf_op jit(solution)/shard_map/ppermute | solution.py:27
  64.7 1.5 %collective-permute-start.30 = (f32[5,16,256]{2,1,0:T(8,128)S(1)}, f32[5,16,256]{2,1,0:T(8,128)S(1)}, u32[]{:S(2)}, u32[]{:S(2)}) collective-permute-start(f32[5,16,256]{2,1,0:T(8,128)S(1)} %get-tuple-element.85), channel_id=1, source_target_pairs={{0,8},{8,0},{16,24},{24,16},{1,9},{9,1},{17,25},{25,17},{2,10},{10... | collective-permute-start | bytes 245768 | tf_op jit(solution)/shard_map/ppermute | solution.py:27
  66.3 1.8 %collective-permute-start.31 = (f32[5,16,256]{2,1,0:T(8,128)S(1)}, f32[5,16,256]{2,1,0:T(8,128)S(1)}, u32[]{:S(2)}, u32[]{:S(2)}) collective-permute-start(f32[5,16,256]{2,1,0:T(8,128)S(1)} %get-tuple-element.86), channel_id=1, source_target_pairs={{0,24},{8,16},{16,8},{24,0},{1,25},{9,17},{17,9},{25,1},{2,26},{10... | collective-permute-start | bytes 245768 | tf_op jit(solution)/shard_map/ppermute | solution.py:27
  68.0 1.6 %collective-permute-start.33 = (f32[5,8,128]{2,1,0:T(8,128)S(1)}, f32[5,8,128]{2,1,0:T(8,128)S(1)}, u32[]{:S(2)}, u32[]{:S(2)}) collective-permute-start(f32[5,8,128]{2,1,0:T(8,128)S(1)} %get-tuple-element.88), channel_id=1, source_target_pairs={{0,7},{1,2},{2,1},{3,4},{4,3},{5,6},{6,5},{7,0},{8,15},{9,10},{10,... | collective-permute-start | bytes 61448 | tf_op jit(solution)/shard_map/ppermute | solution.py:27
  69.6 0.7 local_part.10.base_ref
  70.3 1.8 %collective-permute-done.33.yb_ref = f32[5,8,128]{2,1,0:T(8,128)S(1)} collective-permute-done((f32[5,8,128]{2,1,0:T(8,128)S(1)}, f32[5,8,128]{2,1,0:T(8,128)S(1)}, u32[]{:S(2)}, u32[]{:S(2)}) %collective-permute-start.33) | collective-permute-done | bytes 20512 | tf_op jit(solution)/shard_map/ppermute | solution.py:27
  72.8 1.8 %collective-permute-start.35 = (f32[5,16,256]{2,1,0:T(8,128)S(1)}, f32[5,16,256]{2,1,0:T(8,128)S(1)}, u32[]{:S(2)}, u32[]{:S(2)}) collective-permute-start(f32[5,16,256]{2,1,0:T(8,128)S(1)} %get-tuple-element.91), channel_id=1, source_target_pairs={{0,24},{8,16},{16,8},{24,0},{1,25},{9,17},{17,9},{25,1},{2,26},{10... | collective-permute-start | bytes 245768 | tf_op jit(solution)/shard_map/ppermute | solution.py:27
  74.6 2.4 %collective-permute-start.37 = (f32[5,8,128]{2,1,0:T(8,128)S(1)}, f32[5,8,128]{2,1,0:T(8,128)S(1)}, u32[]{:S(2)}, u32[]{:S(2)}) collective-permute-start(f32[5,8,128]{2,1,0:T(8,128)S(1)} %get-tuple-element.93), channel_id=1, source_target_pairs={{0,7},{1,2},{2,1},{3,4},{4,3},{5,6},{6,5},{7,0},{8,15},{9,10},{10,... | collective-permute-start | bytes 61448 | tf_op jit(solution)/shard_map/ppermute | solution.py:27
  77.0 0.8 local_part.11.base_ref
  77.8 0.9 %collective-permute-done.37.yb_ref = f32[5,8,128]{2,1,0:T(8,128)S(1)} collective-permute-done((f32[5,8,128]{2,1,0:T(8,128)S(1)}, f32[5,8,128]{2,1,0:T(8,128)S(1)}, u32[]{:S(2)}, u32[]{:S(2)}) %collective-permute-start.37) | collective-permute-done | bytes 20512 | tf_op jit(solution)/shard_map/ppermute | solution.py:27
  79.2 0.9 %finish.11 = f32[5,64,256]{2,1,0:T(8,128)} custom-call(f32[3,5,64,256]{3,2,1,0:T(8,128)S(1)} %bitcast.18, f32[5,64,256]{2,1,0:T(8,128)S(1)} %local_part.11.base_ref, f32[5,16,256]{2,1,0:T(8,128)S(1)} %collective-permute-done.34.xa_ref, f32[5,16,256]{2,1,0:T(8,128)S(1)} %collective-permute-done.35.xb_ref, f32[5,8,128]{2,1,0:T(8,128)S(1)} %collective-permute-done.36.ya_ref, ...), custom_call_target="tpu_custom_call" | custom-call | tf_op jit(solution)/shard_map/finish/pallas_call | solution.py:377
  (66 shorter events, 5.8 us)
Async XLA Ops:
  0.6 1.0 %copy-start.2 = (f32[1,5,64,256]{3,2,1,0:T(8,128)S(1)}, f32[1,5,64,256]{3,2,1,0:T(8,128)}, u32[]{:S(2)}) copy-start(f32[1,5,64,256]{3,2,1,0:T(8,128)} %param.6) | copy-start | bytes 983044
  1.6 15.7 %copy-start.6 = (s32[1,512,1]{1,2,0:T(1,128)S(1)}, s32[1,512,1]{1,2,0:T(1,128)}, u32[]{:S(2)}) copy-start(s32[1,512,1]{1,2,0:T(1,128)} %param.9) | copy-start | bytes 6148
  1.7 12.1 %collective-permute-start = (f32[5,16,256]{2,1,0:T(8,128)S(1)}, f32[5,16,256]{2,1,0:T(8,128)S(1)}, u32[]{:S(2)}, u32[]{:S(2)}) collective-permute-start(f32[5,16,256]{2,1,0:T(8,128)S(1)} %get-tuple-element.48), channel_id=1, source_target_pairs={{0,8},{8,0},{16,24},{24,16},{1,9},{9,1},{17,25},{25,17},{2,10},{10... | collective-permute-start | bytes 245768 | tf_op jit(solution)/shard_map/ppermute | solution.py:27
  4.8 9.0 %collective-permute-start.1 = (f32[5,16,256]{2,1,0:T(8,128)S(1)}, f32[5,16,256]{2,1,0:T(8,128)S(1)}, u32[]{:S(2)}, u32[]{:S(2)}) collective-permute-start(f32[5,16,256]{2,1,0:T(8,128)S(1)} %get-tuple-element.49), channel_id=1, source_target_pairs={{0,24},{8,16},{16,8},{24,0},{1,25},{9,17},{17,9},{25,1},{2,26},{10... | collective-permute-start | bytes 245768 | tf_op jit(solution)/shard_map/ppermute | solution.py:27
  7.3 6.5 %collective-permute-start.2 = (f32[5,8,128]{2,1,0:T(8,128)S(1)}, f32[5,8,128]{2,1,0:T(8,128)S(1)}, u32[]{:S(2)}, u32[]{:S(2)}) collective-permute-start(f32[5,8,128]{2,1,0:T(8,128)S(1)} %get-tuple-element.50), channel_id=1, source_target_pairs={{0,1},{1,0},{2,3},{3,2},{4,5},{5,4},{6,7},{7,6},{8,9},{9,8},{10,11... | collective-permute-start | bytes 61448 | tf_op jit(solution)/shard_map/ppermute | solution.py:27
  7.3 6.5 %collective-permute-start.3 = (f32[5,8,128]{2,1,0:T(8,128)S(1)}, f32[5,8,128]{2,1,0:T(8,128)S(1)}, u32[]{:S(2)}, u32[]{:S(2)}) collective-permute-start(f32[5,8,128]{2,1,0:T(8,128)S(1)} %get-tuple-element.51), channel_id=1, source_target_pairs={{0,7},{1,2},{2,1},{3,4},{4,3},{5,6},{6,5},{7,0},{8,15},{9,10},{10,... | collective-permute-start | bytes 61448 | tf_op jit(solution)/shard_map/ppermute | solution.py:27
  10.8 1.2 %copy-start = (f32[1,3,5,64,256]{4,3,2,1,0:T(8,128)S(1)}, f32[1,3,5,64,256]{4,3,2,1,0:T(8,128)}, u32[]{:S(2)}) copy-start(f32[1,3,5,64,256]{4,3,2,1,0:T(8,128)} %param.7) | copy-start | bytes 2949124
  12.0 1.0 %copy-start.3 = (f32[1,5,64,256]{3,2,1,0:T(8,128)S(1)}, f32[1,5,64,256]{3,2,1,0:T(8,128)}, u32[]{:S(2)}) copy-start(f32[1,5,64,256]{3,2,1,0:T(8,128)} %param.6) | copy-start | bytes 983044
  14.0 5.8 %collective-permute-start.4 = (f32[5,16,256]{2,1,0:T(8,128)S(1)}, f32[5,16,256]{2,1,0:T(8,128)S(1)}, u32[]{:S(2)}, u32[]{:S(2)}) collective-permute-start(f32[5,16,256]{2,1,0:T(8,128)S(1)} %get-tuple-element.53), channel_id=1, source_target_pairs={{0,8},{8,0},{16,24},{24,16},{1,9},{9,1},{17,25},{25,17},{2,10},{10... | collective-permute-start | bytes 245768 | tf_op jit(solution)/shard_map/ppermute | solution.py:27
  14.7 6.2 %collective-permute-start.5 = (f32[5,16,256]{2,1,0:T(8,128)S(1)}, f32[5,16,256]{2,1,0:T(8,128)S(1)}, u32[]{:S(2)}, u32[]{:S(2)}) collective-permute-start(f32[5,16,256]{2,1,0:T(8,128)S(1)} %get-tuple-element.54), channel_id=1, source_target_pairs={{0,24},{8,16},{16,8},{24,0},{1,25},{9,17},{17,9},{25,1},{2,26},{10... | collective-permute-start | bytes 245768 | tf_op jit(solution)/shard_map/ppermute | solution.py:27
  15.6 2.5 %collective-permute-start.6 = (f32[5,8,128]{2,1,0:T(8,128)S(1)}, f32[5,8,128]{2,1,0:T(8,128)S(1)}, u32[]{:S(2)}, u32[]{:S(2)}) collective-permute-start(f32[5,8,128]{2,1,0:T(8,128)S(1)} %get-tuple-element.55), channel_id=1, source_target_pairs={{0,1},{1,0},{2,3},{3,2},{4,5},{5,4},{6,7},{7,6},{8,9},{9,8},{10,11... | collective-permute-start | bytes 61448 | tf_op jit(solution)/shard_map/ppermute | solution.py:27
  15.6 4.1 %collective-permute-start.7 = (f32[5,8,128]{2,1,0:T(8,128)S(1)}, f32[5,8,128]{2,1,0:T(8,128)S(1)}, u32[]{:S(2)}, u32[]{:S(2)}) collective-permute-start(f32[5,8,128]{2,1,0:T(8,128)S(1)} %get-tuple-element.56), channel_id=1, source_target_pairs={{0,7},{1,2},{2,1},{3,4},{4,3},{5,6},{6,5},{7,0},{8,15},{9,10},{10,... | collective-permute-start | bytes 61448 | tf_op jit(solution)/shard_map/ppermute | solution.py:27
  17.3 7.5 %copy-start.7 = (s32[1,512]{1,0:T(1,128)S(1)}, s32[1,512]{1,0:T(1,128)}, u32[]{:S(2)}) copy-start(s32[1,512]{1,0:T(1,128)} %param.10) | copy-start | bytes 6148
  17.3 7.5 %copy-start.4 = (f32[1,5,64,256]{3,2,1,0:T(8,128)S(1)}, f32[1,5,64,256]{3,2,1,0:T(8,128)}, u32[]{:S(2)}) copy-start(f32[1,5,64,256]{3,2,1,0:T(8,128)} %param.6) | copy-start | bytes 983044
  21.2 6.3 %collective-permute-start.8 = (f32[5,16,256]{2,1,0:T(8,128)S(1)}, f32[5,16,256]{2,1,0:T(8,128)S(1)}, u32[]{:S(2)}, u32[]{:S(2)}) collective-permute-start(f32[5,16,256]{2,1,0:T(8,128)S(1)} %get-tuple-element.58), channel_id=1, source_target_pairs={{0,8},{8,0},{16,24},{24,16},{1,9},{9,1},{17,25},{25,17},{2,10},{10... | collective-permute-start | bytes 245768 | tf_op jit(solution)/shard_map/ppermute | solution.py:27
  21.3 6.4 %collective-permute-start.9 = (f32[5,16,256]{2,1,0:T(8,128)S(1)}, f32[5,16,256]{2,1,0:T(8,128)S(1)}, u32[]{:S(2)}, u32[]{:S(2)}) collective-permute-start(f32[5,16,256]{2,1,0:T(8,128)S(1)} %get-tuple-element.59), channel_id=1, source_target_pairs={{0,24},{8,16},{16,8},{24,0},{1,25},{9,17},{17,9},{25,1},{2,26},{10... | collective-permute-start | bytes 245768 | tf_op jit(solution)/shard_map/ppermute | solution.py:27
  23.4 2.3 %collective-permute-start.10 = (f32[5,8,128]{2,1,0:T(8,128)S(1)}, f32[5,8,128]{2,1,0:T(8,128)S(1)}, u32[]{:S(2)}, u32[]{:S(2)}) collective-permute-start(f32[5,8,128]{2,1,0:T(8,128)S(1)} %get-tuple-element.60), channel_id=1, source_target_pairs={{0,1},{1,0},{2,3},{3,2},{4,5},{5,4},{6,7},{7,6},{8,9},{9,8},{10,11... | collective-permute-start | bytes 61448 | tf_op jit(solution)/shard_map/ppermute | solution.py:27
  23.4 4.1 %collective-permute-start.11 = (f32[5,8,128]{2,1,0:T(8,128)S(1)}, f32[5,8,128]{2,1,0:T(8,128)S(1)}, u32[]{:S(2)}, u32[]{:S(2)}) collective-permute-start(f32[5,8,128]{2,1,0:T(8,128)S(1)} %get-tuple-element.61), channel_id=1, source_target_pairs={{0,7},{1,2},{2,1},{3,4},{4,3},{5,6},{6,5},{7,0},{8,15},{9,10},{10,... | collective-permute-start | bytes 61448 | tf_op jit(solution)/shard_map/ppermute | solution.py:27
  27.9 3.4 %copy-start.5 = (f32[1,64,64,512]{3,2,1,0:T(8,128)S(1)}, f32[1,64,64,512]{3,2,1,0:T(8,128)}, u32[]{:S(2)}) copy-start(f32[1,64,64,512]{3,2,1,0:T(8,128)} %refs_1_.3) | copy-start | bytes 25165828
  33.6 6.1 %collective-permute-start.19 = (f32[168,128]{1,0:T(8,128)S(1)}, f32[168,128]{1,0:T(8,128)S(1)}, u32[]{:S(2)}, u32[]{:S(2)}) collective-permute-start(f32[168,128]{1,0:T(8,128)S(1)} %get-tuple-element.72), channel_id=1, source_target_pairs={{0,1},{1,0},{2,3},{3,2},{4,5},{5,4},{6,7},{7,6},{8,9},{9,8},{10,11... | collective-permute-start | bytes 258056 | tf_op jit(solution)/shard_map/ppermute | solution.py:529
  33.7 7.6 %collective-permute-start.20 = (f32[168,128]{1,0:T(8,128)S(1)}, f32[168,128]{1,0:T(8,128)S(1)}, u32[]{:S(2)}, u32[]{:S(2)}) collective-permute-start(f32[168,128]{1,0:T(8,128)S(1)} %get-tuple-element.73), channel_id=1, source_target_pairs={{0,2},{1,3},{2,0},{3,1},{4,6},{5,7},{6,4},{7,5},{8,10},{9,11},{10,... | collective-permute-start | bytes 258056 | tf_op jit(solution)/shard_map/ppermute | solution.py:529
  35.1 7.3 %collective-permute-start.21 = (f32[168,128]{1,0:T(8,128)S(1)}, f32[168,128]{1,0:T(8,128)S(1)}, u32[]{:S(2)}, u32[]{:S(2)}) collective-permute-start(f32[168,128]{1,0:T(8,128)S(1)} %get-tuple-element.74), channel_id=1, source_target_pairs={{0,3},{1,2},{2,1},{3,0},{4,7},{5,6},{6,5},{7,4},{8,11},{9,10},{10,... | collective-permute-start | bytes 258056 | tf_op jit(solution)/shard_map/ppermute | solution.py:529
  35.6 7.2 %collective-permute-start.22 = (f32[168,128]{1,0:T(8,128)S(1)}, f32[168,128]{1,0:T(8,128)S(1)}, u32[]{:S(2)}, u32[]{:S(2)}) collective-permute-start(f32[168,128]{1,0:T(8,128)S(1)} %get-tuple-element.75), channel_id=1, source_target_pairs={{0,4},{1,5},{2,6},{3,7},{4,0},{5,1},{6,2},{7,3},{8,12},{9,13},{10,... | collective-permute-start | bytes 258056 | tf_op jit(solution)/shard_map/ppermute | solution.py:529
  39.4 4.7 %collective-permute-start.23 = (f32[168,128]{1,0:T(8,128)S(1)}, f32[168,128]{1,0:T(8,128)S(1)}, u32[]{:S(2)}, u32[]{:S(2)}) collective-permute-start(f32[168,128]{1,0:T(8,128)S(1)} %get-tuple-element.76), channel_id=1, source_target_pairs={{0,5},{1,4},{2,7},{3,6},{4,1},{5,0},{6,3},{7,2},{8,13},{9,12},{10,... | collective-permute-start | bytes 258056 | tf_op jit(solution)/shard_map/ppermute | solution.py:529
  39.7 6.9 %collective-permute-start.24 = (f32[168,128]{1,0:T(8,128)S(1)}, f32[168,128]{1,0:T(8,128)S(1)}, u32[]{:S(2)}, u32[]{:S(2)}) collective-permute-start(f32[168,128]{1,0:T(8,128)S(1)} %get-tuple-element.77), channel_id=1, source_target_pairs={{0,6},{1,7},{2,4},{3,5},{4,2},{5,3},{6,0},{7,1},{8,14},{9,15},{10,... | collective-permute-start | bytes 258056 | tf_op jit(solution)/shard_map/ppermute | solution.py:529
  41.3 6.7 %collective-permute-start.25 = (f32[168,128]{1,0:T(8,128)S(1)}, f32[168,128]{1,0:T(8,128)S(1)}, u32[]{:S(2)}, u32[]{:S(2)}) collective-permute-start(f32[168,128]{1,0:T(8,128)S(1)} %get-tuple-element.78), channel_id=1, source_target_pairs={{0,7},{1,6},{2,5},{3,4},{4,3},{5,2},{6,1},{7,0},{8,15},{9,14},{10,... | collective-permute-start | bytes 258056 | tf_op jit(solution)/shard_map/ppermute | solution.py:529
  42.4 6.5 %collective-permute-start.12 = (f32[168,128]{1,0:T(8,128)S(1)}, f32[168,128]{1,0:T(8,128)S(1)}, u32[]{:S(2)}, u32[]{:S(2)}) collective-permute-start(f32[168,128]{1,0:T(8,128)S(1)} %get-tuple-element.64), channel_id=1, source_target_pairs={{0,1},{1,0},{2,3},{3,2},{4,5},{5,4},{6,7},{7,6},{8,9},{9,8},{10,11... | collective-permute-start | bytes 258056 | tf_op jit(solution)/shard_map/ppermute | solution.py:529
  42.8 7.7 %collective-permute-start.13 = (f32[168,128]{1,0:T(8,128)S(1)}, f32[168,128]{1,0:T(8,128)S(1)}, u32[]{:S(2)}, u32[]{:S(2)}) collective-permute-start(f32[168,128]{1,0:T(8,128)S(1)} %get-tuple-element.65), channel_id=1, source_target_pairs={{0,2},{1,3},{2,0},{3,1},{4,6},{5,7},{6,4},{7,5},{8,10},{9,11},{10,... | collective-permute-start | bytes 258056 | tf_op jit(solution)/shard_map/ppermute | solution.py:529
  44.1 8.2 %collective-permute-start.14 = (f32[168,128]{1,0:T(8,128)S(1)}, f32[168,128]{1,0:T(8,128)S(1)}, u32[]{:S(2)}, u32[]{:S(2)}) collective-permute-start(f32[168,128]{1,0:T(8,128)S(1)} %get-tuple-element.66), channel_id=1, source_target_pairs={{0,3},{1,2},{2,1},{3,0},{4,7},{5,6},{6,5},{7,4},{8,11},{9,10},{10,... | collective-permute-start | bytes 258056 | tf_op jit(solution)/shard_map/ppermute | solution.py:529
  46.6 5.7 %collective-permute-start.15 = (f32[168,128]{1,0:T(8,128)S(1)}, f32[168,128]{1,0:T(8,128)S(1)}, u32[]{:S(2)}, u32[]{:S(2)}) collective-permute-start(f32[168,128]{1,0:T(8,128)S(1)} %get-tuple-element.67), channel_id=1, source_target_pairs={{0,4},{1,5},{2,6},{3,7},{4,0},{5,1},{6,2},{7,3},{8,12},{9,13},{10,... | collective-permute-start | bytes 258056 | tf_op jit(solution)/shard_map/ppermute | solution.py:529
  48.0 4.8 %collective-permute-start.16 = (f32[168,128]{1,0:T(8,128)S(1)}, f32[168,128]{1,0:T(8,128)S(1)}, u32[]{:S(2)}, u32[]{:S(2)}) collective-permute-start(f32[168,128]{1,0:T(8,128)S(1)} %get-tuple-element.68), channel_id=1, source_target_pairs={{0,5},{1,4},{2,7},{3,6},{4,1},{5,0},{6,3},{7,2},{8,13},{9,12},{10,... | collective-permute-start | bytes 258056 | tf_op jit(solution)/shard_map/ppermute | solution.py:529
  48.9 6.8 %collective-permute-start.17 = (f32[168,128]{1,0:T(8,128)S(1)}, f32[168,128]{1,0:T(8,128)S(1)}, u32[]{:S(2)}, u32[]{:S(2)}) collective-permute-start(f32[168,128]{1,0:T(8,128)S(1)} %get-tuple-element.69), channel_id=1, source_target_pairs={{0,6},{1,7},{2,4},{3,5},{4,2},{5,3},{6,0},{7,1},{8,14},{9,15},{10,... | collective-permute-start | bytes 258056 | tf_op jit(solution)/shard_map/ppermute | solution.py:529
  50.4 6.8 %collective-permute-start.18 = (f32[168,128]{1,0:T(8,128)S(1)}, f32[168,128]{1,0:T(8,128)S(1)}, u32[]{:S(2)}, u32[]{:S(2)}) collective-permute-start(f32[168,128]{1,0:T(8,128)S(1)} %get-tuple-element.70), channel_id=1, source_target_pairs={{0,7},{1,6},{2,5},{3,4},{4,3},{5,2},{6,1},{7,0},{8,15},{9,14},{10,... | collective-permute-start | bytes 258056 | tf_op jit(solution)/shard_map/ppermute | solution.py:529
  52.3 9.4 %copy-start.1 = (f32[1,3,5,64,256]{4,3,2,1,0:T(8,128)S(1)}, f32[1,3,5,64,256]{4,3,2,1,0:T(8,128)}, u32[]{:S(2)}) copy-start(f32[1,3,5,64,256]{4,3,2,1,0:T(8,128)} %param.8) | copy-start | bytes 2949124
  58.0 6.4 %collective-permute-start.26 = (f32[5,16,256]{2,1,0:T(8,128)S(1)}, f32[5,16,256]{2,1,0:T(8,128)S(1)}, u32[]{:S(2)}, u32[]{:S(2)}) collective-permute-start(f32[5,16,256]{2,1,0:T(8,128)S(1)} %get-tuple-element.80), channel_id=1, source_target_pairs={{0,8},{8,0},{16,24},{24,16},{1,9},{9,1},{17,25},{25,17},{2,10},{10... | collective-permute-start | bytes 245768 | tf_op jit(solution)/shard_map/ppermute | solution.py:27
  58.1 6.5 %collective-permute-start.27 = (f32[5,16,256]{2,1,0:T(8,128)S(1)}, f32[5,16,256]{2,1,0:T(8,128)S(1)}, u32[]{:S(2)}, u32[]{:S(2)}) collective-permute-start(f32[5,16,256]{2,1,0:T(8,128)S(1)} %get-tuple-element.81), channel_id=1, source_target_pairs={{0,24},{8,16},{16,8},{24,0},{1,25},{9,17},{17,9},{25,1},{2,26},{10... | collective-permute-start | bytes 245768 | tf_op jit(solution)/shard_map/ppermute | solution.py:27
  60.3 2.2 %collective-permute-start.28 = (f32[5,8,128]{2,1,0:T(8,128)S(1)}, f32[5,8,128]{2,1,0:T(8,128)S(1)}, u32[]{:S(2)}, u32[]{:S(2)}) collective-permute-start(f32[5,8,128]{2,1,0:T(8,128)S(1)} %get-tuple-element.82), channel_id=1, source_target_pairs={{0,1},{1,0},{2,3},{3,2},{4,5},{5,4},{6,7},{7,6},{8,9},{9,8},{10,11... | collective-permute-start | bytes 61448 | tf_op jit(solution)/shard_map/ppermute | solution.py:27
  60.3 4.1 %collective-permute-start.29 = (f32[5,8,128]{2,1,0:T(8,128)S(1)}, f32[5,8,128]{2,1,0:T(8,128)S(1)}, u32[]{:S(2)}, u32[]{:S(2)}) collective-permute-start(f32[5,8,128]{2,1,0:T(8,128)S(1)} %get-tuple-element.83), channel_id=1, source_target_pairs={{0,7},{1,2},{2,1},{3,4},{4,3},{5,6},{6,5},{7,0},{8,15},{9,10},{10,... | collective-permute-start | bytes 61448 | tf_op jit(solution)/shard_map/ppermute | solution.py:27
  64.7 7.4 %collective-permute-start.30 = (f32[5,16,256]{2,1,0:T(8,128)S(1)}, f32[5,16,256]{2,1,0:T(8,128)S(1)}, u32[]{:S(2)}, u32[]{:S(2)}) collective-permute-start(f32[5,16,256]{2,1,0:T(8,128)S(1)} %get-tuple-element.85), channel_id=1, source_target_pairs={{0,8},{8,0},{16,24},{24,16},{1,9},{9,1},{17,25},{25,17},{2,10},{10... | collective-permute-start | bytes 245768 | tf_op jit(solution)/shard_map/ppermute | solution.py:27
  66.3 6.2 %collective-permute-start.31 = (f32[5,16,256]{2,1,0:T(8,128)S(1)}, f32[5,16,256]{2,1,0:T(8,128)S(1)}, u32[]{:S(2)}, u32[]{:S(2)}) collective-permute-start(f32[5,16,256]{2,1,0:T(8,128)S(1)} %get-tuple-element.86), channel_id=1, source_target_pairs={{0,24},{8,16},{16,8},{24,0},{1,25},{9,17},{17,9},{25,1},{2,26},{10... | collective-permute-start | bytes 245768 | tf_op jit(solution)/shard_map/ppermute | solution.py:27
  68.0 2.3 %collective-permute-start.32 = (f32[5,8,128]{2,1,0:T(8,128)S(1)}, f32[5,8,128]{2,1,0:T(8,128)S(1)}, u32[]{:S(2)}, u32[]{:S(2)}) collective-permute-start(f32[5,8,128]{2,1,0:T(8,128)S(1)} %get-tuple-element.87), channel_id=1, source_target_pairs={{0,1},{1,0},{2,3},{3,2},{4,5},{5,4},{6,7},{7,6},{8,9},{9,8},{10,11... | collective-permute-start | bytes 61448 | tf_op jit(solution)/shard_map/ppermute | solution.py:27
  68.0 4.1 %collective-permute-start.33 = (f32[5,8,128]{2,1,0:T(8,128)S(1)}, f32[5,8,128]{2,1,0:T(8,128)S(1)}, u32[]{:S(2)}, u32[]{:S(2)}) collective-permute-start(f32[5,8,128]{2,1,0:T(8,128)S(1)} %get-tuple-element.88), channel_id=1, source_target_pairs={{0,7},{1,2},{2,1},{3,4},{4,3},{5,6},{6,5},{7,0},{8,15},{9,10},{10,... | collective-permute-start | bytes 61448 | tf_op jit(solution)/shard_map/ppermute | solution.py:27
  72.7 6.0 %collective-permute-start.34 = (f32[5,16,256]{2,1,0:T(8,128)S(1)}, f32[5,16,256]{2,1,0:T(8,128)S(1)}, u32[]{:S(2)}, u32[]{:S(2)}) collective-permute-start(f32[5,16,256]{2,1,0:T(8,128)S(1)} %get-tuple-element.90), channel_id=1, source_target_pairs={{0,8},{8,0},{16,24},{24,16},{1,9},{9,1},{17,25},{25,17},{2,10},{10... | collective-permute-start | bytes 245768 | tf_op jit(solution)/shard_map/ppermute | solution.py:27
  72.8 6.4 %collective-permute-start.35 = (f32[5,16,256]{2,1,0:T(8,128)S(1)}, f32[5,16,256]{2,1,0:T(8,128)S(1)}, u32[]{:S(2)}, u32[]{:S(2)}) collective-permute-start(f32[5,16,256]{2,1,0:T(8,128)S(1)} %get-tuple-element.91), channel_id=1, source_target_pairs={{0,24},{8,16},{16,8},{24,0},{1,25},{9,17},{17,9},{25,1},{2,26},{10... | collective-permute-start | bytes 245768 | tf_op jit(solution)/shard_map/ppermute | solution.py:27
  74.6 3.2 %collective-permute-start.36 = (f32[5,8,128]{2,1,0:T(8,128)S(1)}, f32[5,8,128]{2,1,0:T(8,128)S(1)}, u32[]{:S(2)}, u32[]{:S(2)}) collective-permute-start(f32[5,8,128]{2,1,0:T(8,128)S(1)} %get-tuple-element.92), channel_id=1, source_target_pairs={{0,1},{1,0},{2,3},{3,2},{4,5},{5,4},{6,7},{7,6},{8,9},{9,8},{10,11... | collective-permute-start | bytes 61448 | tf_op jit(solution)/shard_map/ppermute | solution.py:27
  74.6 4.1 %collective-permute-start.37 = (f32[5,8,128]{2,1,0:T(8,128)S(1)}, f32[5,8,128]{2,1,0:T(8,128)S(1)}, u32[]{:S(2)}, u32[]{:S(2)}) collective-permute-start(f32[5,8,128]{2,1,0:T(8,128)S(1)} %get-tuple-element.93), channel_id=1, source_target_pairs={{0,7},{1,2},{2,1},{3,4},{4,3},{5,6},{6,5},{7,0},{8,15},{9,10},{10,... | collective-permute-start | bytes 61448 | tf_op jit(solution)/shard_map/ppermute | solution.py:27

commit v2 on v1

--- a/solution.py
+++ b/solution.py
@@ -13,7 +13,7 @@
 step_rate = 0.01
 lift_scale = 6.0
 half_lift = 3.0
-vmem_limit = 40 * 1024 * 1024
+vmem_limit = 24 * 1024 * 1024
 VARS = 5
 LANES = 128
 
@@ -232,21 +232,24 @@
                 out_ref[var, 8 * i : 8 * i + 8, LANES * j : LANES * (j + 1)] = base + change
 
 
-def pack_faces(w_ref, halves, xa_ref, xb_ref, ya_ref, yb_ref):
-    even_x, even_y = even_places()
+def pack_x(lower, upper, xa_ref, xb_ref):
+    even_x, _ = even_places()
+    for var in range(VARS):
+        xa_ref[var] = jnp.where(even_x, upper[var], lower[var])
+        xb_ref[var] = jnp.where(even_x, lower[var], upper[var])
+
+
+def pack_y(low_of, high_of, ya_ref, yb_ref):
+    _, even_y = even_places()
     row, lane = iotas()
     low_rows = row < 4
     low_lanes = lane < 64
     for var in range(VARS):
-        lower = w_ref[var, 0:16, :]
-        upper = w_ref[var, 48:64, :]
-        xa_ref[var] = jnp.where(even_x, upper, lower)
-        xb_ref[var] = jnp.where(even_x, lower, upper)
-        low = [tile_of(w_ref, var, 2 * a, 0) for a in range(4)]
+        low = [low_of(var, a) for a in range(4)]
         left = jnp.where(low_rows, low[0], pltpu.roll(low[1], 4, 0))
         right = jnp.where(low_rows, low[2], pltpu.roll(low[3], 4, 0))
         lower = jnp.where(low_lanes, left, pltpu.roll(right, 64, 1))
-        high = [tile_of(w_ref, var, 2 * a + 1, halves - 1) for a in range(4)]
+        high = [high_of(var, a) for a in range(4)]
         left = jnp.where(low_rows, pltpu.roll(high[0], 4, 0), high[1])
         right = jnp.where(low_rows, pltpu.roll(high[2], 4, 0), high[3])
         upper = jnp.where(low_lanes, pltpu.roll(left, 64, 1), right)
@@ -254,8 +257,27 @@
         yb_ref[var] = jnp.where(even_y, lower, upper)
 
 
-def face_kernel(halves, w_ref, *out_refs):
-    pack_faces(w_ref, halves, *out_refs)
+def pack_faces(w_ref, halves, xa_ref, xb_ref, ya_ref, yb_ref):
+    lower = [w_ref[var, 0:16, :] for var in range(VARS)]
+    upper = [w_ref[var, 48:64, :] for var in range(VARS)]
+    pack_x(lower, upper, xa_ref, xb_ref)
+    pack_y(
+        lambda var, a: tile_of(w_ref, var, 2 * a, 0),
+        lambda var, a: tile_of(w_ref, var, 2 * a + 1, halves - 1),
+        ya_ref,
+        yb_ref,
+    )
+
+
+def face_kernel(halves, w_hbm, state_hbm, w_ref, state_ref, *refs):
+    sems = refs[-1]
+    first = pltpu.make_async_copy(w_hbm.at[0], w_ref, sems.at[0])
+    second = pltpu.make_async_copy(state_hbm.at[0], state_ref, sems.at[1])
+    first.start()
+    second.start()
+    first.wait()
+    pack_faces(w_ref, halves, *refs[:-1])
+    second.wait()
 
 
 def finish_kernel(
@@ -334,33 +356,113 @@
     ]
 
 
-def get_faces(w):
-    columns = w.shape[2]
-    return pl.pallas_call(
+def in_hbm(x):
+    return pltpu.with_memory_space_constraint(x, pltpu.HBM)
+
+
+def hbm_spec():
+    return pl.BlockSpec(memory_space=pltpu.HBM)
+
+
+def get_faces(w, states):
+    columns = w.shape[3]
+    shapes = [
+        jax.ShapeDtypeStruct(w.shape[1:], jnp.float32),
+        jax.ShapeDtypeStruct(states.shape[1:], jnp.float32),
+    ] + face_shapes(columns)
+    begin, states, *faces = pl.pallas_call(
         functools.partial(face_kernel, columns // LANES),
-        out_shape=face_shapes(columns),
-        in_specs=[vmem_spec()],
-        out_specs=[vmem_spec()] * 4,
+        out_shape=shapes,
+        in_specs=[hbm_spec()] * 2,
+        out_specs=[vmem_spec()] * len(shapes),
+        scratch_shapes=[pltpu.SemaphoreType.DMA((2,))],
         compiler_params=params(),
         name="faces",
-    )(w)
+    )(in_hbm(w), in_hbm(states))
+    return begin, states, faces
+
+
+def prepare_kernel(spans, group, direct, owner_ref, local_ref, block_ref, after_ref, *refs):
+    del after_ref
+    out_ref, placing_ref, extra_ref, sems = refs
+    copies = []
+    at = 0
+    for number, (start, size) in enumerate(spans):
+        copies.append(
+            pltpu.make_async_copy(
+                block_ref.at[0, :, start : start + size, :],
+                out_ref.at[:, at : at + size, :],
+                sems.at[number],
+            )
+        )
+        copies[-1].start()
+        at += size
+    places, slots = placing_ref.shape
+    capacity = places // group
+    target = owner_ref[...]
+    if direct:
+        here = lax.axis_index("gy") * lax.axis_size("gz") + lax.axis_index("gz")
+        target = jnp.bitwise_xor(target, here)
+    owner = lax.broadcasted_iota(jnp.int32, (group, slots), 0)
+    named = jnp.where(owner == target, np.float32(1), np.float32(0))
+    earlier = jnp.where(
+        lax.broadcasted_iota(jnp.int32, (slots, slots), 0)
+        < lax.broadcasted_iota(jnp.int32, (slots, slots), 1),
+        np.float32(1),
+        np.float32(0),
+    )
+    ranks = jnp.dot(
+        named.astype(jnp.bfloat16),
+        earlier.astype(jnp.bfloat16),
+        preferred_element_type=jnp.float32,
+    )
+    rank = jnp.sum(named * ranks, axis=0, keepdims=True).astype(jnp.int32)
+    place = target * capacity + rank
+    index = lax.broadcasted_iota(jnp.int32, (places, slots), 0)
+    placing_ref[...] = jnp.where(index == place, np.float32(1), np.float32(0)).astype(
+        jnp.bfloat16
+    )
+    extra_ref[...] = jnp.broadcast_to(local_ref[...].astype(jnp.float32), extra_ref.shape)
+    for copy in copies:
+        copy.wait()
+
+
+def prepare(owners, local, blocks, after, group, capacity, direct):
+    slots = blocks.shape[3]
+    return pl.pallas_call(
+        functools.partial(prepare_kernel, ((0, 16), (48, 16)), group, direct),
+        out_shape=[
+            jax.ShapeDtypeStruct((64, 32, slots), jnp.float32),
+            jax.ShapeDtypeStruct((group * capacity, slots), jnp.bfloat16),
+            jax.ShapeDtypeStruct((8, slots), jnp.float32),
+        ],
+        in_specs=[vmem_spec(), vmem_spec(), hbm_spec(), vmem_spec()],
+        out_specs=[vmem_spec()] * 3,
+        scratch_shapes=[pltpu.SemaphoreType.DMA((2,))],
+        compiler_params=params(),
+        name="prepare",
+    )(owners, local, in_hbm(blocks), after)
+
+
+def exchange_x(faces):
+    return swapped(faces[1], "gx", 1), swapped(faces[0], "gx", 0)
+
+
+def exchange_y(faces):
+    ring = ("gy", "gz")
+    return swapped(faces[1], ring, 1), swapped(faces[0], ring, 0)
 
 
 def exchange(faces):
-    xa, xb, ya, yb = faces
-    ring = ("gy", "gz")
-    xb = swapped(xb, "gx", 1)
-    xa = swapped(xa, "gx", 0)
-    yb = swapped(yb, ring, 1)
-    ya = swapped(ya, ring, 0)
+    xb, xa = exchange_x(faces[:2])
+    yb, ya = exchange_y(faces[2:])
     return xa, xb, ya, yb
 
 
-def section(states, index, w, faces, scale, extras, with_faces):
+def section(states, index, w, received, scale, extras, with_faces):
     columns = w.shape[2]
     halves = columns // LANES
     shape = jax.ShapeDtypeStruct(w.shape, jnp.float32)
-    received = exchange(faces)
     factors = tuple(f for _, f in extras)
     base = pl.pallas_call(
         functools.partial(local_kernel, scale, index, factors, halves),
@@ -374,7 +476,7 @@
         name="local_part",
     )(states, w, *[x for x, _ in extras])
     out_shape = [shape] + (face_shapes(columns) if with_faces else [])
-    return pl.pallas_call(
+    results = pl.pallas_call(
         functools.partial(finish_kernel, scale, index, with_faces, halves),
         out_shape=out_shape,
         in_specs=[vmem_spec()] * 6,
@@ -382,13 +484,16 @@
         compiler_params=params(),
         name="finish",
     )(states, base, *received)
-
-
-def reverse_step(states, begin, faces):
-    second, *faces = section(states, 2, begin, faces, 2.0 / 3.0, [], True)
-    first, *faces = section(states, 1, second, faces, 0.25, [], True)
+    if with_faces:
+        results = [results[0], exchange(results[1:])]
+    return results
+
+
+def reverse_step(states, begin, received):
+    second, received = section(states, 2, begin, received, 2.0 / 3.0, [], True)
+    first, received = section(states, 1, second, received, 0.25, [], True)
     (result,) = section(
-        states, 0, first, faces, 1.0, [(begin, 1.0 / 3.0), (second, 0.75)], False
+        states, 0, first, received, 1.0, [(begin, 1.0 / 3.0), (second, 0.75)], False
     )
     return result
 
@@ -401,15 +506,29 @@
     return high, middle, low
 
 
-def project_kernel(first, m_tiles, blocks, with_copy, *refs):
-    w_ref, block_ref, placing_ref, extra_ref = refs[:4]
-    out_refs = refs[4 : 4 + blocks]
-    held = refs[-2]
+X_TILES = (0, 1, 6, 7)
+REST_TILES = (2, 3, 4, 5)
+
+
+def project_kernel(tiles, sources, blocks, span, with_copy, *refs):
+    w_ref = refs[0]
+    block_refs = refs[1 : 1 + sources]
+    placing_ref, extra_ref = refs[1 + sources : 3 + sources]
+    at = 3 + sources + (1 if span else 0)
+    out_refs = refs[at : at + blocks]
+    held, sem = refs[-2:]
     if with_copy:
-        copy = pltpu.make_async_copy(w_ref, refs[4 + blocks], refs[-1].at[0])
+        copy = pltpu.make_async_copy(w_ref, refs[at + blocks], sem.at[0])
+        copy.start()
+    if span:
+        start, size = span
+        copy = pltpu.make_async_copy(
+            refs[at - 1].at[0, :, start : start + size, :], refs[at + blocks], sem.at[0]
+        )
         copy.start()
     halves = w_ref.shape[2] // LANES
-    for r in range(block_ref.shape[3] // LANES):
+    count = len(tiles) * VARS
+    for r in range(placing_ref.shape[1] // LANES):
         lanes = slice(LANES * r, LANES * (r + 1))
         half = r % halves
         w_lanes = slice(LANES * half, LANES * (half + 1))
@@ -420,43 +539,59 @@
             sums = list(sums)
             for s in range(8):
                 rows = [jnp.broadcast_to(group[s : s + 1], (8, LANES)) for group in groups]
-                for m in range(m_tiles):
-                    node = 8 * (first + m)
-                    block = block_ref[0, start + s, node : node + 8, lanes]
+                for m, (source, at) in enumerate(tiles):
+                    block = block_refs[source][start + s, 8 * at : 8 * at + 8, lanes]
                     for var in range(VARS):
                         q = m * VARS + var
                         sums[q] = sums[q] + block * rows[var]
             return tuple(sums)
 
-        start = tuple(jnp.zeros((8, LANES), jnp.float32) for _ in range(m_tiles * VARS))
+        start = tuple(jnp.zeros((8, LANES), jnp.float32) for _ in range(count))
         sums = lax.fori_loop(0, 8, body, start)
-        for q in range(m_tiles * VARS):
+        for q in range(count):
             held[8 * q : 8 * q + 8, lanes] = sums[q]
 
     values = jnp.concatenate([held[...], extra_ref[...]], axis=0)
     total = values.shape[0]
     pieces = jnp.concatenate(split_three(values), axis=0)
-    result = jnp.dot(pieces, placing_ref[...], preferred_element_type=jnp.float32)
+    result = lax.dot_general(
+        pieces,
+        placing_ref[...],
+        (((1,), (1,)), ((), ())),
+        preferred_element_type=jnp.float32,
+    )
     result = result[0:total] + result[total : 2 * total] + result[2 * total :]
+    per = result.shape[1] // blocks
     for g in range(blocks):
-        out_refs[g][...] = result[:, LANES * g : LANES * (g + 1)]
-    if with_copy:
+        for part in range(per // LANES):
+            at = per * g + LANES * part
+            out_refs[g][part] = result[:, at : at + LANES]
+    if with_copy or span:
         copy.wait()
 
 
-def project(w, blocks, placing, extra, first, m_tiles, with_copy):
-    slots = blocks.shape[3]
-    rows = m_tiles * VARS * 8
-    count = placing.shape[1] // LANES
-    out_shape = [jax.ShapeDtypeStruct((rows + 8, LANES), jnp.float32)] * count
-    out_specs = [vmem_spec()] * count
+def project(w, sources, placing, extra, tiles, outputs, load=None, with_copy=False):
+    slots = placing.shape[1]
+    rows = len(tiles) * VARS * 8
+    per = placing.shape[0] // outputs // LANES
+    operands = [w, *sources, placing, extra]
+    in_specs = [vmem_spec()] * len(operands)
+    out_shape = [jax.ShapeDtypeStruct((per, rows + 8, LANES), jnp.float32)] * outputs
+    out_specs = [vmem_spec()] * outputs
+    span = None
+    if load is not None:
+        blocks, span = load
+        operands.append(in_hbm(blocks))
+        in_specs.append(hbm_spec())
+        out_shape.append(jax.ShapeDtypeStruct((64, span[1], slots), jnp.float32))
+        out_specs.append(vmem_spec())
     if with_copy:
         out_shape.append(jax.ShapeDtypeStruct(w.shape, jnp.float32))
         out_specs.append(pl.BlockSpec(memory_space=pl.ANY))
-    return pl.pallas_call(
-        functools.partial(project_kernel, first * m_tiles, m_tiles, count, with_copy),
+    results = pl.pallas_call(
+        functools.partial(project_kernel, tiles, len(sources), outputs, span, with_copy),
         out_shape=out_shape,
-        in_specs=[vmem_spec()] * 4,
+        in_specs=in_specs,
         out_specs=out_specs,
         scratch_shapes=[
             pltpu.VMEM((rows, slots), jnp.float32),
@@ -464,51 +599,66 @@
         ],
         compiler_params=params(),
         cost_estimate=pl.CostEstimate(
-            flops=5 * 1000 * 1000 * 1000,
+            flops=1000 * 1000 * 1000 * len(tiles),
             bytes_accessed=4 * rows * 64 * slots,
             transcendentals=0,
         ),
         name="project",
-    )(w, blocks, placing, extra)
-
-
-def receive_kernel(blocks, node, m_tiles, last, halves, *refs):
-    out_ref = refs[blocks + (1 if last else 0)]
+    )(*operands)
+    return results[:outputs], results[outputs:]
+
+
+def add_slots(block_refs, firsts, rows, columns):
+    result = jnp.zeros((rows, columns), jnp.float32)
+    index = lax.broadcasted_iota(jnp.int32, (columns, LANES), 0)
+    for number, ref in enumerate(block_refs):
+        for g in range(1 if number < firsts else ref.shape[0]):
+            local = ref[g, rows : rows + 1, :].astype(jnp.int32)
+            spot = (index == local).astype(jnp.float32).astype(jnp.bfloat16)
+            for piece in split_three(ref[g, 0:rows, :]):
+                result = result + lax.dot_general(
+                    piece, spot, (((1,), (1,)), ((), ())), preferred_element_type=jnp.float32
+                )
+    return result
+
+
+def receive_x_kernel(count, firsts, *refs):
+    out_ref, xa_ref, xb_ref = refs[count:]
+    rows, columns = out_ref.shape
+    result = add_slots(refs[:count], firsts, rows, columns)
+    out_ref[...] = result
+
+    def tile(m, var):
+        q = m * VARS + var
+        return result[8 * q : 8 * q + 8]
+
+    lower = [jnp.concatenate([tile(0, v), tile(1, v)], axis=0) for v in range(VARS)]
+    upper = [jnp.concatenate([tile(2, v), tile(3, v)], axis=0) for v in range(VARS)]
+    pack_x(lower, upper, xa_ref, xb_ref)
+
+
+def receive_rest_kernel(count, firsts, halves, *refs):
+    x_ref, out_ref, ya_ref, yb_ref = refs[count:]
     columns = out_ref.shape[2]
-    rows = m_tiles * VARS * 8
-    if last:
-        done_ref = refs[blocks]
-        for var in range(VARS):
-            out_ref[var, 0:node, :] = done_ref[var]
-    result = jnp.zeros((rows, columns), jnp.float32)
-    for g in range(blocks):
-        local = refs[g][rows : rows + 1, :].astype(jnp.int32)
-        index = lax.broadcasted_iota(jnp.int32, (columns, LANES), 0)
-        spot = (index == local).astype(jnp.float32).astype(jnp.bfloat16)
-        for piece in split_three(refs[g][0:rows, :]):
-            result = result + lax.dot_general(
-                piece, spot, (((1,), (1,)), ((), ())), preferred_element_type=jnp.float32
-            )
-    base = node if last else 0
-    for m in range(m_tiles):
-        for var in range(VARS):
-            q = m * VARS + var
-            out_ref[var, base + 8 * m : base + 8 * m + 8, :] = result[8 * q : 8 * q + 8, :]
-    if last:
-        pack_faces(out_ref, halves, *refs[blocks + 2 :])
-
-
-def receive(incoming, columns, node, m_tiles, done):
-    last = done is not None
-    if last:
-        shapes = [jax.ShapeDtypeStruct((VARS, 64, columns), jnp.float32)] + face_shapes(columns)
-    else:
-        shapes = [jax.ShapeDtypeStruct((VARS, 8 * m_tiles, columns), jnp.float32)]
-    operands = list(incoming) + ([done] if last else [])
+    rest = add_slots(refs[:count], firsts, len(REST_TILES) * VARS * 8, columns)
+    for var in range(VARS):
+        for m, tile in enumerate(X_TILES):
+            q = 8 * (m * VARS + var)
+            out_ref[var, 8 * tile : 8 * tile + 8, :] = x_ref[q : q + 8, :]
+        for m, tile in enumerate(REST_TILES):
+            q = 8 * (m * VARS + var)
+            out_ref[var, 8 * tile : 8 * tile + 8, :] = rest[q : q + 8]
+    pack_y(
+        lambda var, a: tile_of(out_ref, var, 2 * a, 0),
+        lambda var, a: tile_of(out_ref, var, 2 * a + 1, halves - 1),
+        ya_ref,
+        yb_ref,
+    )
+
+
+def receive(kernel, operands, shapes, *settings):
     return pl.pallas_call(
-        functools.partial(
-            receive_kernel, len(incoming), node, m_tiles, last, columns // LANES
-        ),
+        functools.partial(kernel, *settings),
         out_shape=shapes,
         in_specs=[vmem_spec()] * len(operands),
         out_specs=[vmem_spec()] * len(shapes),
@@ -520,29 +670,31 @@
     )(*operands)
 
 
-def send_direct(values):
+def send_chips(values):
     ring = ("gy", "gz")
     count = len(values)
-    received = [values[0]] * count
-    for k in (6, 7, 2, 4, 3, 5, 1):
-        if k < count:
-            received[k] = lax.ppermute(values[k], ring, [(s, s ^ k) for s in range(count)])
-    return received
+    mine = [values[0]] * count
+    for d in range(count - 1, 0, -1):
+        pairs = [(s, s ^ (2 * d)) for s in range(2 * count)]
+        mine[d] = lax.ppermute(values[d], ring, pairs)
+    return mine
+
+
+def send_cores(mine):
+    others = jnp.concatenate([part[1:2] for part in mine], axis=0)
+    pairs = [(s, s ^ 1) for s in range(2 * len(mine))]
+    return mine + [lax.ppermute(others, ("gy", "gz"), pairs)]
 
 
 def send_all(values, group, capacity):
-    values = jnp.stack(values)
+    (values,) = values
     blocks, rows, lanes = values.shape
     per = lanes // capacity
     values = values.reshape(blocks, rows, per, capacity).transpose(0, 2, 1, 3)
     values = values.reshape(group, rows, capacity)
     values = lax.all_to_all(values, ("gy", "gz"), split_axis=0, concat_axis=0, tiled=True)
     values = values.reshape(blocks, per, rows, capacity).transpose(0, 2, 1, 3)
-    values = values.reshape(blocks, rows, lanes)
-    return [values[g] for g in range(blocks)]
-
-
-CHUNKS = 2
+    return [values.reshape(blocks, rows, lanes)]
 
 
 def per_device(
@@ -552,35 +704,59 @@
     slots = proj_blocks.shape[3]
     group = lax.axis_size("gy") * lax.axis_size("gz")
     capacity = max(2, (2 * slots + group - 1) // group)
-    target = owner_device_index[0, :, 0]
-    order = jnp.arange(slots)
-    earlier_same = (target[:, None] == target[None, :]) & (order[None, :] < order[:, None])
-    rank_in = jnp.sum(earlier_same.astype(jnp.int32), axis=1)
+    begin, states, faces = get_faces(adj_final, new_states)
+    received = exchange(faces)
+    second, received = section(states, 2, begin, received, 2.0 / 3.0, [], True)
+
     direct = group in (2, 4, 8) and capacity == LANES
-    if direct:
-        here = lax.axis_index("gy") * lax.axis_size("gz") + lax.axis_index("gz")
-        target = jnp.bitwise_xor(target, here)
-    place = target * capacity + rank_in
-    placing = (place[:, None] == jnp.arange(group * capacity)[None, :]).astype(jnp.bfloat16)
-    extra = jnp.broadcast_to(owner_element_index.astype(jnp.float32), (8, slots))
-
-    begin = adj_final[0]
-    result = reverse_step(new_states[0], begin, get_faces(begin))
-
-    m_tiles = 8 // CHUNKS
-    incoming = []
-    for chunk in range(CHUNKS):
-        last = chunk == CHUNKS - 1
-        outgoing = project(result, proj_blocks, placing, extra, chunk, m_tiles, last)
-        if last:
-            adj_new = outgoing[-1]
-            outgoing = outgoing[:-1]
-        incoming.append(
-            send_direct(outgoing) if direct else send_all(outgoing, group, capacity)
-        )
-    (half,) = receive(incoming[0], columns, 0, m_tiles, None)
-    adj_proj, *faces = receive(incoming[1], columns, 8 * m_tiles, m_tiles, half)
-    adj_old = reverse_step(old_states[0], adj_proj, faces)
+    outputs = group // 2 if direct else 1
+    outer, placing, extra = prepare(
+        owner_device_index.reshape(1, slots),
+        owner_element_index,
+        proj_blocks,
+        second,
+        group,
+        capacity,
+        direct,
+    )
+    first, received = section(states, 1, second, received, 0.25, [], True)
+    (result,) = section(
+        states, 0, first, received, 1.0, [(begin, 1.0 / 3.0), (second, 0.75)], False
+    )
+
+    tiles = tuple((0, m) for m in range(4))
+    x_out, (inner,) = project(
+        result, [outer], placing, extra, tiles, outputs, load=(proj_blocks, (16, 32))
+    )
+    rest_out, (adj_new,) = project(
+        result, [inner], placing, extra, tiles, outputs, with_copy=True
+    )
+    send = send_chips if direct else lambda out: send_all(out, group, capacity)
+    x_in = send(x_out)
+    rest_in = send(rest_out)
+    firsts = group // 2 if direct else 0
+    cross = send_cores if direct else lambda blocks: blocks
+
+    def rows_of(tiles):
+        return jax.ShapeDtypeStruct((len(tiles) * VARS * 8, columns), jnp.float32)
+
+    faces = face_shapes(columns)
+    x_in = cross(x_in)
+    x_part, *x_faces = receive(
+        receive_x_kernel, x_in, [rows_of(X_TILES)] + faces[:2], len(x_in), firsts
+    )
+    xb, xa = exchange_x(x_faces)
+    rest_in = cross(rest_in)
+    adj_proj, *y_faces = receive(
+        receive_rest_kernel,
+        rest_in + [x_part],
+        [jax.ShapeDtypeStruct((VARS, 64, columns), jnp.float32)] + faces[2:],
+        len(rest_in),
+        firsts,
+        columns // LANES,
+    )
+    yb, ya = exchange_y(y_faces)
+    adj_old = reverse_step(old_states[0], adj_proj, (xa, xb, ya, yb))
     return (adj_new.reshape(adj_final.shape), adj_old.reshape(adj_final.shape))
 
 

time: 80.4 us -> 72.6 us (0.903)
  local copies, waits for them, and re-layouts: 6.54 us -> 0.07 us
  waiting for transfers between devices: 17.5 us -> 13.7 us
  Pallas kernels: 12.6 us -> 16.2 us
  other arithmetic: 1.24 us -> 0.07 us
    unnamed x16 -> x6, local copies, waits for them, and re-layouts: 6.53 us -> 0.01 us
    ppermute x24, starting transfers between devices: 27.8 us -> 34.2 us  [swapped(): return lax.ppermute(value, axis, pairs)]
    ppermute x14 -> x8, starting transfers between devices: 13.4 us -> 7.25 us  [the longest x6 7.11 us: send_chips(): mine[d] = lax.ppermute(values[d], ring, pairs)]
    ppermute x24, waiting for transfers between devices: 10.5 us -> 5.58 us  [swapped(): return lax.ppermute(value, axis, pairs)]
    pallas_call x4 -> x5, Pallas kernels: 6.16 us -> 8.47 us  [the longest x2 4.8 us: project(): pl.pallas_call(functools.partial(project_kernel, tiles, len(sources), out...]
    pallas_call x1, Pallas kernels: 0.08 us -> 1.33 us  [get_faces(): pl.pallas_call(functools.partial(face_kernel, columns // LANES), out_shap...]
    ppermute x14 -> x8, waiting for transfers between devices: 7.04 us -> 8.16 us  [the longest x6 8.15 us: send_chips(): mine[d] = lax.ppermute(values[d], ring, pairs)]
    reduce_sum x1 -> x0, other arithmetic: 1 us -> none  [per_device(): rank_in = jnp.sum(earlier_same.astype(jnp.int32), axis=1)]
  transfers between devices with their start and end apart: 38 -> 32, of which waited for: 15 -> 11; matrix products, arithmetic and copies ran while one was open for 2% -> 0% of each run, Pallas kernels for 9% -> 15%
where the time goes in v2:
time: 72.6 us; the launch traced here: 72.4 us
  starting transfers between devices  41.4 us (57%)
  Pallas kernels  16.2 us (22%)
  waiting for transfers between devices  13.7 us (19%)
  between operations  0.9 us (1%)
    ppermute x24, starting transfers between devices, swapped(): return lax.ppermute(value, axis, pairs)  34.2 us
    ppermute x6, waiting for transfers between devices, send_chips(): mine[d] = lax.ppermute(values[d], ring, pairs)  8.15 us
    ppermute x6, starting transfers between devices, send_chips(): mine[d] = lax.ppermute(values[d], ring, pairs)  7.11 us
    ppermute x24, waiting for transfers between devices, swapped(): return lax.ppermute(value, axis, pairs)  5.58 us
    pallas_call x2, Pallas kernels, project(): pl.pallas_call(functools.partial(project_kernel, tiles, len(sources), out...  4.8 us
    pallas_call x6, Pallas kernels, section(): pl.pallas_call(functools.partial(local_kernel, scale, index, factors, hal...  4.5 us
    pallas_call x1, Pallas kernels, prepare(): pl.pallas_call(functools.partial(prepare_kernel, ((0, 16), (48, 16)), gro...  2.25 us
    pallas_call x6, Pallas kernels, section(): pl.pallas_call(functools.partial(finish_kernel, scale, index, with_faces,...  1.92 us
  transfers between devices with their start and end apart: 32, of which 11 were waited for; matrix products, arithmetic and copies ran while one was open for 0% of the time, Pallas kernels for 15%

profile of v2, /device:TPU:0, one launch (start us, length us, event | category | flops | bytes accessed | tf_op | source)
XLA Modules:
  0.0 72.4 jit_solution(6822316776014110438)
XLA Ops:
  0.7 1.3 %faces.1 = (f32[5,64,256]{2,1,0:T(8,128)S(1)}, f32[3,5,64,256]{3,2,1,0:T(8,128)S(1)}, f32[5,16,256]{2,1,0:T(8,128)S(1)}, f32[5,16,256]{2,1,0:T(8,128)S(1)}, f32[...) custom-call(f32[1,5,64,256]{3,2,1,0:T(8,128)} %w_hbm.1, f32[1,3,5,64,256]{4,3,2,1,0:T(8,128)} %state_hbm.1), custom_call_target="tpu_custom_call" | custom-call | tf_op jit(solution)/shard_map/faces/pallas_call | solution.py:373
  2.0 3.1 %collective-permute-start = (f32[5,16,256]{2,1,0:T(8,128)S(1)}, f32[5,16,256]{2,1,0:T(8,128)S(1)}, u32[]{:S(2)}, u32[]{:S(2)}) collective-permute-start(f32[5,16,256]{2,1,0:T(8,128)S(1)} %get-tuple-element.49), channel_id=1, source_target_pairs={{0,8},{8,0},{16,24},{24,16},{1,9},{9,1},{17,25},{25,17},{2,10},{10... | collective-permute-start | bytes 245768 | tf_op jit(solution)/shard_map/ppermute | solution.py:27
  5.1 2.5 %collective-permute-start.1 = (f32[5,16,256]{2,1,0:T(8,128)S(1)}, f32[5,16,256]{2,1,0:T(8,128)S(1)}, u32[]{:S(2)}, u32[]{:S(2)}) collective-permute-start(f32[5,16,256]{2,1,0:T(8,128)S(1)} %get-tuple-element.50), channel_id=1, source_target_pairs={{0,24},{8,16},{16,8},{24,0},{1,25},{9,17},{17,9},{25,1},{2,26},{10... | collective-permute-start | bytes 245768 | tf_op jit(solution)/shard_map/ppermute | solution.py:27
  7.6 2.6 %collective-permute-start.3 = (f32[5,8,128]{2,1,0:T(8,128)S(1)}, f32[5,8,128]{2,1,0:T(8,128)S(1)}, u32[]{:S(2)}, u32[]{:S(2)}) collective-permute-start(f32[5,8,128]{2,1,0:T(8,128)S(1)} %get-tuple-element.52), channel_id=1, source_target_pairs={{0,7},{1,2},{2,1},{3,4},{4,3},{5,6},{6,5},{7,0},{8,15},{9,10},{10,... | collective-permute-start | bytes 61448 | tf_op jit(solution)/shard_map/ppermute | solution.py:27
  10.1 0.8 %local_part.6.base_ref = f32[5,64,256]{2,1,0:T(8,128)S(1)} custom-call(f32[3,5,64,256]{3,2,1,0:T(8,128)S(1)} %get-tuple-element.47.refs_0_.state_ref, f32[5,64,256]{2,1,0:T(8,128)S(1)} %get-tuple-element.48.refs_1_.refs_2_), custom_call_target="tpu_custom_call" | custom-call | flops 6553600 | bytes 983040 | tf_op jit(solution)/shard_map/local_part/pallas_call | solution.py:467
  10.9 0.8 %collective-permute-done.3.yb_ref = f32[5,8,128]{2,1,0:T(8,128)S(1)} collective-permute-done((f32[5,8,128]{2,1,0:T(8,128)S(1)}, f32[5,8,128]{2,1,0:T(8,128)S(1)}, u32[]{:S(2)}, u32[]{:S(2)}) %collective-permute-start.3) | collective-permute-done | bytes 20512 | tf_op jit(solution)/shard_map/ppermute | solution.py:27
  11.7 0.2 finish.6
  11.9 0.7 collective-permute-start.4
  12.6 2.4 %collective-permute-start.5 = (f32[5,16,256]{2,1,0:T(8,128)S(1)}, f32[5,16,256]{2,1,0:T(8,128)S(1)}, u32[]{:S(2)}, u32[]{:S(2)}) collective-permute-start(f32[5,16,256]{2,1,0:T(8,128)S(1)} %get-tuple-element.55), channel_id=1, source_target_pairs={{0,24},{8,16},{16,8},{24,0},{1,25},{9,17},{17,9},{25,1},{2,26},{10... | collective-permute-start | bytes 245768 | tf_op jit(solution)/shard_map/ppermute | solution.py:27
  15.1 2.6 %collective-permute-start.7 = (f32[5,8,128]{2,1,0:T(8,128)S(1)}, f32[5,8,128]{2,1,0:T(8,128)S(1)}, u32[]{:S(2)}, u32[]{:S(2)}) collective-permute-start(f32[5,8,128]{2,1,0:T(8,128)S(1)} %get-tuple-element.57), channel_id=1, source_target_pairs={{0,7},{1,2},{2,1},{3,4},{4,3},{5,6},{6,5},{7,0},{8,15},{9,10},{10,... | collective-permute-start | bytes 61448 | tf_op jit(solution)/shard_map/ppermute | solution.py:27
  17.6 0.8 %local_part.7.base_ref = f32[5,64,256]{2,1,0:T(8,128)S(1)} custom-call(f32[3,5,64,256]{3,2,1,0:T(8,128)S(1)} %get-tuple-element.47.refs_0_.state_ref, f32[5,64,256]{2,1,0:T(8,128)S(1)} %get-tuple-element.53.refs_1_.refs_3_.after_ref), custom_call_target="tpu_custom_call" | custom-call | flops 6553600 | bytes 983040 | tf_op jit(solution)/shard_map/local_part/pallas_call | solution.py:467
  18.4 0.8 %collective-permute-done.7.yb_ref = f32[5,8,128]{2,1,0:T(8,128)S(1)} collective-permute-done((f32[5,8,128]{2,1,0:T(8,128)S(1)}, f32[5,8,128]{2,1,0:T(8,128)S(1)}, u32[]{:S(2)}, u32[]{:S(2)}) %collective-permute-start.7) | collective-permute-done | bytes 20512 | tf_op jit(solution)/shard_map/ppermute | solution.py:27
  19.3 0.2 finish.7
  19.6 0.8 %collective-permute-start.8 = (f32[5,16,256]{2,1,0:T(8,128)S(1)}, f32[5,16,256]{2,1,0:T(8,128)S(1)}, u32[]{:S(2)}, u32[]{:S(2)}) collective-permute-start(f32[5,16,256]{2,1,0:T(8,128)S(1)} %get-tuple-element.59), channel_id=1, source_target_pairs={{0,8},{8,0},{16,24},{24,16},{1,9},{9,1},{17,25},{25,17},{2,10},{10... | collective-permute-start | bytes 245768 | tf_op jit(solution)/shard_map/ppermute | solution.py:27
  20.3 1.3 %collective-permute-start.9 = (f32[5,16,256]{2,1,0:T(8,128)S(1)}, f32[5,16,256]{2,1,0:T(8,128)S(1)}, u32[]{:S(2)}, u32[]{:S(2)}) collective-permute-start(f32[5,16,256]{2,1,0:T(8,128)S(1)} %get-tuple-element.60), channel_id=1, source_target_pairs={{0,24},{8,16},{16,8},{24,0},{1,25},{9,17},{17,9},{25,1},{2,26},{10... | collective-permute-start | bytes 245768 | tf_op jit(solution)/shard_map/ppermute | solution.py:27
  21.7 3.5 %collective-permute-start.11 = (f32[5,8,128]{2,1,0:T(8,128)S(1)}, f32[5,8,128]{2,1,0:T(8,128)S(1)}, u32[]{:S(2)}, u32[]{:S(2)}) collective-permute-start(f32[5,8,128]{2,1,0:T(8,128)S(1)} %get-tuple-element.62), channel_id=1, source_target_pairs={{0,7},{1,2},{2,1},{3,4},{4,3},{5,6},{6,5},{7,0},{8,15},{9,10},{10,... | collective-permute-start | bytes 61448 | tf_op jit(solution)/shard_map/ppermute | solution.py:27
  25.2 2.3 %prepare.1 = (f32[64,32,512]{2,1,0:T(8,128)S(1)}, bf16[1024,512]{1,0:T(8,128)(2,1)S(1)}, f32[8,512]{1,0:T(8,128)S(1)}) custom-call(s32[1,512]{1,0:T(1,128)S(1)} %bitcast.10, s32[1,512]{1,0:T(1,128)S(1)} %copy-done.2, f32[1,64,64,512]{3,2,1,0:T(8,128)} %refs_4_.1, f32[5,64,256]{2,1,0:T(8,128)S(1)} %get-tuple-element.53.refs_1_.refs_3_.after_ref), custom_call_target="tpu_custom_call" | custom-call | tf_op jit(solution)/shard_map/prepare/pallas_call | solution.py:432
  27.4 0.8 %local_part.8.base_ref = f32[5,64,256]{2,1,0:T(8,128)S(1)} custom-call(f32[3,5,64,256]{3,2,1,0:T(8,128)S(1)} %get-tuple-element.47.refs_0_.state_ref, f32[5,64,256]{2,1,0:T(8,128)S(1)} %get-tuple-element.58.refs_1_, f32[5,64,256]{2,1,0:T(8,128)S(1)} %get-tuple-element.48.refs_1_.refs_2_, f32[5,64,256]{2,1,0:T(8,128)S(1)} %get-tuple-element.53.refs_1_.refs_3_.after_ref), custom_call_target="tpu_custom_call" | custom-call | flops 6553600 | bytes 983040 | tf_op jit(solution)/shard_map/local_part/pallas_call | solution.py:467
  28.5 2.4 %project.2 = (f32[2,168,128]{2,1,0:T(8,128)S(1)}, f32[2,168,128]{2,1,0:T(8,128)S(1)}, f32[2,168,128]{2,1,0:T(8,128)S(1)}, f32[2,168,128]{2,1,0:T(8,128)S(1)}, f32[64,32,512]{2,1,0:T(8,128)S(1)}) custom-call(f32[5,64,256]{2,1,0:T(8,128)S(1)} %finish.8.refs_0_, f32[64,32,512]{2,1,0:T(8,128)S(1)} %get-tuple-element.63.refs_1_, ...), custom_call_target="tpu_custom_call" | custom-call | flops 4000000000 | bytes 20971520 | tf_op jit(solution)/shard_map/project/pallas_call | solution.py:591
  31.1 1.5 %collective-permute-start.17 = (f32[2,168,128]{2,1,0:T(8,128)S(1)}, f32[2,168,128]{2,1,0:T(8,128)S(1)}, u32[]{:S(2)}, u32[]{:S(2)}) collective-permute-start(f32[2,168,128]{2,1,0:T(8,128)S(1)} %get-tuple-element.74), channel_id=1, source_target_pairs={{0,4},{1,5},{2,6},{3,7},{4,0},{5,1},{6,2},{7,3},{8,12},{9,13},{10,... | collective-permute-start | bytes 516104 | tf_op jit(solution)/shard_map/ppermute | solution.py:679
  32.6 1.9 %collective-permute-start.18 = (f32[2,168,128]{2,1,0:T(8,128)S(1)}, f32[2,168,128]{2,1,0:T(8,128)S(1)}, u32[]{:S(2)}, u32[]{:S(2)}) collective-permute-start(f32[2,168,128]{2,1,0:T(8,128)S(1)} %get-tuple-element.75), channel_id=1, source_target_pairs={{0,6},{1,7},{2,4},{3,5},{4,2},{5,3},{6,0},{7,1},{8,14},{9,15},{10,... | collective-permute-start | bytes 516104 | tf_op jit(solution)/shard_map/ppermute | solution.py:679
  34.4 2.4 %project.3 = (f32[2,168,128]{2,1,0:T(8,128)S(1)}, f32[2,168,128]{2,1,0:T(8,128)S(1)}, f32[2,168,128]{2,1,0:T(8,128)S(1)}, f32[2,168,128]{2,1,0:T(8,128)S(1)}, f32[5,64,256]{2,1,0:T(8,128)}) custom-call(f32[5,64,256]{2,1,0:T(8,128)S(1)} %finish.8.refs_0_, f32[64,32,512]{2,1,0:T(8,128)S(1)} %get-tuple-element.66.refs_1_, ...), custom_call_target="tpu_custom_call" | custom-call | flops 4000000000 | bytes 20971520 | tf_op jit(solution)/shard_map/project/pallas_call | solution.py:591
  37.0 1.5 %collective-permute-start.13 = (f32[2,168,128]{2,1,0:T(8,128)S(1)}, f32[2,168,128]{2,1,0:T(8,128)S(1)}, u32[]{:S(2)}, u32[]{:S(2)}) collective-permute-start(f32[2,168,128]{2,1,0:T(8,128)S(1)} %get-tuple-element.70), channel_id=1, source_target_pairs={{0,4},{1,5},{2,6},{3,7},{4,0},{5,1},{6,2},{7,3},{8,12},{9,13},{10,... | collective-permute-start | bytes 516104 | tf_op jit(solution)/shard_map/ppermute | solution.py:679
  38.5 1.9 %collective-permute-start.14 = (f32[2,168,128]{2,1,0:T(8,128)S(1)}, f32[2,168,128]{2,1,0:T(8,128)S(1)}, u32[]{:S(2)}, u32[]{:S(2)}) collective-permute-start(f32[2,168,128]{2,1,0:T(8,128)S(1)} %get-tuple-element.71), channel_id=1, source_target_pairs={{0,6},{1,7},{2,4},{3,5},{4,2},{5,3},{6,0},{7,1},{8,14},{9,15},{10,... | collective-permute-start | bytes 516104 | tf_op jit(solution)/shard_map/ppermute | solution.py:679
  40.4 2.9 %collective-permute-done.18.refs_3_ = f32[2,168,128]{2,1,0:T(8,128)S(1)} collective-permute-done((f32[2,168,128]{2,1,0:T(8,128)S(1)}, f32[2,168,128]{2,1,0:T(8,128)S(1)}, u32[]{:S(2)}, u32[]{:S(2)}) %collective-permute-start.18) | collective-permute-done | bytes 172064 | tf_op jit(solution)/shard_map/ppermute | solution.py:679
  43.5 1.6 %collective-permute-done.12.refs_1_ = f32[2,168,128]{2,1,0:T(8,128)S(1)} collective-permute-done((f32[2,168,128]{2,1,0:T(8,128)S(1)}, f32[2,168,128]{2,1,0:T(8,128)S(1)}, u32[]{:S(2)}, u32[]{:S(2)}) %collective-permute-start.12) | collective-permute-done | bytes 172064 | tf_op jit(solution)/shard_map/ppermute | solution.py:679
  45.1 0.6 collective-permute-done.13.refs_2_
  45.7 3.0 %collective-permute-done.14.refs_3_ = f32[2,168,128]{2,1,0:T(8,128)S(1)} collective-permute-done((f32[2,168,128]{2,1,0:T(8,128)S(1)}, f32[2,168,128]{2,1,0:T(8,128)S(1)}, u32[]{:S(2)}, u32[]{:S(2)}) %collective-permute-start.14) | collective-permute-done | bytes 172064 | tf_op jit(solution)/shard_map/ppermute | solution.py:679
  48.9 0.7 receive.2
  49.5 0.2 collective-permute-start.20
  49.8 1.8 %collective-permute-start.21 = (f32[5,16,256]{2,1,0:T(8,128)S(1)}, f32[5,16,256]{2,1,0:T(8,128)S(1)}, u32[]{:S(2)}, u32[]{:S(2)}) collective-permute-start(f32[5,16,256]{2,1,0:T(8,128)S(1)} %get-tuple-element.79), channel_id=1, source_target_pairs={{0,24},{8,16},{16,8},{24,0},{1,25},{9,17},{17,9},{25,1},{2,26},{10... | collective-permute-start | bytes 245768 | tf_op jit(solution)/shard_map/ppermute | solution.py:27
  51.6 0.7 %receive.3 = (f32[5,64,256]{2,1,0:T(8,128)S(1)}, f32[5,8,128]{2,1,0:T(8,128)S(1)}, f32[5,8,128]{2,1,0:T(8,128)S(1)}) custom-call(f32[2,168,128]{2,1,0:T(8,128)S(1)} %get-tuple-element.68.refs_0_, f32[2,168,128]{2,1,0:T(8,128)S(1)} %collective-permute-done.12.refs_1_, f32[2,168,128]{2,1,0:T(8,128)S(1)} %collective-permute-done.13.refs_2_, ...), custom_call_target="tpu_custom_call" | custom-call | flops 1000000000 | bytes 1000000 | tf_op jit(solution)/shard_map/receive/pallas_call | solution.py:660
  52.3 0.2 collective-permute-start.22
  52.5 2.1 %collective-permute-start.23 = (f32[5,8,128]{2,1,0:T(8,128)S(1)}, f32[5,8,128]{2,1,0:T(8,128)S(1)}, u32[]{:S(2)}, u32[]{:S(2)}) collective-permute-start(f32[5,8,128]{2,1,0:T(8,128)S(1)} %get-tuple-element.81), channel_id=1, source_target_pairs={{0,7},{1,2},{2,1},{3,4},{4,3},{5,6},{6,5},{7,0},{8,15},{9,10},{10,... | collective-permute-start | bytes 61448 | tf_op jit(solution)/shard_map/ppermute | solution.py:27
  54.6 0.7 local_part.9.base_ref
  55.3 1.3 %collective-permute-done.23.yb_ref = f32[5,8,128]{2,1,0:T(8,128)S(1)} collective-permute-done((f32[5,8,128]{2,1,0:T(8,128)S(1)}, f32[5,8,128]{2,1,0:T(8,128)S(1)}, u32[]{:S(2)}, u32[]{:S(2)}) %collective-permute-start.23) | collective-permute-done | bytes 20512 | tf_op jit(solution)/shard_map/ppermute | solution.py:27
  56.7 0.2 finish.9
  56.9 1.4 %collective-permute-start.24 = (f32[5,16,256]{2,1,0:T(8,128)S(1)}, f32[5,16,256]{2,1,0:T(8,128)S(1)}, u32[]{:S(2)}, u32[]{:S(2)}) collective-permute-start(f32[5,16,256]{2,1,0:T(8,128)S(1)} %get-tuple-element.83), channel_id=1, source_target_pairs={{0,8},{8,0},{16,24},{24,16},{1,9},{9,1},{17,25},{25,17},{2,10},{10... | collective-permute-start | bytes 245768 | tf_op jit(solution)/shard_map/ppermute | solution.py:27
  58.2 1.8 %collective-permute-start.25 = (f32[5,16,256]{2,1,0:T(8,128)S(1)}, f32[5,16,256]{2,1,0:T(8,128)S(1)}, u32[]{:S(2)}, u32[]{:S(2)}) collective-permute-start(f32[5,16,256]{2,1,0:T(8,128)S(1)} %get-tuple-element.84), channel_id=1, source_target_pairs={{0,24},{8,16},{16,8},{24,0},{1,25},{9,17},{17,9},{25,1},{2,26},{10... | collective-permute-start | bytes 245768 | tf_op jit(solution)/shard_map/ppermute | solution.py:27
  60.1 2.3 %collective-permute-start.27 = (f32[5,8,128]{2,1,0:T(8,128)S(1)}, f32[5,8,128]{2,1,0:T(8,128)S(1)}, u32[]{:S(2)}, u32[]{:S(2)}) collective-permute-start(f32[5,8,128]{2,1,0:T(8,128)S(1)} %get-tuple-element.86), channel_id=1, source_target_pairs={{0,7},{1,2},{2,1},{3,4},{4,3},{5,6},{6,5},{7,0},{8,15},{9,10},{10,... | collective-permute-start | bytes 61448 | tf_op jit(solution)/shard_map/ppermute | solution.py:27
  62.3 0.7 local_part.10.base_ref
  63.1 1.1 %collective-permute-done.27.yb_ref = f32[5,8,128]{2,1,0:T(8,128)S(1)} collective-permute-done((f32[5,8,128]{2,1,0:T(8,128)S(1)}, f32[5,8,128]{2,1,0:T(8,128)S(1)}, u32[]{:S(2)}, u32[]{:S(2)}) %collective-permute-start.27) | collective-permute-done | bytes 20512 | tf_op jit(solution)/shard_map/ppermute | solution.py:27
  64.2 0.3 collective-permute-done.25.xb_ref
  64.8 2.6 %collective-permute-start.29 = (f32[5,16,256]{2,1,0:T(8,128)S(1)}, f32[5,16,256]{2,1,0:T(8,128)S(1)}, u32[]{:S(2)}, u32[]{:S(2)}) collective-permute-start(f32[5,16,256]{2,1,0:T(8,128)S(1)} %get-tuple-element.89), channel_id=1, source_target_pairs={{0,24},{8,16},{16,8},{24,0},{1,25},{9,17},{17,9},{25,1},{2,26},{10... | collective-permute-start | bytes 245768 | tf_op jit(solution)/shard_map/ppermute | solution.py:27
  67.4 2.3 %collective-permute-start.31 = (f32[5,8,128]{2,1,0:T(8,128)S(1)}, f32[5,8,128]{2,1,0:T(8,128)S(1)}, u32[]{:S(2)}, u32[]{:S(2)}) collective-permute-start(f32[5,8,128]{2,1,0:T(8,128)S(1)} %get-tuple-element.91), channel_id=1, source_target_pairs={{0,7},{1,2},{2,1},{3,4},{4,3},{5,6},{6,5},{7,0},{8,15},{9,10},{10,... | collective-permute-start | bytes 61448 | tf_op jit(solution)/shard_map/ppermute | solution.py:27
  69.7 0.8 %local_part.11.base_ref = f32[5,64,256]{2,1,0:T(8,128)S(1)} custom-call(f32[3,5,64,256]{3,2,1,0:T(8,128)S(1)} %bitcast.8, f32[5,64,256]{2,1,0:T(8,128)S(1)} %get-tuple-element.87.refs_1_, f32[5,64,256]{2,1,0:T(8,128)S(1)} %get-tuple-element.77.refs_1_.refs_2_, f32[5,64,256]{2,1,0:T(8,128)S(1)} %get-tuple-element.82.refs_1_.refs_3_), custom_call_target="tpu_custom_call" | custom-call | flops 6553600 | bytes 983040 | tf_op jit(solution)/shard_map/local_part/pallas_call | solution.py:467
  70.5 1.0 %collective-permute-done.31.yb_ref = f32[5,8,128]{2,1,0:T(8,128)S(1)} collective-permute-done((f32[5,8,128]{2,1,0:T(8,128)S(1)}, f32[5,8,128]{2,1,0:T(8,128)S(1)}, u32[]{:S(2)}, u32[]{:S(2)}) %collective-permute-start.31) | collective-permute-done | bytes 20512 | tf_op jit(solution)/shard_map/ppermute | solution.py:27
  71.5 0.9 %finish.11 = f32[5,64,256]{2,1,0:T(8,128)} custom-call(f32[3,5,64,256]{3,2,1,0:T(8,128)S(1)} %bitcast.9, f32[5,64,256]{2,1,0:T(8,128)S(1)} %local_part.11.base_ref, f32[5,16,256]{2,1,0:T(8,128)S(1)} %collective-permute-done.28.xa_ref, f32[5,16,256]{2,1,0:T(8,128)S(1)} %collective-permute-done.29.xb_ref, f32[5,8,128]{2,1,0:T(8,128)S(1)} %collective-permute-done.30.ya_ref, ...), custom_call_target="tpu_custom_call" | custom-call | tf_op jit(solution)/shard_map/finish/pallas_call | solution.py:479
  (50 shorter events, 1.4 us)
Async XLA Ops:
  0.6 24.5 %copy-start.2 = (s32[1,512]{1,0:T(1,128)S(1)}, s32[1,512]{1,0:T(1,128)}, u32[]{:S(2)}) copy-start(s32[1,512]{1,0:T(1,128)} %local_ref.1) | copy-start | bytes 6148
  0.6 24.5 %copy-start.1 = (s32[1,512,1]{1,2,0:T(1,128)S(1)}, s32[1,512,1]{1,2,0:T(1,128)}, u32[]{:S(2)}) copy-start(s32[1,512,1]{1,2,0:T(1,128)} %param.9) | copy-start | bytes 6148
  2.0 9.7 %collective-permute-start = (f32[5,16,256]{2,1,0:T(8,128)S(1)}, f32[5,16,256]{2,1,0:T(8,128)S(1)}, u32[]{:S(2)}, u32[]{:S(2)}) collective-permute-start(f32[5,16,256]{2,1,0:T(8,128)S(1)} %get-tuple-element.49), channel_id=1, source_target_pairs={{0,8},{8,0},{16,24},{24,16},{1,9},{9,1},{17,25},{25,17},{2,10},{10... | collective-permute-start | bytes 245768 | tf_op jit(solution)/shard_map/ppermute | solution.py:27
  5.1 6.6 %collective-permute-start.1 = (f32[5,16,256]{2,1,0:T(8,128)S(1)}, f32[5,16,256]{2,1,0:T(8,128)S(1)}, u32[]{:S(2)}, u32[]{:S(2)}) collective-permute-start(f32[5,16,256]{2,1,0:T(8,128)S(1)} %get-tuple-element.50), channel_id=1, source_target_pairs={{0,24},{8,16},{16,8},{24,0},{1,25},{9,17},{17,9},{25,1},{2,26},{10... | collective-permute-start | bytes 245768 | tf_op jit(solution)/shard_map/ppermute | solution.py:27
  7.6 3.3 %collective-permute-start.2 = (f32[5,8,128]{2,1,0:T(8,128)S(1)}, f32[5,8,128]{2,1,0:T(8,128)S(1)}, u32[]{:S(2)}, u32[]{:S(2)}) collective-permute-start(f32[5,8,128]{2,1,0:T(8,128)S(1)} %get-tuple-element.51), channel_id=1, source_target_pairs={{0,1},{1,0},{2,3},{3,2},{4,5},{5,4},{6,7},{7,6},{8,9},{9,8},{10,11... | collective-permute-start | bytes 61448 | tf_op jit(solution)/shard_map/ppermute | solution.py:27
  7.6 4.1 %collective-permute-start.3 = (f32[5,8,128]{2,1,0:T(8,128)S(1)}, f32[5,8,128]{2,1,0:T(8,128)S(1)}, u32[]{:S(2)}, u32[]{:S(2)}) collective-permute-start(f32[5,8,128]{2,1,0:T(8,128)S(1)} %get-tuple-element.52), channel_id=1, source_target_pairs={{0,7},{1,2},{2,1},{3,4},{4,3},{5,6},{6,5},{7,0},{8,15},{9,10},{10,... | collective-permute-start | bytes 61448 | tf_op jit(solution)/shard_map/ppermute | solution.py:27
  11.9 7.3 %collective-permute-start.4 = (f32[5,16,256]{2,1,0:T(8,128)S(1)}, f32[5,16,256]{2,1,0:T(8,128)S(1)}, u32[]{:S(2)}, u32[]{:S(2)}) collective-permute-start(f32[5,16,256]{2,1,0:T(8,128)S(1)} %get-tuple-element.54), channel_id=1, source_target_pairs={{0,8},{8,0},{16,24},{24,16},{1,9},{9,1},{17,25},{25,17},{2,10},{10... | collective-permute-start | bytes 245768 | tf_op jit(solution)/shard_map/ppermute | solution.py:27
  12.6 6.7 %collective-permute-start.5 = (f32[5,16,256]{2,1,0:T(8,128)S(1)}, f32[5,16,256]{2,1,0:T(8,128)S(1)}, u32[]{:S(2)}, u32[]{:S(2)}) collective-permute-start(f32[5,16,256]{2,1,0:T(8,128)S(1)} %get-tuple-element.55), channel_id=1, source_target_pairs={{0,24},{8,16},{16,8},{24,0},{1,25},{9,17},{17,9},{25,1},{2,26},{10... | collective-permute-start | bytes 245768 | tf_op jit(solution)/shard_map/ppermute | solution.py:27
  15.1 3.3 %collective-permute-start.6 = (f32[5,8,128]{2,1,0:T(8,128)S(1)}, f32[5,8,128]{2,1,0:T(8,128)S(1)}, u32[]{:S(2)}, u32[]{:S(2)}) collective-permute-start(f32[5,8,128]{2,1,0:T(8,128)S(1)} %get-tuple-element.56), channel_id=1, source_target_pairs={{0,1},{1,0},{2,3},{3,2},{4,5},{5,4},{6,7},{7,6},{8,9},{9,8},{10,11... | collective-permute-start | bytes 61448 | tf_op jit(solution)/shard_map/ppermute | solution.py:27
  15.1 4.1 %collective-permute-start.7 = (f32[5,8,128]{2,1,0:T(8,128)S(1)}, f32[5,8,128]{2,1,0:T(8,128)S(1)}, u32[]{:S(2)}, u32[]{:S(2)}) collective-permute-start(f32[5,8,128]{2,1,0:T(8,128)S(1)} %get-tuple-element.57), channel_id=1, source_target_pairs={{0,7},{1,2},{2,1},{3,4},{4,3},{5,6},{6,5},{7,0},{8,15},{9,10},{10,... | collective-permute-start | bytes 61448 | tf_op jit(solution)/shard_map/ppermute | solution.py:27
  19.6 8.7 %collective-permute-start.8 = (f32[5,16,256]{2,1,0:T(8,128)S(1)}, f32[5,16,256]{2,1,0:T(8,128)S(1)}, u32[]{:S(2)}, u32[]{:S(2)}) collective-permute-start(f32[5,16,256]{2,1,0:T(8,128)S(1)} %get-tuple-element.59), channel_id=1, source_target_pairs={{0,8},{8,0},{16,24},{24,16},{1,9},{9,1},{17,25},{25,17},{2,10},{10... | collective-permute-start | bytes 245768 | tf_op jit(solution)/shard_map/ppermute | solution.py:27
  20.3 7.9 %collective-permute-start.9 = (f32[5,16,256]{2,1,0:T(8,128)S(1)}, f32[5,16,256]{2,1,0:T(8,128)S(1)}, u32[]{:S(2)}, u32[]{:S(2)}) collective-permute-start(f32[5,16,256]{2,1,0:T(8,128)S(1)} %get-tuple-element.60), channel_id=1, source_target_pairs={{0,24},{8,16},{16,8},{24,0},{1,25},{9,17},{17,9},{25,1},{2,26},{10... | collective-permute-start | bytes 245768 | tf_op jit(solution)/shard_map/ppermute | solution.py:27
  21.7 6.6 %collective-permute-start.10 = (f32[5,8,128]{2,1,0:T(8,128)S(1)}, f32[5,8,128]{2,1,0:T(8,128)S(1)}, u32[]{:S(2)}, u32[]{:S(2)}) collective-permute-start(f32[5,8,128]{2,1,0:T(8,128)S(1)} %get-tuple-element.61), channel_id=1, source_target_pairs={{0,1},{1,0},{2,3},{3,2},{4,5},{5,4},{6,7},{7,6},{8,9},{9,8},{10,11... | collective-permute-start | bytes 61448 | tf_op jit(solution)/shard_map/ppermute | solution.py:27
  21.7 6.6 %collective-permute-start.11 = (f32[5,8,128]{2,1,0:T(8,128)S(1)}, f32[5,8,128]{2,1,0:T(8,128)S(1)}, u32[]{:S(2)}, u32[]{:S(2)}) collective-permute-start(f32[5,8,128]{2,1,0:T(8,128)S(1)} %get-tuple-element.62), channel_id=1, source_target_pairs={{0,7},{1,2},{2,1},{3,4},{4,3},{5,6},{6,5},{7,0},{8,15},{9,10},{10,... | collective-permute-start | bytes 61448 | tf_op jit(solution)/shard_map/ppermute | solution.py:27
  30.9 7.6 %collective-permute-start.16 = (f32[2,168,128]{2,1,0:T(8,128)S(1)}, f32[2,168,128]{2,1,0:T(8,128)S(1)}, u32[]{:S(2)}, u32[]{:S(2)}) collective-permute-start(f32[2,168,128]{2,1,0:T(8,128)S(1)} %get-tuple-element.73), channel_id=1, source_target_pairs={{0,2},{1,3},{2,0},{3,1},{4,6},{5,7},{6,4},{7,5},{8,10},{9,11},{10,... | collective-permute-start | bytes 516104 | tf_op jit(solution)/shard_map/ppermute | solution.py:679
  31.1 9.3 %collective-permute-start.17 = (f32[2,168,128]{2,1,0:T(8,128)S(1)}, f32[2,168,128]{2,1,0:T(8,128)S(1)}, u32[]{:S(2)}, u32[]{:S(2)}) collective-permute-start(f32[2,168,128]{2,1,0:T(8,128)S(1)} %get-tuple-element.74), channel_id=1, source_target_pairs={{0,4},{1,5},{2,6},{3,7},{4,0},{5,1},{6,2},{7,3},{8,12},{9,13},{10,... | collective-permute-start | bytes 516104 | tf_op jit(solution)/shard_map/ppermute | solution.py:679
  32.6 10.8 %collective-permute-start.18 = (f32[2,168,128]{2,1,0:T(8,128)S(1)}, f32[2,168,128]{2,1,0:T(8,128)S(1)}, u32[]{:S(2)}, u32[]{:S(2)}) collective-permute-start(f32[2,168,128]{2,1,0:T(8,128)S(1)} %get-tuple-element.75), channel_id=1, source_target_pairs={{0,6},{1,7},{2,4},{3,5},{4,2},{5,3},{6,0},{7,1},{8,14},{9,15},{10,... | collective-permute-start | bytes 516104 | tf_op jit(solution)/shard_map/ppermute | solution.py:679
  36.8 8.3 %collective-permute-start.12 = (f32[2,168,128]{2,1,0:T(8,128)S(1)}, f32[2,168,128]{2,1,0:T(8,128)S(1)}, u32[]{:S(2)}, u32[]{:S(2)}) collective-permute-start(f32[2,168,128]{2,1,0:T(8,128)S(1)} %get-tuple-element.69), channel_id=1, source_target_pairs={{0,2},{1,3},{2,0},{3,1},{4,6},{5,7},{6,4},{7,5},{8,10},{9,11},{10,... | collective-permute-start | bytes 516104 | tf_op jit(solution)/shard_map/ppermute | solution.py:679
  37.0 8.7 %collective-permute-start.13 = (f32[2,168,128]{2,1,0:T(8,128)S(1)}, f32[2,168,128]{2,1,0:T(8,128)S(1)}, u32[]{:S(2)}, u32[]{:S(2)}) collective-permute-start(f32[2,168,128]{2,1,0:T(8,128)S(1)} %get-tuple-element.70), channel_id=1, source_target_pairs={{0,4},{1,5},{2,6},{3,7},{4,0},{5,1},{6,2},{7,3},{8,12},{9,13},{10,... | collective-permute-start | bytes 516104 | tf_op jit(solution)/shard_map/ppermute | solution.py:679
  38.5 10.2 %collective-permute-start.14 = (f32[2,168,128]{2,1,0:T(8,128)S(1)}, f32[2,168,128]{2,1,0:T(8,128)S(1)}, u32[]{:S(2)}, u32[]{:S(2)}) collective-permute-start(f32[2,168,128]{2,1,0:T(8,128)S(1)} %get-tuple-element.71), channel_id=1, source_target_pairs={{0,6},{1,7},{2,4},{3,5},{4,2},{5,3},{6,0},{7,1},{8,14},{9,15},{10,... | collective-permute-start | bytes 516104 | tf_op jit(solution)/shard_map/ppermute | solution.py:679
  43.4 5.5 %collective-permute-start.19 = (f32[4,168,128]{2,1,0:T(8,128)S(1)}, f32[4,168,128]{2,1,0:T(8,128)S(1)}, u32[]{:S(2)}, u32[]{:S(2)}) collective-permute-start(f32[4,168,128]{2,1,0:T(8,128)S(1)} %pad_maximum_fusion.1), channel_id=1, source_target_pairs={{0,1},{1,0},{2,3},{3,2},{4,5},{5,4},{6,7},{7,6},{8,9},{9,8},{10,11... | collective-permute-start | bytes 1032200 | tf_op jit(solution)/shard_map/ppermute | solution.py:686
  45.1 9.5 %copy-start = (f32[1,3,5,64,256]{4,3,2,1,0:T(8,128)S(1)}, f32[1,3,5,64,256]{4,3,2,1,0:T(8,128)}, u32[]{:S(2)}) copy-start(f32[1,3,5,64,256]{4,3,2,1,0:T(8,128)} %param.8) | copy-start | bytes 2949124
  48.8 2.8 %collective-permute-start.15 = (f32[4,168,128]{2,1,0:T(8,128)S(1)}, f32[4,168,128]{2,1,0:T(8,128)S(1)}, u32[]{:S(2)}, u32[]{:S(2)}) collective-permute-start(f32[4,168,128]{2,1,0:T(8,128)S(1)} %pad_maximum_fusion), channel_id=1, source_target_pairs={{0,1},{1,0},{2,3},{3,2},{4,5},{5,4},{6,7},{7,6},{8,9},{9,8},{10,11... | collective-permute-start | bytes 1032200 | tf_op jit(solution)/shard_map/ppermute | solution.py:686
  49.5 7.1 %collective-permute-start.20 = (f32[5,16,256]{2,1,0:T(8,128)S(1)}, f32[5,16,256]{2,1,0:T(8,128)S(1)}, u32[]{:S(2)}, u32[]{:S(2)}) collective-permute-start(f32[5,16,256]{2,1,0:T(8,128)S(1)} %get-tuple-element.78), channel_id=1, source_target_pairs={{0,8},{8,0},{16,24},{24,16},{1,9},{9,1},{17,25},{25,17},{2,10},{10... | collective-permute-start | bytes 245768 | tf_op jit(solution)/shard_map/ppermute | solution.py:27
  49.8 6.9 %collective-permute-start.21 = (f32[5,16,256]{2,1,0:T(8,128)S(1)}, f32[5,16,256]{2,1,0:T(8,128)S(1)}, u32[]{:S(2)}, u32[]{:S(2)}) collective-permute-start(f32[5,16,256]{2,1,0:T(8,128)S(1)} %get-tuple-element.79), channel_id=1, source_target_pairs={{0,24},{8,16},{16,8},{24,0},{1,25},{9,17},{17,9},{25,1},{2,26},{10... | collective-permute-start | bytes 245768 | tf_op jit(solution)/shard_map/ppermute | solution.py:27
  52.3 3.0 %collective-permute-start.22 = (f32[5,8,128]{2,1,0:T(8,128)S(1)}, f32[5,8,128]{2,1,0:T(8,128)S(1)}, u32[]{:S(2)}, u32[]{:S(2)}) collective-permute-start(f32[5,8,128]{2,1,0:T(8,128)S(1)} %get-tuple-element.80), channel_id=1, source_target_pairs={{0,1},{1,0},{2,3},{3,2},{4,5},{5,4},{6,7},{7,6},{8,9},{9,8},{10,11... | collective-permute-start | bytes 61448 | tf_op jit(solution)/shard_map/ppermute | solution.py:27
  52.5 4.1 %collective-permute-start.23 = (f32[5,8,128]{2,1,0:T(8,128)S(1)}, f32[5,8,128]{2,1,0:T(8,128)S(1)}, u32[]{:S(2)}, u32[]{:S(2)}) collective-permute-start(f32[5,8,128]{2,1,0:T(8,128)S(1)} %get-tuple-element.81), channel_id=1, source_target_pairs={{0,7},{1,2},{2,1},{3,4},{4,3},{5,6},{6,5},{7,0},{8,15},{9,10},{10,... | collective-permute-start | bytes 61448 | tf_op jit(solution)/shard_map/ppermute | solution.py:27
  56.9 7.3 %collective-permute-start.24 = (f32[5,16,256]{2,1,0:T(8,128)S(1)}, f32[5,16,256]{2,1,0:T(8,128)S(1)}, u32[]{:S(2)}, u32[]{:S(2)}) collective-permute-start(f32[5,16,256]{2,1,0:T(8,128)S(1)} %get-tuple-element.83), channel_id=1, source_target_pairs={{0,8},{8,0},{16,24},{24,16},{1,9},{9,1},{17,25},{25,17},{2,10},{10... | collective-permute-start | bytes 245768 | tf_op jit(solution)/shard_map/ppermute | solution.py:27
  58.2 6.3 %collective-permute-start.25 = (f32[5,16,256]{2,1,0:T(8,128)S(1)}, f32[5,16,256]{2,1,0:T(8,128)S(1)}, u32[]{:S(2)}, u32[]{:S(2)}) collective-permute-start(f32[5,16,256]{2,1,0:T(8,128)S(1)} %get-tuple-element.84), channel_id=1, source_target_pairs={{0,24},{8,16},{16,8},{24,0},{1,25},{9,17},{17,9},{25,1},{2,26},{10... | collective-permute-start | bytes 245768 | tf_op jit(solution)/shard_map/ppermute | solution.py:27
  60.1 3.0 %collective-permute-start.26 = (f32[5,8,128]{2,1,0:T(8,128)S(1)}, f32[5,8,128]{2,1,0:T(8,128)S(1)}, u32[]{:S(2)}, u32[]{:S(2)}) collective-permute-start(f32[5,8,128]{2,1,0:T(8,128)S(1)} %get-tuple-element.85), channel_id=1, source_target_pairs={{0,1},{1,0},{2,3},{3,2},{4,5},{5,4},{6,7},{7,6},{8,9},{9,8},{10,11... | collective-permute-start | bytes 61448 | tf_op jit(solution)/shard_map/ppermute | solution.py:27
  60.1 4.1 %collective-permute-start.27 = (f32[5,8,128]{2,1,0:T(8,128)S(1)}, f32[5,8,128]{2,1,0:T(8,128)S(1)}, u32[]{:S(2)}, u32[]{:S(2)}) collective-permute-start(f32[5,8,128]{2,1,0:T(8,128)S(1)} %get-tuple-element.86), channel_id=1, source_target_pairs={{0,7},{1,2},{2,1},{3,4},{4,3},{5,6},{6,5},{7,0},{8,15},{9,10},{10,... | collective-permute-start | bytes 61448 | tf_op jit(solution)/shard_map/ppermute | solution.py:27
  64.7 6.8 %collective-permute-start.28 = (f32[5,16,256]{2,1,0:T(8,128)S(1)}, f32[5,16,256]{2,1,0:T(8,128)S(1)}, u32[]{:S(2)}, u32[]{:S(2)}) collective-permute-start(f32[5,16,256]{2,1,0:T(8,128)S(1)} %get-tuple-element.88), channel_id=1, source_target_pairs={{0,8},{8,0},{16,24},{24,16},{1,9},{9,1},{17,25},{25,17},{2,10},{10... | collective-permute-start | bytes 245768 | tf_op jit(solution)/shard_map/ppermute | solution.py:27
  64.8 6.7 %collective-permute-start.29 = (f32[5,16,256]{2,1,0:T(8,128)S(1)}, f32[5,16,256]{2,1,0:T(8,128)S(1)}, u32[]{:S(2)}, u32[]{:S(2)}) collective-permute-start(f32[5,16,256]{2,1,0:T(8,128)S(1)} %get-tuple-element.89), channel_id=1, source_target_pairs={{0,24},{8,16},{16,8},{24,0},{1,25},{9,17},{17,9},{25,1},{2,26},{10... | collective-permute-start | bytes 245768 | tf_op jit(solution)/shard_map/ppermute | solution.py:27
  67.4 3.1 %collective-permute-start.30 = (f32[5,8,128]{2,1,0:T(8,128)S(1)}, f32[5,8,128]{2,1,0:T(8,128)S(1)}, u32[]{:S(2)}, u32[]{:S(2)}) collective-permute-start(f32[5,8,128]{2,1,0:T(8,128)S(1)} %get-tuple-element.90), channel_id=1, source_target_pairs={{0,1},{1,0},{2,3},{3,2},{4,5},{5,4},{6,7},{7,6},{8,9},{9,8},{10,11... | collective-permute-start | bytes 61448 | tf_op jit(solution)/shard_map/ppermute | solution.py:27
  67.4 4.1 %collective-permute-start.31 = (f32[5,8,128]{2,1,0:T(8,128)S(1)}, f32[5,8,128]{2,1,0:T(8,128)S(1)}, u32[]{:S(2)}, u32[]{:S(2)}) collective-permute-start(f32[5,8,128]{2,1,0:T(8,128)S(1)} %get-tuple-element.91), channel_id=1, source_target_pairs={{0,7},{1,2},{2,1},{3,4},{4,3},{5,6},{6,5},{7,0},{8,15},{9,10},{10,... | collective-permute-start | bytes 61448 | tf_op jit(solution)/shard_map/ppermute | solution.py:27

commit v3 on v2

--- a/solution.py
+++ b/solution.py
@@ -126,10 +126,25 @@
     return out
 
 
-def local_kernel(scale, index, extras, halves, *refs):
+def local_kernel(scale, index, extras, halves, spans, *refs):
     state_ref, w_ref = refs[0], refs[1]
     extra_refs = refs[2 : 2 + len(extras)]
-    out_ref = refs[2 + len(extras)]
+    copies = []
+    if spans:
+        block_ref, out_ref, loaded_ref, sems = refs[2 + len(extras) :]
+        at = 0
+        for number, (start, size) in enumerate(spans):
+            copies.append(
+                pltpu.make_async_copy(
+                    block_ref.at[0, :, start : start + size, :],
+                    loaded_ref.at[:, at : at + size, :],
+                    sems.at[number],
+                )
+            )
+            copies[-1].start()
+            at += size
+    else:
+        out_ref = refs[2 + len(extras)]
     row, lane = iotas()
     low_half_rows = row < 4
     low_half_lanes = lane < 64
@@ -230,6 +245,8 @@
                 for ref, factor in zip(extra_refs, extras):
                     base = base + np.float32(factor) * tile_of(ref, var, i, j)
                 out_ref[var, 8 * i : 8 * i + 8, LANES * j : LANES * (j + 1)] = base + change
+    for copy in copies:
+        copy.wait()
 
 
 def pack_x(lower, upper, xa_ref, xb_ref):
@@ -281,8 +298,9 @@
 
 
 def finish_kernel(
-    scale, index, with_faces, halves, state_ref, base_ref, xa_ref, xb_ref, ya_ref, yb_ref, *outs
+    scale, index, skip, halves, state_ref, base_ref, xa_ref, xb_ref, ya_ref, yb_ref, *outs
 ):
+    outs = outs[skip:]
     out_ref = outs[0]
     even_x, even_y = even_places()
     row, lane = iotas()
@@ -335,7 +353,7 @@
                 ]
             for var in range(VARS):
                 out_ref[(var,) + place] = values[var]
-    if with_faces:
+    if len(outs) > 1:
         pack_faces(out_ref, halves, *outs[1:])
 
 
@@ -382,21 +400,8 @@
     return begin, states, faces
 
 
-def prepare_kernel(spans, group, direct, owner_ref, local_ref, block_ref, after_ref, *refs):
+def prepare_kernel(group, direct, owner_ref, local_ref, after_ref, placing_ref, extra_ref):
     del after_ref
-    out_ref, placing_ref, extra_ref, sems = refs
-    copies = []
-    at = 0
-    for number, (start, size) in enumerate(spans):
-        copies.append(
-            pltpu.make_async_copy(
-                block_ref.at[0, :, start : start + size, :],
-                out_ref.at[:, at : at + size, :],
-                sems.at[number],
-            )
-        )
-        copies[-1].start()
-        at += size
     places, slots = placing_ref.shape
     capacity = places // group
     target = owner_ref[...]
@@ -423,25 +428,21 @@
         jnp.bfloat16
     )
     extra_ref[...] = jnp.broadcast_to(local_ref[...].astype(jnp.float32), extra_ref.shape)
-    for copy in copies:
-        copy.wait()
-
-
-def prepare(owners, local, blocks, after, group, capacity, direct):
-    slots = blocks.shape[3]
+
+
+def prepare(owners, local, after, group, capacity, direct):
+    slots = local.shape[1]
     return pl.pallas_call(
-        functools.partial(prepare_kernel, ((0, 16), (48, 16)), group, direct),
+        functools.partial(prepare_kernel, group, direct),
         out_shape=[
-            jax.ShapeDtypeStruct((64, 32, slots), jnp.float32),
             jax.ShapeDtypeStruct((group * capacity, slots), jnp.bfloat16),
             jax.ShapeDtypeStruct((8, slots), jnp.float32),
         ],
-        in_specs=[vmem_spec(), vmem_spec(), hbm_spec(), vmem_spec()],
-        out_specs=[vmem_spec()] * 3,
-        scratch_shapes=[pltpu.SemaphoreType.DMA((2,))],
+        in_specs=[vmem_spec()] * 3,
+        out_specs=[vmem_spec()] * 2,
         compiler_params=params(),
         name="prepare",
-    )(owners, local, in_hbm(blocks), after)
+    )(owners, local, after)
 
 
 def exchange_x(faces):
@@ -459,34 +460,47 @@
     return xa, xb, ya, yb
 
 
-def section(states, index, w, received, scale, extras, with_faces):
+def section(states, index, w, received, scale, extras, with_faces, load=None, after=()):
     columns = w.shape[2]
     halves = columns // LANES
     shape = jax.ShapeDtypeStruct(w.shape, jnp.float32)
     factors = tuple(f for _, f in extras)
-    base = pl.pallas_call(
-        functools.partial(local_kernel, scale, index, factors, halves),
-        out_shape=shape,
-        in_specs=[vmem_spec()] * (2 + len(extras)),
-        out_specs=vmem_spec(),
+    operands = [states, w] + [x for x, _ in extras]
+    in_specs = [vmem_spec()] * len(operands)
+    out_shape = [shape]
+    scratch = []
+    spans = ()
+    if load is not None:
+        blocks, spans = load
+        operands.append(in_hbm(blocks))
+        in_specs.append(hbm_spec())
+        nodes = sum(size for _, size in spans)
+        out_shape.append(jax.ShapeDtypeStruct((64, nodes, blocks.shape[3]), jnp.float32))
+        scratch = [pltpu.SemaphoreType.DMA((len(spans),))]
+    base, *loaded = pl.pallas_call(
+        functools.partial(local_kernel, scale, index, factors, halves, spans),
+        out_shape=out_shape,
+        in_specs=in_specs,
+        out_specs=[vmem_spec()] * len(out_shape),
+        scratch_shapes=scratch,
         compiler_params=params(),
         cost_estimate=pl.CostEstimate(
             flops=400 * 64 * columns, bytes_accessed=12 * VARS * 64 * columns, transcendentals=0
         ),
         name="local_part",
-    )(states, w, *[x for x, _ in extras])
+    )(*operands)
     out_shape = [shape] + (face_shapes(columns) if with_faces else [])
     results = pl.pallas_call(
-        functools.partial(finish_kernel, scale, index, with_faces, halves),
+        functools.partial(finish_kernel, scale, index, len(after), halves),
         out_shape=out_shape,
-        in_specs=[vmem_spec()] * 6,
+        in_specs=[vmem_spec()] * (6 + len(after)),
         out_specs=[vmem_spec()] * len(out_shape),
         compiler_params=params(),
         name="finish",
-    )(states, base, *received)
+    )(states, base, *received, *after)
     if with_faces:
         results = [results[0], exchange(results[1:])]
-    return results
+    return list(results) + loaded
 
 
 def reverse_step(states, begin, received):
@@ -498,12 +512,10 @@
     return result
 
 
-def split_three(x):
+def split_two(x):
     high = x.astype(jnp.bfloat16)
-    rest = x - high.astype(jnp.float32)
-    middle = rest.astype(jnp.bfloat16)
-    low = (rest - middle.astype(jnp.float32)).astype(jnp.bfloat16)
-    return high, middle, low
+    low = (x - high.astype(jnp.float32)).astype(jnp.bfloat16)
+    return high, low
 
 
 X_TILES = (0, 1, 6, 7)
@@ -553,14 +565,14 @@
 
     values = jnp.concatenate([held[...], extra_ref[...]], axis=0)
     total = values.shape[0]
-    pieces = jnp.concatenate(split_three(values), axis=0)
+    pieces = jnp.concatenate(split_two(values), axis=0)
     result = lax.dot_general(
         pieces,
         placing_ref[...],
         (((1,), (1,)), ((), ())),
         preferred_element_type=jnp.float32,
     )
-    result = result[0:total] + result[total : 2 * total] + result[2 * total :]
+    result = result[0:total] + result[total:]
     per = result.shape[1] // blocks
     for g in range(blocks):
         for part in range(per // LANES):
@@ -615,7 +627,7 @@
         for g in range(1 if number < firsts else ref.shape[0]):
             local = ref[g, rows : rows + 1, :].astype(jnp.int32)
             spot = (index == local).astype(jnp.float32).astype(jnp.bfloat16)
-            for piece in split_three(ref[g, 0:rows, :]):
+            for piece in split_two(ref[g, 0:rows, :]):
                 result = result + lax.dot_general(
                     piece, spot, (((1,), (1,)), ((), ())), preferred_element_type=jnp.float32
                 )
@@ -710,18 +722,26 @@
 
     direct = group in (2, 4, 8) and capacity == LANES
     outputs = group // 2 if direct else 1
-    outer, placing, extra = prepare(
+    placing, extra = prepare(
         owner_device_index.reshape(1, slots),
         owner_element_index,
-        proj_blocks,
         second,
         group,
         capacity,
         direct,
     )
-    first, received = section(states, 1, second, received, 0.25, [], True)
-    (result,) = section(
-        states, 0, first, received, 1.0, [(begin, 1.0 / 3.0), (second, 0.75)], False
+    first, received = section(
+        states, 1, second, received, 0.25, [], True, after=[extra]
+    )
+    result, outer = section(
+        states,
+        0,
+        first,
+        received,
+        1.0,
+        [(begin, 1.0 / 3.0), (second, 0.75)],
+        False,
+        load=(proj_blocks, ((0, 16), (48, 16))),
     )
 
     tiles = tuple((0, m) for m in range(4))

time: 72.6 us -> 71.8 us (0.989)
  waiting for transfers between devices: 13.7 us -> 12.2 us
  starting transfers between devices: 41.4 us -> 42.8 us
    ppermute x24, waiting for transfers between devices: 5.58 us -> 3.71 us  [swapped(): return lax.ppermute(value, axis, pairs)]
    pallas_call x7, Pallas kernels: 4.18 us -> 2.56 us  [the longest x6 1.92 us: section(): pl.pallas_call(functools.partial(finish_kernel, scale, index, len(after),...]
    pallas_call x6, Pallas kernels: 4.5 us -> 6.11 us  [section(): pl.pallas_call(functools.partial(local_kernel, scale, index, factors, hal...]
    ppermute x24, starting transfers between devices: 34.2 us -> 35.6 us  [swapped(): return lax.ppermute(value, axis, pairs)]
  transfers between devices with their start and end apart: 32 -> 32, of which waited for: 11 -> 11; matrix products, arithmetic and copies ran while one was open for 0% -> 0% of each run, Pallas kernels for 15% -> 14%
where the time goes in v3:
time: 71.8 us; the launch traced here: 71.6 us
  starting transfers between devices  42.8 us (60%)
  Pallas kernels  15.5 us (22%)
  waiting for transfers between devices  12.2 us (17%)
  between operations  0.91 us (1%)
    ppermute x24, starting transfers between devices, swapped(): return lax.ppermute(value, axis, pairs)  35.6 us
    ppermute x6, waiting for transfers between devices, send_chips(): mine[d] = lax.ppermute(values[d], ring, pairs)  8.47 us
    ppermute x6, starting transfers between devices, send_chips(): mine[d] = lax.ppermute(values[d], ring, pairs)  7.11 us
    pallas_call x6, Pallas kernels, section(): pl.pallas_call(functools.partial(local_kernel, scale, index, factors, hal...  6.11 us
    pallas_call x2, Pallas kernels, project(): pl.pallas_call(functools.partial(project_kernel, tiles, len(sources), out...  4.41 us
    ppermute x24, waiting for transfers between devices, swapped(): return lax.ppermute(value, axis, pairs)  3.71 us
    pallas_call x6, Pallas kernels, section(): pl.pallas_call(functools.partial(finish_kernel, scale, index, len(after),...  1.92 us
  transfers between devices with their start and end apart: 32, of which 11 were waited for; matrix products, arithmetic and copies ran while one was open for 0% of the time, Pallas kernels for 14%

profile of v3, /device:TPU:0, one launch (start us, length us, event | category | flops | bytes accessed | tf_op | source)
XLA Modules:
  0.0 71.6 jit_solution(1205643279154771062)
XLA Ops:
  0.7 1.3 %faces.1 = (f32[5,64,256]{2,1,0:T(8,128)S(1)}, f32[3,5,64,256]{3,2,1,0:T(8,128)S(1)}, f32[5,16,256]{2,1,0:T(8,128)S(1)}, f32[5,16,256]{2,1,0:T(8,128)S(1)}, f32[...) custom-call(f32[1,5,64,256]{3,2,1,0:T(8,128)} %w_hbm.1, f32[1,3,5,64,256]{4,3,2,1,0:T(8,128)} %state_hbm.1), custom_call_target="tpu_custom_call" | custom-call | tf_op jit(solution)/shard_map/faces/pallas_call | solution.py:391
  2.0 3.1 %collective-permute-start = (f32[5,16,256]{2,1,0:T(8,128)S(1)}, f32[5,16,256]{2,1,0:T(8,128)S(1)}, u32[]{:S(2)}, u32[]{:S(2)}) collective-permute-start(f32[5,16,256]{2,1,0:T(8,128)S(1)} %get-tuple-element.50), channel_id=1, source_target_pairs={{0,8},{8,0},{16,24},{24,16},{1,9},{9,1},{17,25},{25,17},{2,10},{10... | collective-permute-start | bytes 245768 | tf_op jit(solution)/shard_map/ppermute | solution.py:27
  5.1 2.5 %collective-permute-start.1 = (f32[5,16,256]{2,1,0:T(8,128)S(1)}, f32[5,16,256]{2,1,0:T(8,128)S(1)}, u32[]{:S(2)}, u32[]{:S(2)}) collective-permute-start(f32[5,16,256]{2,1,0:T(8,128)S(1)} %get-tuple-element.51), channel_id=1, source_target_pairs={{0,24},{8,16},{16,8},{24,0},{1,25},{9,17},{17,9},{25,1},{2,26},{10... | collective-permute-start | bytes 245768 | tf_op jit(solution)/shard_map/ppermute | solution.py:27
  7.6 2.6 %collective-permute-start.3 = (f32[5,8,128]{2,1,0:T(8,128)S(1)}, f32[5,8,128]{2,1,0:T(8,128)S(1)}, u32[]{:S(2)}, u32[]{:S(2)}) collective-permute-start(f32[5,8,128]{2,1,0:T(8,128)S(1)} %get-tuple-element.53), channel_id=1, source_target_pairs={{0,7},{1,2},{2,1},{3,4},{4,3},{5,6},{6,5},{7,0},{8,15},{9,10},{10,... | collective-permute-start | bytes 61448 | tf_op jit(solution)/shard_map/ppermute | solution.py:27
  10.1 0.7 local_part.6.base_ref
  10.8 0.8 %collective-permute-done.3.yb_ref = f32[5,8,128]{2,1,0:T(8,128)S(1)} collective-permute-done((f32[5,8,128]{2,1,0:T(8,128)S(1)}, f32[5,8,128]{2,1,0:T(8,128)S(1)}, u32[]{:S(2)}, u32[]{:S(2)}) %collective-permute-start.3) | collective-permute-done | bytes 20512 | tf_op jit(solution)/shard_map/ppermute | solution.py:27
  11.7 0.2 finish.6
  11.9 0.7 collective-permute-start.4
  12.6 2.4 %collective-permute-start.5 = (f32[5,16,256]{2,1,0:T(8,128)S(1)}, f32[5,16,256]{2,1,0:T(8,128)S(1)}, u32[]{:S(2)}, u32[]{:S(2)}) collective-permute-start(f32[5,16,256]{2,1,0:T(8,128)S(1)} %get-tuple-element.56), channel_id=1, source_target_pairs={{0,24},{8,16},{16,8},{24,0},{1,25},{9,17},{17,9},{25,1},{2,26},{10... | collective-permute-start | bytes 245768 | tf_op jit(solution)/shard_map/ppermute | solution.py:27
  15.1 2.6 %collective-permute-start.7 = (f32[5,8,128]{2,1,0:T(8,128)S(1)}, f32[5,8,128]{2,1,0:T(8,128)S(1)}, u32[]{:S(2)}, u32[]{:S(2)}) collective-permute-start(f32[5,8,128]{2,1,0:T(8,128)S(1)} %get-tuple-element.58), channel_id=1, source_target_pairs={{0,7},{1,2},{2,1},{3,4},{4,3},{5,6},{6,5},{7,0},{8,15},{9,10},{10,... | collective-permute-start | bytes 61448 | tf_op jit(solution)/shard_map/ppermute | solution.py:27
  17.6 0.6 prepare.1
  18.3 0.7 local_part.7.base_ref
  19.3 0.2 finish.7
  19.6 0.8 %collective-permute-start.8 = (f32[5,16,256]{2,1,0:T(8,128)S(1)}, f32[5,16,256]{2,1,0:T(8,128)S(1)}, u32[]{:S(2)}, u32[]{:S(2)}) collective-permute-start(f32[5,16,256]{2,1,0:T(8,128)S(1)} %get-tuple-element.62), channel_id=1, source_target_pairs={{0,8},{8,0},{16,24},{24,16},{1,9},{9,1},{17,25},{25,17},{2,10},{10... | collective-permute-start | bytes 245768 | tf_op jit(solution)/shard_map/ppermute | solution.py:27
  20.3 1.3 %collective-permute-start.9 = (f32[5,16,256]{2,1,0:T(8,128)S(1)}, f32[5,16,256]{2,1,0:T(8,128)S(1)}, u32[]{:S(2)}, u32[]{:S(2)}) collective-permute-start(f32[5,16,256]{2,1,0:T(8,128)S(1)} %get-tuple-element.63), channel_id=1, source_target_pairs={{0,24},{8,16},{16,8},{24,0},{1,25},{9,17},{17,9},{25,1},{2,26},{10... | collective-permute-start | bytes 245768 | tf_op jit(solution)/shard_map/ppermute | solution.py:27
  21.7 3.5 %collective-permute-start.11 = (f32[5,8,128]{2,1,0:T(8,128)S(1)}, f32[5,8,128]{2,1,0:T(8,128)S(1)}, u32[]{:S(2)}, u32[]{:S(2)}) collective-permute-start(f32[5,8,128]{2,1,0:T(8,128)S(1)} %get-tuple-element.65), channel_id=1, source_target_pairs={{0,7},{1,2},{2,1},{3,4},{4,3},{5,6},{6,5},{7,0},{8,15},{9,10},{10,... | collective-permute-start | bytes 61448 | tf_op jit(solution)/shard_map/ppermute | solution.py:27
  25.2 2.5 %local_part.8 = (f32[5,64,256]{2,1,0:T(8,128)S(1)}, f32[64,32,512]{2,1,0:T(8,128)S(1)}) custom-call(f32[3,5,64,256]{3,2,1,0:T(8,128)S(1)} %get-tuple-element.48.refs_0_.state_ref, f32[5,64,256]{2,1,0:T(8,128)S(1)} %get-tuple-element.60.refs_1_, f32[5,64,256]{2,1,0:T(8,128)S(1)} %get-tuple-element.49.refs_1_.refs_2_, ...), custom_call_target="tpu_custom_call" | custom-call | flops 6553600 | bytes 983040 | tf_op jit(solution)/shard_map/local_part/pallas_call | solution.py:480
  27.9 2.2 %project.2 = (f32[2,168,128]{2,1,0:T(8,128)S(1)}, f32[2,168,128]{2,1,0:T(8,128)S(1)}, f32[2,168,128]{2,1,0:T(8,128)S(1)}, f32[2,168,128]{2,1,0:T(8,128)S(1)}, f32[64,32,512]{2,1,0:T(8,128)S(1)}) custom-call(f32[5,64,256]{2,1,0:T(8,128)S(1)} %finish.8.refs_0_, f32[64,32,512]{2,1,0:T(8,128)S(1)} %get-tuple-element.66.refs_1_, ...), custom_call_target="tpu_custom_call" | custom-call | flops 4000000000 | bytes 20971520 | tf_op jit(solution)/shard_map/project/pallas_call | solution.py:603
  30.1 0.8 %collective-permute-start.16 = (f32[2,168,128]{2,1,0:T(8,128)S(1)}, f32[2,168,128]{2,1,0:T(8,128)S(1)}, u32[]{:S(2)}, u32[]{:S(2)}) collective-permute-start(f32[2,168,128]{2,1,0:T(8,128)S(1)} %get-tuple-element.75), channel_id=1, source_target_pairs={{0,2},{1,3},{2,0},{3,1},{4,6},{5,7},{6,4},{7,5},{8,10},{9,11},{10,... | collective-permute-start | bytes 516104 | tf_op jit(solution)/shard_map/ppermute | solution.py:691
  30.9 1.5 %collective-permute-start.17 = (f32[2,168,128]{2,1,0:T(8,128)S(1)}, f32[2,168,128]{2,1,0:T(8,128)S(1)}, u32[]{:S(2)}, u32[]{:S(2)}) collective-permute-start(f32[2,168,128]{2,1,0:T(8,128)S(1)} %get-tuple-element.76), channel_id=1, source_target_pairs={{0,4},{1,5},{2,6},{3,7},{4,0},{5,1},{6,2},{7,3},{8,12},{9,13},{10,... | collective-permute-start | bytes 516104 | tf_op jit(solution)/shard_map/ppermute | solution.py:691
  32.4 1.3 %collective-permute-start.18 = (f32[2,168,128]{2,1,0:T(8,128)S(1)}, f32[2,168,128]{2,1,0:T(8,128)S(1)}, u32[]{:S(2)}, u32[]{:S(2)}) collective-permute-start(f32[2,168,128]{2,1,0:T(8,128)S(1)} %get-tuple-element.77), channel_id=1, source_target_pairs={{0,6},{1,7},{2,4},{3,5},{4,2},{5,3},{6,0},{7,1},{8,14},{9,15},{10,... | collective-permute-start | bytes 516104 | tf_op jit(solution)/shard_map/ppermute | solution.py:691
  33.6 2.2 %project.3 = (f32[2,168,128]{2,1,0:T(8,128)S(1)}, f32[2,168,128]{2,1,0:T(8,128)S(1)}, f32[2,168,128]{2,1,0:T(8,128)S(1)}, f32[2,168,128]{2,1,0:T(8,128)S(1)}, f32[5,64,256]{2,1,0:T(8,128)}) custom-call(f32[5,64,256]{2,1,0:T(8,128)S(1)} %finish.8.refs_0_, f32[64,32,512]{2,1,0:T(8,128)S(1)} %get-tuple-element.68.refs_1_, ...), custom_call_target="tpu_custom_call" | custom-call | flops 4000000000 | bytes 20971520 | tf_op jit(solution)/shard_map/project/pallas_call | solution.py:603
  35.8 0.8 %collective-permute-start.12 = (f32[2,168,128]{2,1,0:T(8,128)S(1)}, f32[2,168,128]{2,1,0:T(8,128)S(1)}, u32[]{:S(2)}, u32[]{:S(2)}) collective-permute-start(f32[2,168,128]{2,1,0:T(8,128)S(1)} %get-tuple-element.71), channel_id=1, source_target_pairs={{0,2},{1,3},{2,0},{3,1},{4,6},{5,7},{6,4},{7,5},{8,10},{9,11},{10,... | collective-permute-start | bytes 516104 | tf_op jit(solution)/shard_map/ppermute | solution.py:691
  36.6 1.5 %collective-permute-start.13 = (f32[2,168,128]{2,1,0:T(8,128)S(1)}, f32[2,168,128]{2,1,0:T(8,128)S(1)}, u32[]{:S(2)}, u32[]{:S(2)}) collective-permute-start(f32[2,168,128]{2,1,0:T(8,128)S(1)} %get-tuple-element.72), channel_id=1, source_target_pairs={{0,4},{1,5},{2,6},{3,7},{4,0},{5,1},{6,2},{7,3},{8,12},{9,13},{10,... | collective-permute-start | bytes 516104 | tf_op jit(solution)/shard_map/ppermute | solution.py:691
  38.1 1.3 %collective-permute-start.14 = (f32[2,168,128]{2,1,0:T(8,128)S(1)}, f32[2,168,128]{2,1,0:T(8,128)S(1)}, u32[]{:S(2)}, u32[]{:S(2)}) collective-permute-start(f32[2,168,128]{2,1,0:T(8,128)S(1)} %get-tuple-element.73), channel_id=1, source_target_pairs={{0,6},{1,7},{2,4},{3,5},{4,2},{5,3},{6,0},{7,1},{8,14},{9,15},{10,... | collective-permute-start | bytes 516104 | tf_op jit(solution)/shard_map/ppermute | solution.py:691
  39.5 2.7 %collective-permute-done.18.refs_3_ = f32[2,168,128]{2,1,0:T(8,128)S(1)} collective-permute-done((f32[2,168,128]{2,1,0:T(8,128)S(1)}, f32[2,168,128]{2,1,0:T(8,128)S(1)}, u32[]{:S(2)}, u32[]{:S(2)}) %collective-permute-start.18) | collective-permute-done | bytes 172064 | tf_op jit(solution)/shard_map/ppermute | solution.py:691
  42.3 2.1 %collective-permute-done.12.refs_1_ = f32[2,168,128]{2,1,0:T(8,128)S(1)} collective-permute-done((f32[2,168,128]{2,1,0:T(8,128)S(1)}, f32[2,168,128]{2,1,0:T(8,128)S(1)}, u32[]{:S(2)}, u32[]{:S(2)}) %collective-permute-start.12) | collective-permute-done | bytes 172064 | tf_op jit(solution)/shard_map/ppermute | solution.py:691
  44.4 1.1 %collective-permute-done.13.refs_2_ = f32[2,168,128]{2,1,0:T(8,128)S(1)} collective-permute-done((f32[2,168,128]{2,1,0:T(8,128)S(1)}, f32[2,168,128]{2,1,0:T(8,128)S(1)}, u32[]{:S(2)}, u32[]{:S(2)}) %collective-permute-start.13) | collective-permute-done | bytes 172064 | tf_op jit(solution)/shard_map/ppermute | solution.py:691
  45.5 2.5 %collective-permute-done.14.refs_3_ = f32[2,168,128]{2,1,0:T(8,128)S(1)} collective-permute-done((f32[2,168,128]{2,1,0:T(8,128)S(1)}, f32[2,168,128]{2,1,0:T(8,128)S(1)}, u32[]{:S(2)}, u32[]{:S(2)}) %collective-permute-start.14) | collective-permute-done | bytes 172064 | tf_op jit(solution)/shard_map/ppermute | solution.py:691
  48.2 0.5 receive.2
  48.7 0.2 collective-permute-start.20
  49.0 1.8 %collective-permute-start.21 = (f32[5,16,256]{2,1,0:T(8,128)S(1)}, f32[5,16,256]{2,1,0:T(8,128)S(1)}, u32[]{:S(2)}, u32[]{:S(2)}) collective-permute-start(f32[5,16,256]{2,1,0:T(8,128)S(1)} %get-tuple-element.81), channel_id=1, source_target_pairs={{0,24},{8,16},{16,8},{24,0},{1,25},{9,17},{17,9},{25,1},{2,26},{10... | collective-permute-start | bytes 245768 | tf_op jit(solution)/shard_map/ppermute | solution.py:27
  50.7 0.6 receive.3
  51.3 0.2 collective-permute-start.22
  51.6 2.5 %collective-permute-start.23 = (f32[5,8,128]{2,1,0:T(8,128)S(1)}, f32[5,8,128]{2,1,0:T(8,128)S(1)}, u32[]{:S(2)}, u32[]{:S(2)}) collective-permute-start(f32[5,8,128]{2,1,0:T(8,128)S(1)} %get-tuple-element.83), channel_id=1, source_target_pairs={{0,7},{1,2},{2,1},{3,4},{4,3},{5,6},{6,5},{7,0},{8,15},{9,10},{10,... | collective-permute-start | bytes 61448 | tf_op jit(solution)/shard_map/ppermute | solution.py:27
  54.1 0.7 local_part.9.base_ref
  54.8 0.8 %collective-permute-done.23.yb_ref = f32[5,8,128]{2,1,0:T(8,128)S(1)} collective-permute-done((f32[5,8,128]{2,1,0:T(8,128)S(1)}, f32[5,8,128]{2,1,0:T(8,128)S(1)}, u32[]{:S(2)}, u32[]{:S(2)}) %collective-permute-start.23) | collective-permute-done | bytes 20512 | tf_op jit(solution)/shard_map/ppermute | solution.py:27
  55.7 0.2 finish.9
  55.9 1.5 %collective-permute-start.24 = (f32[5,16,256]{2,1,0:T(8,128)S(1)}, f32[5,16,256]{2,1,0:T(8,128)S(1)}, u32[]{:S(2)}, u32[]{:S(2)}) collective-permute-start(f32[5,16,256]{2,1,0:T(8,128)S(1)} %get-tuple-element.85), channel_id=1, source_target_pairs={{0,8},{8,0},{16,24},{24,16},{1,9},{9,1},{17,25},{25,17},{2,10},{10... | collective-permute-start | bytes 245768 | tf_op jit(solution)/shard_map/ppermute | solution.py:27
  57.4 1.8 %collective-permute-start.25 = (f32[5,16,256]{2,1,0:T(8,128)S(1)}, f32[5,16,256]{2,1,0:T(8,128)S(1)}, u32[]{:S(2)}, u32[]{:S(2)}) collective-permute-start(f32[5,16,256]{2,1,0:T(8,128)S(1)} %get-tuple-element.86), channel_id=1, source_target_pairs={{0,24},{8,16},{16,8},{24,0},{1,25},{9,17},{17,9},{25,1},{2,26},{10... | collective-permute-start | bytes 245768 | tf_op jit(solution)/shard_map/ppermute | solution.py:27
  59.2 2.7 %collective-permute-start.27 = (f32[5,8,128]{2,1,0:T(8,128)S(1)}, f32[5,8,128]{2,1,0:T(8,128)S(1)}, u32[]{:S(2)}, u32[]{:S(2)}) collective-permute-start(f32[5,8,128]{2,1,0:T(8,128)S(1)} %get-tuple-element.88), channel_id=1, source_target_pairs={{0,7},{1,2},{2,1},{3,4},{4,3},{5,6},{6,5},{7,0},{8,15},{9,10},{10,... | collective-permute-start | bytes 61448 | tf_op jit(solution)/shard_map/ppermute | solution.py:27
  62.0 0.7 local_part.10.base_ref
  62.7 0.8 %collective-permute-done.27.yb_ref = f32[5,8,128]{2,1,0:T(8,128)S(1)} collective-permute-done((f32[5,8,128]{2,1,0:T(8,128)S(1)}, f32[5,8,128]{2,1,0:T(8,128)S(1)}, u32[]{:S(2)}, u32[]{:S(2)}) %collective-permute-start.27) | collective-permute-done | bytes 20512 | tf_op jit(solution)/shard_map/ppermute | solution.py:27
  63.9 1.9 %collective-permute-start.29 = (f32[5,16,256]{2,1,0:T(8,128)S(1)}, f32[5,16,256]{2,1,0:T(8,128)S(1)}, u32[]{:S(2)}, u32[]{:S(2)}) collective-permute-start(f32[5,16,256]{2,1,0:T(8,128)S(1)} %get-tuple-element.91), channel_id=1, source_target_pairs={{0,24},{8,16},{16,8},{24,0},{1,25},{9,17},{17,9},{25,1},{2,26},{10... | collective-permute-start | bytes 245768 | tf_op jit(solution)/shard_map/ppermute | solution.py:27
  65.9 3.3 %collective-permute-start.31 = (f32[5,8,128]{2,1,0:T(8,128)S(1)}, f32[5,8,128]{2,1,0:T(8,128)S(1)}, u32[]{:S(2)}, u32[]{:S(2)}) collective-permute-start(f32[5,8,128]{2,1,0:T(8,128)S(1)} %get-tuple-element.93), channel_id=1, source_target_pairs={{0,7},{1,2},{2,1},{3,4},{4,3},{5,6},{6,5},{7,0},{8,15},{9,10},{10,... | collective-permute-start | bytes 61448 | tf_op jit(solution)/shard_map/ppermute | solution.py:27
  69.2 0.8 %local_part.11.base_ref = f32[5,64,256]{2,1,0:T(8,128)S(1)} custom-call(f32[3,5,64,256]{3,2,1,0:T(8,128)S(1)} %bitcast.8, f32[5,64,256]{2,1,0:T(8,128)S(1)} %get-tuple-element.89.refs_1_, f32[5,64,256]{2,1,0:T(8,128)S(1)} %get-tuple-element.79.refs_1_.refs_2_, f32[5,64,256]{2,1,0:T(8,128)S(1)} %get-tuple-element.84.refs_1_.refs_3_), custom_call_target="tpu_custom_call" | custom-call | flops 6553600 | bytes 983040 | tf_op jit(solution)/shard_map/local_part/pallas_call | solution.py:480
  70.0 0.7 collective-permute-done.31.yb_ref
  70.7 0.9 %finish.11 = f32[5,64,256]{2,1,0:T(8,128)} custom-call(f32[3,5,64,256]{3,2,1,0:T(8,128)S(1)} %bitcast.9, f32[5,64,256]{2,1,0:T(8,128)S(1)} %local_part.11.base_ref, f32[5,16,256]{2,1,0:T(8,128)S(1)} %collective-permute-done.28.xa_ref, f32[5,16,256]{2,1,0:T(8,128)S(1)} %collective-permute-done.29.xb_ref, f32[5,8,128]{2,1,0:T(8,128)S(1)} %collective-permute-done.30.ya_ref, ...), custom_call_target="tpu_custom_call" | custom-call | tf_op jit(solution)/shard_map/finish/pallas_call | solution.py:493
  (50 shorter events, 1.4 us)
Async XLA Ops:
  0.6 17.0 %copy-start.2 = (s32[1,512]{1,0:T(1,128)S(1)}, s32[1,512]{1,0:T(1,128)}, u32[]{:S(2)}) copy-start(s32[1,512]{1,0:T(1,128)} %local_ref.1) | copy-start | bytes 6148
  0.6 17.0 %copy-start.1 = (s32[1,512,1]{1,2,0:T(1,128)S(1)}, s32[1,512,1]{1,2,0:T(1,128)}, u32[]{:S(2)}) copy-start(s32[1,512,1]{1,2,0:T(1,128)} %param.9) | copy-start | bytes 6148
  2.0 9.7 %collective-permute-start = (f32[5,16,256]{2,1,0:T(8,128)S(1)}, f32[5,16,256]{2,1,0:T(8,128)S(1)}, u32[]{:S(2)}, u32[]{:S(2)}) collective-permute-start(f32[5,16,256]{2,1,0:T(8,128)S(1)} %get-tuple-element.50), channel_id=1, source_target_pairs={{0,8},{8,0},{16,24},{24,16},{1,9},{9,1},{17,25},{25,17},{2,10},{10... | collective-permute-start | bytes 245768 | tf_op jit(solution)/shard_map/ppermute | solution.py:27
  5.1 6.6 %collective-permute-start.1 = (f32[5,16,256]{2,1,0:T(8,128)S(1)}, f32[5,16,256]{2,1,0:T(8,128)S(1)}, u32[]{:S(2)}, u32[]{:S(2)}) collective-permute-start(f32[5,16,256]{2,1,0:T(8,128)S(1)} %get-tuple-element.51), channel_id=1, source_target_pairs={{0,24},{8,16},{16,8},{24,0},{1,25},{9,17},{17,9},{25,1},{2,26},{10... | collective-permute-start | bytes 245768 | tf_op jit(solution)/shard_map/ppermute | solution.py:27
  7.6 3.3 %collective-permute-start.2 = (f32[5,8,128]{2,1,0:T(8,128)S(1)}, f32[5,8,128]{2,1,0:T(8,128)S(1)}, u32[]{:S(2)}, u32[]{:S(2)}) collective-permute-start(f32[5,8,128]{2,1,0:T(8,128)S(1)} %get-tuple-element.52), channel_id=1, source_target_pairs={{0,1},{1,0},{2,3},{3,2},{4,5},{5,4},{6,7},{7,6},{8,9},{9,8},{10,11... | collective-permute-start | bytes 61448 | tf_op jit(solution)/shard_map/ppermute | solution.py:27
  7.6 4.1 %collective-permute-start.3 = (f32[5,8,128]{2,1,0:T(8,128)S(1)}, f32[5,8,128]{2,1,0:T(8,128)S(1)}, u32[]{:S(2)}, u32[]{:S(2)}) collective-permute-start(f32[5,8,128]{2,1,0:T(8,128)S(1)} %get-tuple-element.53), channel_id=1, source_target_pairs={{0,7},{1,2},{2,1},{3,4},{4,3},{5,6},{6,5},{7,0},{8,15},{9,10},{10,... | collective-permute-start | bytes 61448 | tf_op jit(solution)/shard_map/ppermute | solution.py:27
  11.9 7.3 %collective-permute-start.4 = (f32[5,16,256]{2,1,0:T(8,128)S(1)}, f32[5,16,256]{2,1,0:T(8,128)S(1)}, u32[]{:S(2)}, u32[]{:S(2)}) collective-permute-start(f32[5,16,256]{2,1,0:T(8,128)S(1)} %get-tuple-element.55), channel_id=1, source_target_pairs={{0,8},{8,0},{16,24},{24,16},{1,9},{9,1},{17,25},{25,17},{2,10},{10... | collective-permute-start | bytes 245768 | tf_op jit(solution)/shard_map/ppermute | solution.py:27
  12.6 6.7 %collective-permute-start.5 = (f32[5,16,256]{2,1,0:T(8,128)S(1)}, f32[5,16,256]{2,1,0:T(8,128)S(1)}, u32[]{:S(2)}, u32[]{:S(2)}) collective-permute-start(f32[5,16,256]{2,1,0:T(8,128)S(1)} %get-tuple-element.56), channel_id=1, source_target_pairs={{0,24},{8,16},{16,8},{24,0},{1,25},{9,17},{17,9},{25,1},{2,26},{10... | collective-permute-start | bytes 245768 | tf_op jit(solution)/shard_map/ppermute | solution.py:27
  15.1 3.9 %collective-permute-start.6 = (f32[5,8,128]{2,1,0:T(8,128)S(1)}, f32[5,8,128]{2,1,0:T(8,128)S(1)}, u32[]{:S(2)}, u32[]{:S(2)}) collective-permute-start(f32[5,8,128]{2,1,0:T(8,128)S(1)} %get-tuple-element.57), channel_id=1, source_target_pairs={{0,1},{1,0},{2,3},{3,2},{4,5},{5,4},{6,7},{7,6},{8,9},{9,8},{10,11... | collective-permute-start | bytes 61448 | tf_op jit(solution)/shard_map/ppermute | solution.py:27
  15.1 4.1 %collective-permute-start.7 = (f32[5,8,128]{2,1,0:T(8,128)S(1)}, f32[5,8,128]{2,1,0:T(8,128)S(1)}, u32[]{:S(2)}, u32[]{:S(2)}) collective-permute-start(f32[5,8,128]{2,1,0:T(8,128)S(1)} %get-tuple-element.58), channel_id=1, source_target_pairs={{0,7},{1,2},{2,1},{3,4},{4,3},{5,6},{6,5},{7,0},{8,15},{9,10},{10,... | collective-permute-start | bytes 61448 | tf_op jit(solution)/shard_map/ppermute | solution.py:27
  19.6 8.1 %collective-permute-start.8 = (f32[5,16,256]{2,1,0:T(8,128)S(1)}, f32[5,16,256]{2,1,0:T(8,128)S(1)}, u32[]{:S(2)}, u32[]{:S(2)}) collective-permute-start(f32[5,16,256]{2,1,0:T(8,128)S(1)} %get-tuple-element.62), channel_id=1, source_target_pairs={{0,8},{8,0},{16,24},{24,16},{1,9},{9,1},{17,25},{25,17},{2,10},{10... | collective-permute-start | bytes 245768 | tf_op jit(solution)/shard_map/ppermute | solution.py:27
  20.3 7.4 %collective-permute-start.9 = (f32[5,16,256]{2,1,0:T(8,128)S(1)}, f32[5,16,256]{2,1,0:T(8,128)S(1)}, u32[]{:S(2)}, u32[]{:S(2)}) collective-permute-start(f32[5,16,256]{2,1,0:T(8,128)S(1)} %get-tuple-element.63), channel_id=1, source_target_pairs={{0,24},{8,16},{16,8},{24,0},{1,25},{9,17},{17,9},{25,1},{2,26},{10... | collective-permute-start | bytes 245768 | tf_op jit(solution)/shard_map/ppermute | solution.py:27
  21.7 6.0 %collective-permute-start.10 = (f32[5,8,128]{2,1,0:T(8,128)S(1)}, f32[5,8,128]{2,1,0:T(8,128)S(1)}, u32[]{:S(2)}, u32[]{:S(2)}) collective-permute-start(f32[5,8,128]{2,1,0:T(8,128)S(1)} %get-tuple-element.64), channel_id=1, source_target_pairs={{0,1},{1,0},{2,3},{3,2},{4,5},{5,4},{6,7},{7,6},{8,9},{9,8},{10,11... | collective-permute-start | bytes 61448 | tf_op jit(solution)/shard_map/ppermute | solution.py:27
  21.7 6.0 %collective-permute-start.11 = (f32[5,8,128]{2,1,0:T(8,128)S(1)}, f32[5,8,128]{2,1,0:T(8,128)S(1)}, u32[]{:S(2)}, u32[]{:S(2)}) collective-permute-start(f32[5,8,128]{2,1,0:T(8,128)S(1)} %get-tuple-element.65), channel_id=1, source_target_pairs={{0,7},{1,2},{2,1},{3,4},{4,3},{5,6},{6,5},{7,0},{8,15},{9,10},{10,... | collective-permute-start | bytes 61448 | tf_op jit(solution)/shard_map/ppermute | solution.py:27
  30.1 8.0 %collective-permute-start.16 = (f32[2,168,128]{2,1,0:T(8,128)S(1)}, f32[2,168,128]{2,1,0:T(8,128)S(1)}, u32[]{:S(2)}, u32[]{:S(2)}) collective-permute-start(f32[2,168,128]{2,1,0:T(8,128)S(1)} %get-tuple-element.75), channel_id=1, source_target_pairs={{0,2},{1,3},{2,0},{3,1},{4,6},{5,7},{6,4},{7,5},{8,10},{9,11},{10,... | collective-permute-start | bytes 516104 | tf_op jit(solution)/shard_map/ppermute | solution.py:691
  30.9 8.6 %collective-permute-start.17 = (f32[2,168,128]{2,1,0:T(8,128)S(1)}, f32[2,168,128]{2,1,0:T(8,128)S(1)}, u32[]{:S(2)}, u32[]{:S(2)}) collective-permute-start(f32[2,168,128]{2,1,0:T(8,128)S(1)} %get-tuple-element.76), channel_id=1, source_target_pairs={{0,4},{1,5},{2,6},{3,7},{4,0},{5,1},{6,2},{7,3},{8,12},{9,13},{10,... | collective-permute-start | bytes 516104 | tf_op jit(solution)/shard_map/ppermute | solution.py:691
  32.4 9.8 %collective-permute-start.18 = (f32[2,168,128]{2,1,0:T(8,128)S(1)}, f32[2,168,128]{2,1,0:T(8,128)S(1)}, u32[]{:S(2)}, u32[]{:S(2)}) collective-permute-start(f32[2,168,128]{2,1,0:T(8,128)S(1)} %get-tuple-element.77), channel_id=1, source_target_pairs={{0,6},{1,7},{2,4},{3,5},{4,2},{5,3},{6,0},{7,1},{8,14},{9,15},{10,... | collective-permute-start | bytes 516104 | tf_op jit(solution)/shard_map/ppermute | solution.py:691
  35.8 8.6 %collective-permute-start.12 = (f32[2,168,128]{2,1,0:T(8,128)S(1)}, f32[2,168,128]{2,1,0:T(8,128)S(1)}, u32[]{:S(2)}, u32[]{:S(2)}) collective-permute-start(f32[2,168,128]{2,1,0:T(8,128)S(1)} %get-tuple-element.71), channel_id=1, source_target_pairs={{0,2},{1,3},{2,0},{3,1},{4,6},{5,7},{6,4},{7,5},{8,10},{9,11},{10,... | collective-permute-start | bytes 516104 | tf_op jit(solution)/shard_map/ppermute | solution.py:691
  36.6 8.9 %collective-permute-start.13 = (f32[2,168,128]{2,1,0:T(8,128)S(1)}, f32[2,168,128]{2,1,0:T(8,128)S(1)}, u32[]{:S(2)}, u32[]{:S(2)}) collective-permute-start(f32[2,168,128]{2,1,0:T(8,128)S(1)} %get-tuple-element.72), channel_id=1, source_target_pairs={{0,4},{1,5},{2,6},{3,7},{4,0},{5,1},{6,2},{7,3},{8,12},{9,13},{10,... | collective-permute-start | bytes 516104 | tf_op jit(solution)/shard_map/ppermute | solution.py:691
  38.1 9.9 %collective-permute-start.14 = (f32[2,168,128]{2,1,0:T(8,128)S(1)}, f32[2,168,128]{2,1,0:T(8,128)S(1)}, u32[]{:S(2)}, u32[]{:S(2)}) collective-permute-start(f32[2,168,128]{2,1,0:T(8,128)S(1)} %get-tuple-element.73), channel_id=1, source_target_pairs={{0,6},{1,7},{2,4},{3,5},{4,2},{5,3},{6,0},{7,1},{8,14},{9,15},{10,... | collective-permute-start | bytes 516104 | tf_op jit(solution)/shard_map/ppermute | solution.py:691
  42.2 6.0 %collective-permute-start.19 = (f32[4,168,128]{2,1,0:T(8,128)S(1)}, f32[4,168,128]{2,1,0:T(8,128)S(1)}, u32[]{:S(2)}, u32[]{:S(2)}) collective-permute-start(f32[4,168,128]{2,1,0:T(8,128)S(1)} %pad_maximum_fusion.1), channel_id=1, source_target_pairs={{0,1},{1,0},{2,3},{3,2},{4,5},{5,4},{6,7},{7,6},{8,9},{9,8},{10,11... | collective-permute-start | bytes 1032200 | tf_op jit(solution)/shard_map/ppermute | solution.py:698
  44.4 9.7 %copy-start = (f32[1,3,5,64,256]{4,3,2,1,0:T(8,128)S(1)}, f32[1,3,5,64,256]{4,3,2,1,0:T(8,128)}, u32[]{:S(2)}) copy-start(f32[1,3,5,64,256]{4,3,2,1,0:T(8,128)} %param.8) | copy-start | bytes 2949124
  48.1 2.6 %collective-permute-start.15 = (f32[4,168,128]{2,1,0:T(8,128)S(1)}, f32[4,168,128]{2,1,0:T(8,128)S(1)}, u32[]{:S(2)}, u32[]{:S(2)}) collective-permute-start(f32[4,168,128]{2,1,0:T(8,128)S(1)} %pad_maximum_fusion), channel_id=1, source_target_pairs={{0,1},{1,0},{2,3},{3,2},{4,5},{5,4},{6,7},{7,6},{8,9},{9,8},{10,11... | collective-permute-start | bytes 1032200 | tf_op jit(solution)/shard_map/ppermute | solution.py:698
  48.7 6.9 %collective-permute-start.20 = (f32[5,16,256]{2,1,0:T(8,128)S(1)}, f32[5,16,256]{2,1,0:T(8,128)S(1)}, u32[]{:S(2)}, u32[]{:S(2)}) collective-permute-start(f32[5,16,256]{2,1,0:T(8,128)S(1)} %get-tuple-element.80), channel_id=1, source_target_pairs={{0,8},{8,0},{16,24},{24,16},{1,9},{9,1},{17,25},{25,17},{2,10},{10... | collective-permute-start | bytes 245768 | tf_op jit(solution)/shard_map/ppermute | solution.py:27
  49.0 6.7 %collective-permute-start.21 = (f32[5,16,256]{2,1,0:T(8,128)S(1)}, f32[5,16,256]{2,1,0:T(8,128)S(1)}, u32[]{:S(2)}, u32[]{:S(2)}) collective-permute-start(f32[5,16,256]{2,1,0:T(8,128)S(1)} %get-tuple-element.81), channel_id=1, source_target_pairs={{0,24},{8,16},{16,8},{24,0},{1,25},{9,17},{17,9},{25,1},{2,26},{10... | collective-permute-start | bytes 245768 | tf_op jit(solution)/shard_map/ppermute | solution.py:27
  51.3 3.5 %collective-permute-start.22 = (f32[5,8,128]{2,1,0:T(8,128)S(1)}, f32[5,8,128]{2,1,0:T(8,128)S(1)}, u32[]{:S(2)}, u32[]{:S(2)}) collective-permute-start(f32[5,8,128]{2,1,0:T(8,128)S(1)} %get-tuple-element.82), channel_id=1, source_target_pairs={{0,1},{1,0},{2,3},{3,2},{4,5},{5,4},{6,7},{7,6},{8,9},{9,8},{10,11... | collective-permute-start | bytes 61448 | tf_op jit(solution)/shard_map/ppermute | solution.py:27
  51.6 4.1 %collective-permute-start.23 = (f32[5,8,128]{2,1,0:T(8,128)S(1)}, f32[5,8,128]{2,1,0:T(8,128)S(1)}, u32[]{:S(2)}, u32[]{:S(2)}) collective-permute-start(f32[5,8,128]{2,1,0:T(8,128)S(1)} %get-tuple-element.83), channel_id=1, source_target_pairs={{0,7},{1,2},{2,1},{3,4},{4,3},{5,6},{6,5},{7,0},{8,15},{9,10},{10,... | collective-permute-start | bytes 61448 | tf_op jit(solution)/shard_map/ppermute | solution.py:27
  55.9 7.6 %collective-permute-start.24 = (f32[5,16,256]{2,1,0:T(8,128)S(1)}, f32[5,16,256]{2,1,0:T(8,128)S(1)}, u32[]{:S(2)}, u32[]{:S(2)}) collective-permute-start(f32[5,16,256]{2,1,0:T(8,128)S(1)} %get-tuple-element.85), channel_id=1, source_target_pairs={{0,8},{8,0},{16,24},{24,16},{1,9},{9,1},{17,25},{25,17},{2,10},{10... | collective-permute-start | bytes 245768 | tf_op jit(solution)/shard_map/ppermute | solution.py:27
  57.4 6.2 %collective-permute-start.25 = (f32[5,16,256]{2,1,0:T(8,128)S(1)}, f32[5,16,256]{2,1,0:T(8,128)S(1)}, u32[]{:S(2)}, u32[]{:S(2)}) collective-permute-start(f32[5,16,256]{2,1,0:T(8,128)S(1)} %get-tuple-element.86), channel_id=1, source_target_pairs={{0,24},{8,16},{16,8},{24,0},{1,25},{9,17},{17,9},{25,1},{2,26},{10... | collective-permute-start | bytes 245768 | tf_op jit(solution)/shard_map/ppermute | solution.py:27
  59.2 3.5 %collective-permute-start.26 = (f32[5,8,128]{2,1,0:T(8,128)S(1)}, f32[5,8,128]{2,1,0:T(8,128)S(1)}, u32[]{:S(2)}, u32[]{:S(2)}) collective-permute-start(f32[5,8,128]{2,1,0:T(8,128)S(1)} %get-tuple-element.87), channel_id=1, source_target_pairs={{0,1},{1,0},{2,3},{3,2},{4,5},{5,4},{6,7},{7,6},{8,9},{9,8},{10,11... | collective-permute-start | bytes 61448 | tf_op jit(solution)/shard_map/ppermute | solution.py:27
  59.2 4.2 %collective-permute-start.27 = (f32[5,8,128]{2,1,0:T(8,128)S(1)}, f32[5,8,128]{2,1,0:T(8,128)S(1)}, u32[]{:S(2)}, u32[]{:S(2)}) collective-permute-start(f32[5,8,128]{2,1,0:T(8,128)S(1)} %get-tuple-element.88), channel_id=1, source_target_pairs={{0,7},{1,2},{2,1},{3,4},{4,3},{5,6},{6,5},{7,0},{8,15},{9,10},{10,... | collective-permute-start | bytes 61448 | tf_op jit(solution)/shard_map/ppermute | solution.py:27
  63.9 6.8 %collective-permute-start.28 = (f32[5,16,256]{2,1,0:T(8,128)S(1)}, f32[5,16,256]{2,1,0:T(8,128)S(1)}, u32[]{:S(2)}, u32[]{:S(2)}) collective-permute-start(f32[5,16,256]{2,1,0:T(8,128)S(1)} %get-tuple-element.90), channel_id=1, source_target_pairs={{0,8},{8,0},{16,24},{24,16},{1,9},{9,1},{17,25},{25,17},{2,10},{10... | collective-permute-start | bytes 245768 | tf_op jit(solution)/shard_map/ppermute | solution.py:27
  63.9 6.7 %collective-permute-start.29 = (f32[5,16,256]{2,1,0:T(8,128)S(1)}, f32[5,16,256]{2,1,0:T(8,128)S(1)}, u32[]{:S(2)}, u32[]{:S(2)}) collective-permute-start(f32[5,16,256]{2,1,0:T(8,128)S(1)} %get-tuple-element.91), channel_id=1, source_target_pairs={{0,24},{8,16},{16,8},{24,0},{1,25},{9,17},{17,9},{25,1},{2,26},{10... | collective-permute-start | bytes 245768 | tf_op jit(solution)/shard_map/ppermute | solution.py:27
  65.9 4.1 %collective-permute-start.30 = (f32[5,8,128]{2,1,0:T(8,128)S(1)}, f32[5,8,128]{2,1,0:T(8,128)S(1)}, u32[]{:S(2)}, u32[]{:S(2)}) collective-permute-start(f32[5,8,128]{2,1,0:T(8,128)S(1)} %get-tuple-element.92), channel_id=1, source_target_pairs={{0,1},{1,0},{2,3},{3,2},{4,5},{5,4},{6,7},{7,6},{8,9},{9,8},{10,11... | collective-permute-start | bytes 61448 | tf_op jit(solution)/shard_map/ppermute | solution.py:27
  65.9 4.8 %collective-permute-start.31 = (f32[5,8,128]{2,1,0:T(8,128)S(1)}, f32[5,8,128]{2,1,0:T(8,128)S(1)}, u32[]{:S(2)}, u32[]{:S(2)}) collective-permute-start(f32[5,8,128]{2,1,0:T(8,128)S(1)} %get-tuple-element.93), channel_id=1, source_target_pairs={{0,7},{1,2},{2,1},{3,4},{4,3},{5,6},{6,5},{7,0},{8,15},{9,10},{10,... | collective-permute-start | bytes 61448 | tf_op jit(solution)/shard_map/ppermute | solution.py:27

commit v4 on v3

--- a/solution.py
+++ b/solution.py
@@ -298,7 +298,7 @@
 
 
 def finish_kernel(
-    scale, index, skip, halves, state_ref, base_ref, xa_ref, xb_ref, ya_ref, yb_ref, *outs
+    scale, index, skip, halves, state_ref, base_ref, xa_ref, xb_ref, yb_ref, ya_ref, *outs
 ):
     outs = outs[skip:]
     out_ref = outs[0]
@@ -457,7 +457,7 @@
 def exchange(faces):
     xb, xa = exchange_x(faces[:2])
     yb, ya = exchange_y(faces[2:])
-    return xa, xb, ya, yb
+    return xa, xb, yb, ya
 
 
 def section(states, index, w, received, scale, extras, with_faces, load=None, after=()):
@@ -776,7 +776,7 @@
         columns // LANES,
     )
     yb, ya = exchange_y(y_faces)
-    adj_old = reverse_step(old_states[0], adj_proj, (xa, xb, ya, yb))
+    adj_old = reverse_step(old_states[0], adj_proj, (xa, xb, yb, ya))
     return (adj_new.reshape(adj_final.shape), adj_old.reshape(adj_final.shape))
 
 

time: 71.8 us -> 70.6 us (0.983)
  starting transfers between devices: 42.8 us -> 37.1 us
  waiting for transfers between devices: 12.2 us -> 16.9 us
    ppermute x24, starting transfers between devices: 35.6 us -> 29.1 us  [swapped(): return lax.ppermute(value, axis, pairs)]
    ppermute x24, waiting for transfers between devices: 3.71 us -> 8.66 us  [swapped(): return lax.ppermute(value, axis, pairs)]
    ppermute x6, starting transfers between devices: 7.11 us -> 7.85 us  [send_chips(): mine[d] = lax.ppermute(values[d], ring, pairs)]
  transfers between devices with their start and end apart: 32 -> 32, of which waited for: 11 -> 13; matrix products, arithmetic and copies ran while one was open for 0% -> 0% of each run, Pallas kernels for 14% -> 14%
where the time goes in v4:
time: 70.6 us; the launch traced here: 70.4 us
  starting transfers between devices  37.1 us (53%)
  waiting for transfers between devices  16.9 us (24%)
  Pallas kernels  15.5 us (22%)
  between operations  0.86 us (1%)
    ppermute x24, starting transfers between devices, swapped(): return lax.ppermute(value, axis, pairs)  29.1 us
    ppermute x24, waiting for transfers between devices, swapped(): return lax.ppermute(value, axis, pairs)  8.66 us
    ppermute x6, waiting for transfers between devices, send_chips(): mine[d] = lax.ppermute(values[d], ring, pairs)  8.19 us
    ppermute x6, starting transfers between devices, send_chips(): mine[d] = lax.ppermute(values[d], ring, pairs)  7.85 us
    pallas_call x6, Pallas kernels, section(): pl.pallas_call(functools.partial(local_kernel, scale, index, factors, hal...  6.11 us
    pallas_call x2, Pallas kernels, project(): pl.pallas_call(functools.partial(project_kernel, tiles, len(sources), out...  4.41 us
    pallas_call x6, Pallas kernels, section(): pl.pallas_call(functools.partial(finish_kernel, scale, index, len(after),...  1.92 us
  transfers between devices with their start and end apart: 32, of which 13 were waited for; matrix products, arithmetic and copies ran while one was open for 0% of the time, Pallas kernels for 14%

profile of v4, /device:TPU:0, one launch (start us, length us, event | category | flops | bytes accessed | tf_op | source)
XLA Modules:
  0.0 70.4 jit_solution(6842521398840423244)
XLA Ops:
  0.7 1.3 %faces.1 = (f32[5,64,256]{2,1,0:T(8,128)S(1)}, f32[3,5,64,256]{3,2,1,0:T(8,128)S(1)}, f32[5,16,256]{2,1,0:T(8,128)S(1)}, f32[5,16,256]{2,1,0:T(8,128)S(1)}, f32[...) custom-call(f32[1,5,64,256]{3,2,1,0:T(8,128)} %w_hbm.1, f32[1,3,5,64,256]{4,3,2,1,0:T(8,128)} %state_hbm.1), custom_call_target="tpu_custom_call" | custom-call | tf_op jit(solution)/shard_map/faces/pallas_call | solution.py:391
  2.0 3.1 %collective-permute-start = (f32[5,16,256]{2,1,0:T(8,128)S(1)}, f32[5,16,256]{2,1,0:T(8,128)S(1)}, u32[]{:S(2)}, u32[]{:S(2)}) collective-permute-start(f32[5,16,256]{2,1,0:T(8,128)S(1)} %get-tuple-element.50), channel_id=1, source_target_pairs={{0,8},{8,0},{16,24},{24,16},{1,9},{9,1},{17,25},{25,17},{2,10},{10... | collective-permute-start | bytes 245768 | tf_op jit(solution)/shard_map/ppermute | solution.py:27
  5.1 2.5 %collective-permute-start.1 = (f32[5,16,256]{2,1,0:T(8,128)S(1)}, f32[5,16,256]{2,1,0:T(8,128)S(1)}, u32[]{:S(2)}, u32[]{:S(2)}) collective-permute-start(f32[5,16,256]{2,1,0:T(8,128)S(1)} %get-tuple-element.51), channel_id=1, source_target_pairs={{0,24},{8,16},{16,8},{24,0},{1,25},{9,17},{17,9},{25,1},{2,26},{10... | collective-permute-start | bytes 245768 | tf_op jit(solution)/shard_map/ppermute | solution.py:27
  7.6 1.3 %collective-permute-start.2 = (f32[5,8,128]{2,1,0:T(8,128)S(1)}, f32[5,8,128]{2,1,0:T(8,128)S(1)}, u32[]{:S(2)}, u32[]{:S(2)}) collective-permute-start(f32[5,8,128]{2,1,0:T(8,128)S(1)} %get-tuple-element.52), channel_id=1, source_target_pairs={{0,7},{1,2},{2,1},{3,4},{4,3},{5,6},{6,5},{7,0},{8,15},{9,10},{10,... | collective-permute-start | bytes 61448 | tf_op jit(solution)/shard_map/ppermute | solution.py:27
  8.9 0.3 collective-permute-start.3
  9.2 0.7 %local_part.6.base_ref = f32[5,64,256]{2,1,0:T(8,128)S(1)} custom-call(f32[3,5,64,256]{3,2,1,0:T(8,128)S(1)} %get-tuple-element.48.refs_0_.state_ref, f32[5,64,256]{2,1,0:T(8,128)S(1)} %get-tuple-element.49.refs_1_.refs_2_), custom_call_target="tpu_custom_call" | custom-call | flops 6553600 | bytes 983040 | tf_op jit(solution)/shard_map/local_part/pallas_call | solution.py:480
  9.9 1.8 %collective-permute-done.2.yb_ref = f32[5,8,128]{2,1,0:T(8,128)S(1)} collective-permute-done((f32[5,8,128]{2,1,0:T(8,128)S(1)}, f32[5,8,128]{2,1,0:T(8,128)S(1)}, u32[]{:S(2)}, u32[]{:S(2)}) %collective-permute-start.2) | collective-permute-done | bytes 20512 | tf_op jit(solution)/shard_map/ppermute | solution.py:27
  11.9 0.7 collective-permute-start.4
  12.6 2.4 %collective-permute-start.5 = (f32[5,16,256]{2,1,0:T(8,128)S(1)}, f32[5,16,256]{2,1,0:T(8,128)S(1)}, u32[]{:S(2)}, u32[]{:S(2)}) collective-permute-start(f32[5,16,256]{2,1,0:T(8,128)S(1)} %get-tuple-element.56), channel_id=1, source_target_pairs={{0,24},{8,16},{16,8},{24,0},{1,25},{9,17},{17,9},{25,1},{2,26},{10... | collective-permute-start | bytes 245768 | tf_op jit(solution)/shard_map/ppermute | solution.py:27
  15.1 1.6 %collective-permute-start.7 = (f32[5,8,128]{2,1,0:T(8,128)S(1)}, f32[5,8,128]{2,1,0:T(8,128)S(1)}, u32[]{:S(2)}, u32[]{:S(2)}) collective-permute-start(f32[5,8,128]{2,1,0:T(8,128)S(1)} %get-tuple-element.58), channel_id=1, source_target_pairs={{0,1},{1,0},{2,3},{3,2},{4,5},{5,4},{6,7},{7,6},{8,9},{9,8},{10,11... | collective-permute-start | bytes 61448 | tf_op jit(solution)/shard_map/ppermute | solution.py:27
  16.7 0.6 prepare.1
  17.4 0.7 %local_part.7.base_ref = f32[5,64,256]{2,1,0:T(8,128)S(1)} custom-call(f32[3,5,64,256]{3,2,1,0:T(8,128)S(1)} %get-tuple-element.48.refs_0_.state_ref, f32[5,64,256]{2,1,0:T(8,128)S(1)} %get-tuple-element.54.refs_1_.after_ref.refs_3_), custom_call_target="tpu_custom_call" | custom-call | flops 6553600 | bytes 983040 | tf_op jit(solution)/shard_map/local_part/pallas_call | solution.py:480
  18.1 1.1 %collective-permute-done.6.yb_ref = f32[5,8,128]{2,1,0:T(8,128)S(1)} collective-permute-done((f32[5,8,128]{2,1,0:T(8,128)S(1)}, f32[5,8,128]{2,1,0:T(8,128)S(1)}, u32[]{:S(2)}, u32[]{:S(2)}) %collective-permute-start.6) | collective-permute-done | bytes 20512 | tf_op jit(solution)/shard_map/ppermute | solution.py:27
  19.4 0.3 collective-permute-start.8
  19.7 2.0 %collective-permute-start.9 = (f32[5,16,256]{2,1,0:T(8,128)S(1)}, f32[5,16,256]{2,1,0:T(8,128)S(1)}, u32[]{:S(2)}, u32[]{:S(2)}) collective-permute-start(f32[5,16,256]{2,1,0:T(8,128)S(1)} %get-tuple-element.63), channel_id=1, source_target_pairs={{0,24},{8,16},{16,8},{24,0},{1,25},{9,17},{17,9},{25,1},{2,26},{10... | collective-permute-start | bytes 245768 | tf_op jit(solution)/shard_map/ppermute | solution.py:27
  21.9 1.4 %collective-permute-start.11 = (f32[5,8,128]{2,1,0:T(8,128)S(1)}, f32[5,8,128]{2,1,0:T(8,128)S(1)}, u32[]{:S(2)}, u32[]{:S(2)}) collective-permute-start(f32[5,8,128]{2,1,0:T(8,128)S(1)} %get-tuple-element.65), channel_id=1, source_target_pairs={{0,1},{1,0},{2,3},{3,2},{4,5},{5,4},{6,7},{7,6},{8,9},{9,8},{10,11... | collective-permute-start | bytes 61448 | tf_op jit(solution)/shard_map/ppermute | solution.py:27
  23.3 2.5 %local_part.8 = (f32[5,64,256]{2,1,0:T(8,128)S(1)}, f32[64,32,512]{2,1,0:T(8,128)S(1)}) custom-call(f32[3,5,64,256]{3,2,1,0:T(8,128)S(1)} %get-tuple-element.48.refs_0_.state_ref, f32[5,64,256]{2,1,0:T(8,128)S(1)} %get-tuple-element.60.refs_1_, f32[5,64,256]{2,1,0:T(8,128)S(1)} %get-tuple-element.49.refs_1_.refs_2_, ...), custom_call_target="tpu_custom_call" | custom-call | flops 6553600 | bytes 983040 | tf_op jit(solution)/shard_map/local_part/pallas_call | solution.py:480
  26.1 2.2 %project.2 = (f32[2,168,128]{2,1,0:T(8,128)S(1)}, f32[2,168,128]{2,1,0:T(8,128)S(1)}, f32[2,168,128]{2,1,0:T(8,128)S(1)}, f32[2,168,128]{2,1,0:T(8,128)S(1)}, f32[64,32,512]{2,1,0:T(8,128)S(1)}) custom-call(f32[5,64,256]{2,1,0:T(8,128)S(1)} %finish.8.refs_0_, f32[64,32,512]{2,1,0:T(8,128)S(1)} %get-tuple-element.66.refs_1_, ...), custom_call_target="tpu_custom_call" | custom-call | flops 4000000000 | bytes 20971520 | tf_op jit(solution)/shard_map/project/pallas_call | solution.py:603
  28.4 1.7 %collective-permute-start.16 = (f32[2,168,128]{2,1,0:T(8,128)S(1)}, f32[2,168,128]{2,1,0:T(8,128)S(1)}, u32[]{:S(2)}, u32[]{:S(2)}) collective-permute-start(f32[2,168,128]{2,1,0:T(8,128)S(1)} %get-tuple-element.75), channel_id=1, source_target_pairs={{0,2},{1,3},{2,0},{3,1},{4,6},{5,7},{6,4},{7,5},{8,10},{9,11},{10,... | collective-permute-start | bytes 516104 | tf_op jit(solution)/shard_map/ppermute | solution.py:691
  30.0 1.4 %collective-permute-start.17 = (f32[2,168,128]{2,1,0:T(8,128)S(1)}, f32[2,168,128]{2,1,0:T(8,128)S(1)}, u32[]{:S(2)}, u32[]{:S(2)}) collective-permute-start(f32[2,168,128]{2,1,0:T(8,128)S(1)} %get-tuple-element.76), channel_id=1, source_target_pairs={{0,4},{1,5},{2,6},{3,7},{4,0},{5,1},{6,2},{7,3},{8,12},{9,13},{10,... | collective-permute-start | bytes 516104 | tf_op jit(solution)/shard_map/ppermute | solution.py:691
  31.5 0.5 collective-permute-start.18
  31.9 2.2 %project.3 = (f32[2,168,128]{2,1,0:T(8,128)S(1)}, f32[2,168,128]{2,1,0:T(8,128)S(1)}, f32[2,168,128]{2,1,0:T(8,128)S(1)}, f32[2,168,128]{2,1,0:T(8,128)S(1)}, f32[5,64,256]{2,1,0:T(8,128)}) custom-call(f32[5,64,256]{2,1,0:T(8,128)S(1)} %finish.8.refs_0_, f32[64,32,512]{2,1,0:T(8,128)S(1)} %get-tuple-element.68.refs_1_, ...), custom_call_target="tpu_custom_call" | custom-call | flops 4000000000 | bytes 20971520 | tf_op jit(solution)/shard_map/project/pallas_call | solution.py:603
  34.1 1.7 %collective-permute-start.12 = (f32[2,168,128]{2,1,0:T(8,128)S(1)}, f32[2,168,128]{2,1,0:T(8,128)S(1)}, u32[]{:S(2)}, u32[]{:S(2)}) collective-permute-start(f32[2,168,128]{2,1,0:T(8,128)S(1)} %get-tuple-element.71), channel_id=1, source_target_pairs={{0,2},{1,3},{2,0},{3,1},{4,6},{5,7},{6,4},{7,5},{8,10},{9,11},{10,... | collective-permute-start | bytes 516104 | tf_op jit(solution)/shard_map/ppermute | solution.py:691
  35.8 1.4 %collective-permute-start.13 = (f32[2,168,128]{2,1,0:T(8,128)S(1)}, f32[2,168,128]{2,1,0:T(8,128)S(1)}, u32[]{:S(2)}, u32[]{:S(2)}) collective-permute-start(f32[2,168,128]{2,1,0:T(8,128)S(1)} %get-tuple-element.72), channel_id=1, source_target_pairs={{0,4},{1,5},{2,6},{3,7},{4,0},{5,1},{6,2},{7,3},{8,12},{9,13},{10,... | collective-permute-start | bytes 516104 | tf_op jit(solution)/shard_map/ppermute | solution.py:691
  37.2 1.2 %collective-permute-start.14 = (f32[2,168,128]{2,1,0:T(8,128)S(1)}, f32[2,168,128]{2,1,0:T(8,128)S(1)}, u32[]{:S(2)}, u32[]{:S(2)}) collective-permute-start(f32[2,168,128]{2,1,0:T(8,128)S(1)} %get-tuple-element.73), channel_id=1, source_target_pairs={{0,6},{1,7},{2,4},{3,5},{4,2},{5,3},{6,0},{7,1},{8,14},{9,15},{10,... | collective-permute-start | bytes 516104 | tf_op jit(solution)/shard_map/ppermute | solution.py:691
  38.5 2.4 %collective-permute-done.18.refs_3_ = f32[2,168,128]{2,1,0:T(8,128)S(1)} collective-permute-done((f32[2,168,128]{2,1,0:T(8,128)S(1)}, f32[2,168,128]{2,1,0:T(8,128)S(1)}, u32[]{:S(2)}, u32[]{:S(2)}) %collective-permute-start.18) | collective-permute-done | bytes 172064 | tf_op jit(solution)/shard_map/ppermute | solution.py:691
  41.0 2.2 %collective-permute-done.12.refs_1_ = f32[2,168,128]{2,1,0:T(8,128)S(1)} collective-permute-done((f32[2,168,128]{2,1,0:T(8,128)S(1)}, f32[2,168,128]{2,1,0:T(8,128)S(1)}, u32[]{:S(2)}, u32[]{:S(2)}) %collective-permute-start.12) | collective-permute-done | bytes 172064 | tf_op jit(solution)/shard_map/ppermute | solution.py:691
  43.2 1.5 %collective-permute-done.13.refs_2_ = f32[2,168,128]{2,1,0:T(8,128)S(1)} collective-permute-done((f32[2,168,128]{2,1,0:T(8,128)S(1)}, f32[2,168,128]{2,1,0:T(8,128)S(1)}, u32[]{:S(2)}, u32[]{:S(2)}) %collective-permute-start.13) | collective-permute-done | bytes 172064 | tf_op jit(solution)/shard_map/ppermute | solution.py:691
  44.7 2.1 %collective-permute-done.14.refs_3_ = f32[2,168,128]{2,1,0:T(8,128)S(1)} collective-permute-done((f32[2,168,128]{2,1,0:T(8,128)S(1)}, f32[2,168,128]{2,1,0:T(8,128)S(1)}, u32[]{:S(2)}, u32[]{:S(2)}) %collective-permute-start.14) | collective-permute-done | bytes 172064 | tf_op jit(solution)/shard_map/ppermute | solution.py:691
  46.9 0.5 receive.2
  47.5 1.1 %collective-permute-start.20 = (f32[5,16,256]{2,1,0:T(8,128)S(1)}, f32[5,16,256]{2,1,0:T(8,128)S(1)}, u32[]{:S(2)}, u32[]{:S(2)}) collective-permute-start(f32[5,16,256]{2,1,0:T(8,128)S(1)} %get-tuple-element.80), channel_id=1, source_target_pairs={{0,8},{8,0},{16,24},{24,16},{1,9},{9,1},{17,25},{25,17},{2,10},{10... | collective-permute-start | bytes 245768 | tf_op jit(solution)/shard_map/ppermute | solution.py:27
  48.6 1.5 %collective-permute-start.21 = (f32[5,16,256]{2,1,0:T(8,128)S(1)}, f32[5,16,256]{2,1,0:T(8,128)S(1)}, u32[]{:S(2)}, u32[]{:S(2)}) collective-permute-start(f32[5,16,256]{2,1,0:T(8,128)S(1)} %get-tuple-element.81), channel_id=1, source_target_pairs={{0,24},{8,16},{16,8},{24,0},{1,25},{9,17},{17,9},{25,1},{2,26},{10... | collective-permute-start | bytes 245768 | tf_op jit(solution)/shard_map/ppermute | solution.py:27
  50.1 0.6 receive.3
  50.7 1.3 %collective-permute-start.22 = (f32[5,8,128]{2,1,0:T(8,128)S(1)}, f32[5,8,128]{2,1,0:T(8,128)S(1)}, u32[]{:S(2)}, u32[]{:S(2)}) collective-permute-start(f32[5,8,128]{2,1,0:T(8,128)S(1)} %get-tuple-element.82), channel_id=1, source_target_pairs={{0,7},{1,2},{2,1},{3,4},{4,3},{5,6},{6,5},{7,0},{8,15},{9,10},{10,... | collective-permute-start | bytes 61448 | tf_op jit(solution)/shard_map/ppermute | solution.py:27
  51.9 0.6 collective-permute-start.23
  52.5 0.7 %local_part.9.base_ref = f32[5,64,256]{2,1,0:T(8,128)S(1)} custom-call(f32[3,5,64,256]{3,2,1,0:T(8,128)S(1)} %bitcast.4, f32[5,64,256]{2,1,0:T(8,128)S(1)} %get-tuple-element.79.refs_1_.refs_2_), custom_call_target="tpu_custom_call" | custom-call | flops 6553600 | bytes 983040 | tf_op jit(solution)/shard_map/local_part/pallas_call | solution.py:480
  53.2 1.6 %collective-permute-done.22.yb_ref = f32[5,8,128]{2,1,0:T(8,128)S(1)} collective-permute-done((f32[5,8,128]{2,1,0:T(8,128)S(1)}, f32[5,8,128]{2,1,0:T(8,128)S(1)}, u32[]{:S(2)}, u32[]{:S(2)}) %collective-permute-start.22) | collective-permute-done | bytes 20512 | tf_op jit(solution)/shard_map/ppermute | solution.py:27
  55.3 0.9 %collective-permute-start.24 = (f32[5,16,256]{2,1,0:T(8,128)S(1)}, f32[5,16,256]{2,1,0:T(8,128)S(1)}, u32[]{:S(2)}, u32[]{:S(2)}) collective-permute-start(f32[5,16,256]{2,1,0:T(8,128)S(1)} %get-tuple-element.85), channel_id=1, source_target_pairs={{0,8},{8,0},{16,24},{24,16},{1,9},{9,1},{17,25},{25,17},{2,10},{10... | collective-permute-start | bytes 245768 | tf_op jit(solution)/shard_map/ppermute | solution.py:27
  56.2 1.9 %collective-permute-start.25 = (f32[5,16,256]{2,1,0:T(8,128)S(1)}, f32[5,16,256]{2,1,0:T(8,128)S(1)}, u32[]{:S(2)}, u32[]{:S(2)}) collective-permute-start(f32[5,16,256]{2,1,0:T(8,128)S(1)} %get-tuple-element.86), channel_id=1, source_target_pairs={{0,24},{8,16},{16,8},{24,0},{1,25},{9,17},{17,9},{25,1},{2,26},{10... | collective-permute-start | bytes 245768 | tf_op jit(solution)/shard_map/ppermute | solution.py:27
  58.2 1.3 %collective-permute-start.27 = (f32[5,8,128]{2,1,0:T(8,128)S(1)}, f32[5,8,128]{2,1,0:T(8,128)S(1)}, u32[]{:S(2)}, u32[]{:S(2)}) collective-permute-start(f32[5,8,128]{2,1,0:T(8,128)S(1)} %get-tuple-element.88), channel_id=1, source_target_pairs={{0,1},{1,0},{2,3},{3,2},{4,5},{5,4},{6,7},{7,6},{8,9},{9,8},{10,11... | collective-permute-start | bytes 61448 | tf_op jit(solution)/shard_map/ppermute | solution.py:27
  59.5 0.7 %local_part.10.base_ref = f32[5,64,256]{2,1,0:T(8,128)S(1)} custom-call(f32[3,5,64,256]{3,2,1,0:T(8,128)S(1)} %bitcast.6, f32[5,64,256]{2,1,0:T(8,128)S(1)} %get-tuple-element.84.refs_1_.refs_3_), custom_call_target="tpu_custom_call" | custom-call | flops 6553600 | bytes 983040 | tf_op jit(solution)/shard_map/local_part/pallas_call | solution.py:480
  60.3 1.9 %collective-permute-done.26.yb_ref = f32[5,8,128]{2,1,0:T(8,128)S(1)} collective-permute-done((f32[5,8,128]{2,1,0:T(8,128)S(1)}, f32[5,8,128]{2,1,0:T(8,128)S(1)}, u32[]{:S(2)}, u32[]{:S(2)}) %collective-permute-start.26) | collective-permute-done | bytes 20512 | tf_op jit(solution)/shard_map/ppermute | solution.py:27
  62.6 0.4 collective-permute-start.28
  63.0 2.4 %collective-permute-start.29 = (f32[5,16,256]{2,1,0:T(8,128)S(1)}, f32[5,16,256]{2,1,0:T(8,128)S(1)}, u32[]{:S(2)}, u32[]{:S(2)}) collective-permute-start(f32[5,16,256]{2,1,0:T(8,128)S(1)} %get-tuple-element.91), channel_id=1, source_target_pairs={{0,24},{8,16},{16,8},{24,0},{1,25},{9,17},{17,9},{25,1},{2,26},{10... | collective-permute-start | bytes 245768 | tf_op jit(solution)/shard_map/ppermute | solution.py:27
  65.4 1.7 %collective-permute-start.31 = (f32[5,8,128]{2,1,0:T(8,128)S(1)}, f32[5,8,128]{2,1,0:T(8,128)S(1)}, u32[]{:S(2)}, u32[]{:S(2)}) collective-permute-start(f32[5,8,128]{2,1,0:T(8,128)S(1)} %get-tuple-element.93), channel_id=1, source_target_pairs={{0,1},{1,0},{2,3},{3,2},{4,5},{5,4},{6,7},{7,6},{8,9},{9,8},{10,11... | collective-permute-start | bytes 61448 | tf_op jit(solution)/shard_map/ppermute | solution.py:27
  67.1 0.8 %local_part.11.base_ref = f32[5,64,256]{2,1,0:T(8,128)S(1)} custom-call(f32[3,5,64,256]{3,2,1,0:T(8,128)S(1)} %bitcast.8, f32[5,64,256]{2,1,0:T(8,128)S(1)} %get-tuple-element.89.refs_1_, f32[5,64,256]{2,1,0:T(8,128)S(1)} %get-tuple-element.79.refs_1_.refs_2_, f32[5,64,256]{2,1,0:T(8,128)S(1)} %get-tuple-element.84.refs_1_.refs_3_), custom_call_target="tpu_custom_call" | custom-call | flops 6553600 | bytes 983040 | tf_op jit(solution)/shard_map/local_part/pallas_call | solution.py:480
  67.9 1.6 %collective-permute-done.30.yb_ref = f32[5,8,128]{2,1,0:T(8,128)S(1)} collective-permute-done((f32[5,8,128]{2,1,0:T(8,128)S(1)}, f32[5,8,128]{2,1,0:T(8,128)S(1)}, u32[]{:S(2)}, u32[]{:S(2)}) %collective-permute-start.30) | collective-permute-done | bytes 20512 | tf_op jit(solution)/shard_map/ppermute | solution.py:27
  69.5 0.9 %finish.11 = f32[5,64,256]{2,1,0:T(8,128)} custom-call(f32[3,5,64,256]{3,2,1,0:T(8,128)S(1)} %bitcast.9, f32[5,64,256]{2,1,0:T(8,128)S(1)} %local_part.11.base_ref, f32[5,16,256]{2,1,0:T(8,128)S(1)} %collective-permute-done.28.xa_ref, f32[5,16,256]{2,1,0:T(8,128)S(1)} %collective-permute-done.29.xb_ref, f32[5,8,128]{2,1,0:T(8,128)S(1)} %collective-permute-done.30.yb_ref, ...), custom_call_target="tpu_custom_call" | custom-call | tf_op jit(solution)/shard_map/finish/pallas_call | solution.py:493
  (50 shorter events, 2.4 us)
Async XLA Ops:
  0.6 16.1 %copy-start.2 = (s32[1,512]{1,0:T(1,128)S(1)}, s32[1,512]{1,0:T(1,128)}, u32[]{:S(2)}) copy-start(s32[1,512]{1,0:T(1,128)} %local_ref.1) | copy-start | bytes 6148
  0.6 16.1 %copy-start.1 = (s32[1,512,1]{1,2,0:T(1,128)S(1)}, s32[1,512,1]{1,2,0:T(1,128)}, u32[]{:S(2)}) copy-start(s32[1,512,1]{1,2,0:T(1,128)} %param.9) | copy-start | bytes 6148
  2.0 9.7 %collective-permute-start = (f32[5,16,256]{2,1,0:T(8,128)S(1)}, f32[5,16,256]{2,1,0:T(8,128)S(1)}, u32[]{:S(2)}, u32[]{:S(2)}) collective-permute-start(f32[5,16,256]{2,1,0:T(8,128)S(1)} %get-tuple-element.50), channel_id=1, source_target_pairs={{0,8},{8,0},{16,24},{24,16},{1,9},{9,1},{17,25},{25,17},{2,10},{10... | collective-permute-start | bytes 245768 | tf_op jit(solution)/shard_map/ppermute | solution.py:27
  5.1 6.6 %collective-permute-start.1 = (f32[5,16,256]{2,1,0:T(8,128)S(1)}, f32[5,16,256]{2,1,0:T(8,128)S(1)}, u32[]{:S(2)}, u32[]{:S(2)}) collective-permute-start(f32[5,16,256]{2,1,0:T(8,128)S(1)} %get-tuple-element.51), channel_id=1, source_target_pairs={{0,24},{8,16},{16,8},{24,0},{1,25},{9,17},{17,9},{25,1},{2,26},{10... | collective-permute-start | bytes 245768 | tf_op jit(solution)/shard_map/ppermute | solution.py:27
  7.6 4.1 %collective-permute-start.2 = (f32[5,8,128]{2,1,0:T(8,128)S(1)}, f32[5,8,128]{2,1,0:T(8,128)S(1)}, u32[]{:S(2)}, u32[]{:S(2)}) collective-permute-start(f32[5,8,128]{2,1,0:T(8,128)S(1)} %get-tuple-element.52), channel_id=1, source_target_pairs={{0,7},{1,2},{2,1},{3,4},{4,3},{5,6},{6,5},{7,0},{8,15},{9,10},{10,... | collective-permute-start | bytes 61448 | tf_op jit(solution)/shard_map/ppermute | solution.py:27
  8.9 2.8 %collective-permute-start.3 = (f32[5,8,128]{2,1,0:T(8,128)S(1)}, f32[5,8,128]{2,1,0:T(8,128)S(1)}, u32[]{:S(2)}, u32[]{:S(2)}) collective-permute-start(f32[5,8,128]{2,1,0:T(8,128)S(1)} %get-tuple-element.53), channel_id=1, source_target_pairs={{0,1},{1,0},{2,3},{3,2},{4,5},{5,4},{6,7},{7,6},{8,9},{9,8},{10,11... | collective-permute-start | bytes 61448 | tf_op jit(solution)/shard_map/ppermute | solution.py:27
  11.9 7.3 %collective-permute-start.4 = (f32[5,16,256]{2,1,0:T(8,128)S(1)}, f32[5,16,256]{2,1,0:T(8,128)S(1)}, u32[]{:S(2)}, u32[]{:S(2)}) collective-permute-start(f32[5,16,256]{2,1,0:T(8,128)S(1)} %get-tuple-element.55), channel_id=1, source_target_pairs={{0,8},{8,0},{16,24},{24,16},{1,9},{9,1},{17,25},{25,17},{2,10},{10... | collective-permute-start | bytes 245768 | tf_op jit(solution)/shard_map/ppermute | solution.py:27
  12.6 6.5 %collective-permute-start.5 = (f32[5,16,256]{2,1,0:T(8,128)S(1)}, f32[5,16,256]{2,1,0:T(8,128)S(1)}, u32[]{:S(2)}, u32[]{:S(2)}) collective-permute-start(f32[5,16,256]{2,1,0:T(8,128)S(1)} %get-tuple-element.56), channel_id=1, source_target_pairs={{0,24},{8,16},{16,8},{24,0},{1,25},{9,17},{17,9},{25,1},{2,26},{10... | collective-permute-start | bytes 245768 | tf_op jit(solution)/shard_map/ppermute | solution.py:27
  15.1 4.1 %collective-permute-start.6 = (f32[5,8,128]{2,1,0:T(8,128)S(1)}, f32[5,8,128]{2,1,0:T(8,128)S(1)}, u32[]{:S(2)}, u32[]{:S(2)}) collective-permute-start(f32[5,8,128]{2,1,0:T(8,128)S(1)} %get-tuple-element.57), channel_id=1, source_target_pairs={{0,7},{1,2},{2,1},{3,4},{4,3},{5,6},{6,5},{7,0},{8,15},{9,10},{10,... | collective-permute-start | bytes 61448 | tf_op jit(solution)/shard_map/ppermute | solution.py:27
  15.1 4.1 %collective-permute-start.7 = (f32[5,8,128]{2,1,0:T(8,128)S(1)}, f32[5,8,128]{2,1,0:T(8,128)S(1)}, u32[]{:S(2)}, u32[]{:S(2)}) collective-permute-start(f32[5,8,128]{2,1,0:T(8,128)S(1)} %get-tuple-element.58), channel_id=1, source_target_pairs={{0,1},{1,0},{2,3},{3,2},{4,5},{5,4},{6,7},{7,6},{8,9},{9,8},{10,11... | collective-permute-start | bytes 61448 | tf_op jit(solution)/shard_map/ppermute | solution.py:27
  19.4 6.4 %collective-permute-start.8 = (f32[5,16,256]{2,1,0:T(8,128)S(1)}, f32[5,16,256]{2,1,0:T(8,128)S(1)}, u32[]{:S(2)}, u32[]{:S(2)}) collective-permute-start(f32[5,16,256]{2,1,0:T(8,128)S(1)} %get-tuple-element.62), channel_id=1, source_target_pairs={{0,8},{8,0},{16,24},{24,16},{1,9},{9,1},{17,25},{25,17},{2,10},{10... | collective-permute-start | bytes 245768 | tf_op jit(solution)/shard_map/ppermute | solution.py:27
  19.7 6.3 %collective-permute-start.9 = (f32[5,16,256]{2,1,0:T(8,128)S(1)}, f32[5,16,256]{2,1,0:T(8,128)S(1)}, u32[]{:S(2)}, u32[]{:S(2)}) collective-permute-start(f32[5,16,256]{2,1,0:T(8,128)S(1)} %get-tuple-element.63), channel_id=1, source_target_pairs={{0,24},{8,16},{16,8},{24,0},{1,25},{9,17},{17,9},{25,1},{2,26},{10... | collective-permute-start | bytes 245768 | tf_op jit(solution)/shard_map/ppermute | solution.py:27
  21.7 4.1 %collective-permute-start.10 = (f32[5,8,128]{2,1,0:T(8,128)S(1)}, f32[5,8,128]{2,1,0:T(8,128)S(1)}, u32[]{:S(2)}, u32[]{:S(2)}) collective-permute-start(f32[5,8,128]{2,1,0:T(8,128)S(1)} %get-tuple-element.64), channel_id=1, source_target_pairs={{0,7},{1,2},{2,1},{3,4},{4,3},{5,6},{6,5},{7,0},{8,15},{9,10},{10,... | collective-permute-start | bytes 61448 | tf_op jit(solution)/shard_map/ppermute | solution.py:27
  21.9 3.9 %collective-permute-start.11 = (f32[5,8,128]{2,1,0:T(8,128)S(1)}, f32[5,8,128]{2,1,0:T(8,128)S(1)}, u32[]{:S(2)}, u32[]{:S(2)}) collective-permute-start(f32[5,8,128]{2,1,0:T(8,128)S(1)} %get-tuple-element.65), channel_id=1, source_target_pairs={{0,1},{1,0},{2,3},{3,2},{4,5},{5,4},{6,7},{7,6},{8,9},{9,8},{10,11... | collective-permute-start | bytes 61448 | tf_op jit(solution)/shard_map/ppermute | solution.py:27
  28.4 8.9 %collective-permute-start.16 = (f32[2,168,128]{2,1,0:T(8,128)S(1)}, f32[2,168,128]{2,1,0:T(8,128)S(1)}, u32[]{:S(2)}, u32[]{:S(2)}) collective-permute-start(f32[2,168,128]{2,1,0:T(8,128)S(1)} %get-tuple-element.75), channel_id=1, source_target_pairs={{0,2},{1,3},{2,0},{3,1},{4,6},{5,7},{6,4},{7,5},{8,10},{9,11},{10,... | collective-permute-start | bytes 516104 | tf_op jit(solution)/shard_map/ppermute | solution.py:691
  30.0 8.4 %collective-permute-start.17 = (f32[2,168,128]{2,1,0:T(8,128)S(1)}, f32[2,168,128]{2,1,0:T(8,128)S(1)}, u32[]{:S(2)}, u32[]{:S(2)}) collective-permute-start(f32[2,168,128]{2,1,0:T(8,128)S(1)} %get-tuple-element.76), channel_id=1, source_target_pairs={{0,4},{1,5},{2,6},{3,7},{4,0},{5,1},{6,2},{7,3},{8,12},{9,13},{10,... | collective-permute-start | bytes 516104 | tf_op jit(solution)/shard_map/ppermute | solution.py:691
  31.5 9.4 %collective-permute-start.18 = (f32[2,168,128]{2,1,0:T(8,128)S(1)}, f32[2,168,128]{2,1,0:T(8,128)S(1)}, u32[]{:S(2)}, u32[]{:S(2)}) collective-permute-start(f32[2,168,128]{2,1,0:T(8,128)S(1)} %get-tuple-element.77), channel_id=1, source_target_pairs={{0,6},{1,7},{2,4},{3,5},{4,2},{5,3},{6,0},{7,1},{8,14},{9,15},{10,... | collective-permute-start | bytes 516104 | tf_op jit(solution)/shard_map/ppermute | solution.py:691
  34.1 9.0 %collective-permute-start.12 = (f32[2,168,128]{2,1,0:T(8,128)S(1)}, f32[2,168,128]{2,1,0:T(8,128)S(1)}, u32[]{:S(2)}, u32[]{:S(2)}) collective-permute-start(f32[2,168,128]{2,1,0:T(8,128)S(1)} %get-tuple-element.71), channel_id=1, source_target_pairs={{0,2},{1,3},{2,0},{3,1},{4,6},{5,7},{6,4},{7,5},{8,10},{9,11},{10,... | collective-permute-start | bytes 516104 | tf_op jit(solution)/shard_map/ppermute | solution.py:691
  35.8 8.9 %collective-permute-start.13 = (f32[2,168,128]{2,1,0:T(8,128)S(1)}, f32[2,168,128]{2,1,0:T(8,128)S(1)}, u32[]{:S(2)}, u32[]{:S(2)}) collective-permute-start(f32[2,168,128]{2,1,0:T(8,128)S(1)} %get-tuple-element.72), channel_id=1, source_target_pairs={{0,4},{1,5},{2,6},{3,7},{4,0},{5,1},{6,2},{7,3},{8,12},{9,13},{10,... | collective-permute-start | bytes 516104 | tf_op jit(solution)/shard_map/ppermute | solution.py:691
  37.2 9.6 %collective-permute-start.14 = (f32[2,168,128]{2,1,0:T(8,128)S(1)}, f32[2,168,128]{2,1,0:T(8,128)S(1)}, u32[]{:S(2)}, u32[]{:S(2)}) collective-permute-start(f32[2,168,128]{2,1,0:T(8,128)S(1)} %get-tuple-element.73), channel_id=1, source_target_pairs={{0,6},{1,7},{2,4},{3,5},{4,2},{5,3},{6,0},{7,1},{8,14},{9,15},{10,... | collective-permute-start | bytes 516104 | tf_op jit(solution)/shard_map/ppermute | solution.py:691
  40.9 6.0 %collective-permute-start.19 = (f32[4,168,128]{2,1,0:T(8,128)S(1)}, f32[4,168,128]{2,1,0:T(8,128)S(1)}, u32[]{:S(2)}, u32[]{:S(2)}) collective-permute-start(f32[4,168,128]{2,1,0:T(8,128)S(1)} %pad_maximum_fusion.1), channel_id=1, source_target_pairs={{0,1},{1,0},{2,3},{3,2},{4,5},{5,4},{6,7},{7,6},{8,9},{9,8},{10,11... | collective-permute-start | bytes 1032200 | tf_op jit(solution)/shard_map/ppermute | solution.py:698
  43.2 9.3 %copy-start = (f32[1,3,5,64,256]{4,3,2,1,0:T(8,128)S(1)}, f32[1,3,5,64,256]{4,3,2,1,0:T(8,128)}, u32[]{:S(2)}) copy-start(f32[1,3,5,64,256]{4,3,2,1,0:T(8,128)} %param.8) | copy-start | bytes 2949124
  46.9 3.2 %collective-permute-start.15 = (f32[4,168,128]{2,1,0:T(8,128)S(1)}, f32[4,168,128]{2,1,0:T(8,128)S(1)}, u32[]{:S(2)}, u32[]{:S(2)}) collective-permute-start(f32[4,168,128]{2,1,0:T(8,128)S(1)} %pad_maximum_fusion), channel_id=1, source_target_pairs={{0,1},{1,0},{2,3},{3,2},{4,5},{5,4},{6,7},{7,6},{8,9},{9,8},{10,11... | collective-permute-start | bytes 1032200 | tf_op jit(solution)/shard_map/ppermute | solution.py:698
  47.5 7.4 %collective-permute-start.20 = (f32[5,16,256]{2,1,0:T(8,128)S(1)}, f32[5,16,256]{2,1,0:T(8,128)S(1)}, u32[]{:S(2)}, u32[]{:S(2)}) collective-permute-start(f32[5,16,256]{2,1,0:T(8,128)S(1)} %get-tuple-element.80), channel_id=1, source_target_pairs={{0,8},{8,0},{16,24},{24,16},{1,9},{9,1},{17,25},{25,17},{2,10},{10... | collective-permute-start | bytes 245768 | tf_op jit(solution)/shard_map/ppermute | solution.py:27
  48.6 6.5 %collective-permute-start.21 = (f32[5,16,256]{2,1,0:T(8,128)S(1)}, f32[5,16,256]{2,1,0:T(8,128)S(1)}, u32[]{:S(2)}, u32[]{:S(2)}) collective-permute-start(f32[5,16,256]{2,1,0:T(8,128)S(1)} %get-tuple-element.81), channel_id=1, source_target_pairs={{0,24},{8,16},{16,8},{24,0},{1,25},{9,17},{17,9},{25,1},{2,26},{10... | collective-permute-start | bytes 245768 | tf_op jit(solution)/shard_map/ppermute | solution.py:27
  50.7 4.2 %collective-permute-start.22 = (f32[5,8,128]{2,1,0:T(8,128)S(1)}, f32[5,8,128]{2,1,0:T(8,128)S(1)}, u32[]{:S(2)}, u32[]{:S(2)}) collective-permute-start(f32[5,8,128]{2,1,0:T(8,128)S(1)} %get-tuple-element.82), channel_id=1, source_target_pairs={{0,7},{1,2},{2,1},{3,4},{4,3},{5,6},{6,5},{7,0},{8,15},{9,10},{10,... | collective-permute-start | bytes 61448 | tf_op jit(solution)/shard_map/ppermute | solution.py:27
  51.9 2.9 %collective-permute-start.23 = (f32[5,8,128]{2,1,0:T(8,128)S(1)}, f32[5,8,128]{2,1,0:T(8,128)S(1)}, u32[]{:S(2)}, u32[]{:S(2)}) collective-permute-start(f32[5,8,128]{2,1,0:T(8,128)S(1)} %get-tuple-element.83), channel_id=1, source_target_pairs={{0,1},{1,0},{2,3},{3,2},{4,5},{5,4},{6,7},{7,6},{8,9},{9,8},{10,11... | collective-permute-start | bytes 61448 | tf_op jit(solution)/shard_map/ppermute | solution.py:27
  55.3 6.9 %collective-permute-start.24 = (f32[5,16,256]{2,1,0:T(8,128)S(1)}, f32[5,16,256]{2,1,0:T(8,128)S(1)}, u32[]{:S(2)}, u32[]{:S(2)}) collective-permute-start(f32[5,16,256]{2,1,0:T(8,128)S(1)} %get-tuple-element.85), channel_id=1, source_target_pairs={{0,8},{8,0},{16,24},{24,16},{1,9},{9,1},{17,25},{25,17},{2,10},{10... | collective-permute-start | bytes 245768 | tf_op jit(solution)/shard_map/ppermute | solution.py:27
  56.2 6.2 %collective-permute-start.25 = (f32[5,16,256]{2,1,0:T(8,128)S(1)}, f32[5,16,256]{2,1,0:T(8,128)S(1)}, u32[]{:S(2)}, u32[]{:S(2)}) collective-permute-start(f32[5,16,256]{2,1,0:T(8,128)S(1)} %get-tuple-element.86), channel_id=1, source_target_pairs={{0,24},{8,16},{16,8},{24,0},{1,25},{9,17},{17,9},{25,1},{2,26},{10... | collective-permute-start | bytes 245768 | tf_op jit(solution)/shard_map/ppermute | solution.py:27
  58.1 4.1 %collective-permute-start.26 = (f32[5,8,128]{2,1,0:T(8,128)S(1)}, f32[5,8,128]{2,1,0:T(8,128)S(1)}, u32[]{:S(2)}, u32[]{:S(2)}) collective-permute-start(f32[5,8,128]{2,1,0:T(8,128)S(1)} %get-tuple-element.87), channel_id=1, source_target_pairs={{0,7},{1,2},{2,1},{3,4},{4,3},{5,6},{6,5},{7,0},{8,15},{9,10},{10,... | collective-permute-start | bytes 61448 | tf_op jit(solution)/shard_map/ppermute | solution.py:27
  58.2 4.0 %collective-permute-start.27 = (f32[5,8,128]{2,1,0:T(8,128)S(1)}, f32[5,8,128]{2,1,0:T(8,128)S(1)}, u32[]{:S(2)}, u32[]{:S(2)}) collective-permute-start(f32[5,8,128]{2,1,0:T(8,128)S(1)} %get-tuple-element.88), channel_id=1, source_target_pairs={{0,1},{1,0},{2,3},{3,2},{4,5},{5,4},{6,7},{7,6},{8,9},{9,8},{10,11... | collective-permute-start | bytes 61448 | tf_op jit(solution)/shard_map/ppermute | solution.py:27
  62.6 6.9 %collective-permute-start.28 = (f32[5,16,256]{2,1,0:T(8,128)S(1)}, f32[5,16,256]{2,1,0:T(8,128)S(1)}, u32[]{:S(2)}, u32[]{:S(2)}) collective-permute-start(f32[5,16,256]{2,1,0:T(8,128)S(1)} %get-tuple-element.90), channel_id=1, source_target_pairs={{0,8},{8,0},{16,24},{24,16},{1,9},{9,1},{17,25},{25,17},{2,10},{10... | collective-permute-start | bytes 245768 | tf_op jit(solution)/shard_map/ppermute | solution.py:27
  63.0 6.5 %collective-permute-start.29 = (f32[5,16,256]{2,1,0:T(8,128)S(1)}, f32[5,16,256]{2,1,0:T(8,128)S(1)}, u32[]{:S(2)}, u32[]{:S(2)}) collective-permute-start(f32[5,16,256]{2,1,0:T(8,128)S(1)} %get-tuple-element.91), channel_id=1, source_target_pairs={{0,24},{8,16},{16,8},{24,0},{1,25},{9,17},{17,9},{25,1},{2,26},{10... | collective-permute-start | bytes 245768 | tf_op jit(solution)/shard_map/ppermute | solution.py:27
  65.4 4.1 %collective-permute-start.30 = (f32[5,8,128]{2,1,0:T(8,128)S(1)}, f32[5,8,128]{2,1,0:T(8,128)S(1)}, u32[]{:S(2)}, u32[]{:S(2)}) collective-permute-start(f32[5,8,128]{2,1,0:T(8,128)S(1)} %get-tuple-element.92), channel_id=1, source_target_pairs={{0,7},{1,2},{2,1},{3,4},{4,3},{5,6},{6,5},{7,0},{8,15},{9,10},{10,... | collective-permute-start | bytes 61448 | tf_op jit(solution)/shard_map/ppermute | solution.py:27
  65.4 4.1 %collective-permute-start.31 = (f32[5,8,128]{2,1,0:T(8,128)S(1)}, f32[5,8,128]{2,1,0:T(8,128)S(1)}, u32[]{:S(2)}, u32[]{:S(2)}) collective-permute-start(f32[5,8,128]{2,1,0:T(8,128)S(1)} %get-tuple-element.93), channel_id=1, source_target_pairs={{0,1},{1,0},{2,3},{3,2},{4,5},{5,4},{6,7},{7,6},{8,9},{9,8},{10,11... | collective-permute-start | bytes 61448 | tf_op jit(solution)/shard_map/ppermute | solution.py:27

commit v5 on v4

--- a/solution.py
+++ b/solution.py
@@ -686,7 +686,7 @@
     ring = ("gy", "gz")
     count = len(values)
     mine = [values[0]] * count
-    for d in range(count - 1, 0, -1):
+    for d in range(1, count):
         pairs = [(s, s ^ (2 * d)) for s in range(2 * count)]
         mine[d] = lax.ppermute(values[d], ring, pairs)
     return mine

time: 70.6 us -> 70.6 us (level)
  no operation moved by 1% of the time
where the time goes in v5:
time: 70.6 us; the launch traced here: 70.4 us
  starting transfers between devices  37.1 us (53%)
  waiting for transfers between devices  16.9 us (24%)
  Pallas kernels  15.5 us (22%)
  between operations  0.86 us (1%)
    ppermute x24, starting transfers between devices, swapped(): return lax.ppermute(value, axis, pairs)  29.1 us
    ppermute x24, waiting for transfers between devices, swapped(): return lax.ppermute(value, axis, pairs)  8.66 us
    ppermute x6, waiting for transfers between devices, send_chips(): mine[d] = lax.ppermute(values[d], ring, pairs)  8.19 us
    ppermute x6, starting transfers between devices, send_chips(): mine[d] = lax.ppermute(values[d], ring, pairs)  7.85 us
    pallas_call x6, Pallas kernels, section(): pl.pallas_call(functools.partial(local_kernel, scale, index, factors, hal...  6.11 us
    pallas_call x2, Pallas kernels, project(): pl.pallas_call(functools.partial(project_kernel, tiles, len(sources), out...  4.41 us
    pallas_call x6, Pallas kernels, section(): pl.pallas_call(functools.partial(finish_kernel, scale, index, len(after),...  1.92 us
  transfers between devices with their start and end apart: 32, of which 13 were waited for; matrix products, arithmetic and copies ran while one was open for 0% of the time, Pallas kernels for 14%

profile of v5, /device:TPU:0, one launch (start us, length us, event | category | flops | bytes accessed | tf_op | source)
XLA Modules:
  0.0 70.4 jit_solution(6842521398840423244)
XLA Ops:
  0.7 1.3 %faces.1 = (f32[5,64,256]{2,1,0:T(8,128)S(1)}, f32[3,5,64,256]{3,2,1,0:T(8,128)S(1)}, f32[5,16,256]{2,1,0:T(8,128)S(1)}, f32[5,16,256]{2,1,0:T(8,128)S(1)}, f32[...) custom-call(f32[1,5,64,256]{3,2,1,0:T(8,128)} %w_hbm.1, f32[1,3,5,64,256]{4,3,2,1,0:T(8,128)} %state_hbm.1), custom_call_target="tpu_custom_call" | custom-call | tf_op jit(solution)/shard_map/faces/pallas_call | solution.py:391
  2.0 3.1 %collective-permute-start = (f32[5,16,256]{2,1,0:T(8,128)S(1)}, f32[5,16,256]{2,1,0:T(8,128)S(1)}, u32[]{:S(2)}, u32[]{:S(2)}) collective-permute-start(f32[5,16,256]{2,1,0:T(8,128)S(1)} %get-tuple-element.50), channel_id=1, source_target_pairs={{0,8},{8,0},{16,24},{24,16},{1,9},{9,1},{17,25},{25,17},{2,10},{10... | collective-permute-start | bytes 245768 | tf_op jit(solution)/shard_map/ppermute | solution.py:27
  5.1 2.5 %collective-permute-start.1 = (f32[5,16,256]{2,1,0:T(8,128)S(1)}, f32[5,16,256]{2,1,0:T(8,128)S(1)}, u32[]{:S(2)}, u32[]{:S(2)}) collective-permute-start(f32[5,16,256]{2,1,0:T(8,128)S(1)} %get-tuple-element.51), channel_id=1, source_target_pairs={{0,24},{8,16},{16,8},{24,0},{1,25},{9,17},{17,9},{25,1},{2,26},{10... | collective-permute-start | bytes 245768 | tf_op jit(solution)/shard_map/ppermute | solution.py:27
  7.6 1.3 %collective-permute-start.2 = (f32[5,8,128]{2,1,0:T(8,128)S(1)}, f32[5,8,128]{2,1,0:T(8,128)S(1)}, u32[]{:S(2)}, u32[]{:S(2)}) collective-permute-start(f32[5,8,128]{2,1,0:T(8,128)S(1)} %get-tuple-element.52), channel_id=1, source_target_pairs={{0,7},{1,2},{2,1},{3,4},{4,3},{5,6},{6,5},{7,0},{8,15},{9,10},{10,... | collective-permute-start | bytes 61448 | tf_op jit(solution)/shard_map/ppermute | solution.py:27
  8.9 0.3 collective-permute-start.3
  9.2 0.7 %local_part.6.base_ref = f32[5,64,256]{2,1,0:T(8,128)S(1)} custom-call(f32[3,5,64,256]{3,2,1,0:T(8,128)S(1)} %get-tuple-element.48.refs_0_.state_ref, f32[5,64,256]{2,1,0:T(8,128)S(1)} %get-tuple-element.49.refs_1_.refs_2_), custom_call_target="tpu_custom_call" | custom-call | flops 6553600 | bytes 983040 | tf_op jit(solution)/shard_map/local_part/pallas_call | solution.py:480
  9.9 1.8 %collective-permute-done.2.yb_ref = f32[5,8,128]{2,1,0:T(8,128)S(1)} collective-permute-done((f32[5,8,128]{2,1,0:T(8,128)S(1)}, f32[5,8,128]{2,1,0:T(8,128)S(1)}, u32[]{:S(2)}, u32[]{:S(2)}) %collective-permute-start.2) | collective-permute-done | bytes 20512 | tf_op jit(solution)/shard_map/ppermute | solution.py:27
  11.9 0.7 collective-permute-start.4
  12.6 2.4 %collective-permute-start.5 = (f32[5,16,256]{2,1,0:T(8,128)S(1)}, f32[5,16,256]{2,1,0:T(8,128)S(1)}, u32[]{:S(2)}, u32[]{:S(2)}) collective-permute-start(f32[5,16,256]{2,1,0:T(8,128)S(1)} %get-tuple-element.56), channel_id=1, source_target_pairs={{0,24},{8,16},{16,8},{24,0},{1,25},{9,17},{17,9},{25,1},{2,26},{10... | collective-permute-start | bytes 245768 | tf_op jit(solution)/shard_map/ppermute | solution.py:27
  15.1 1.6 %collective-permute-start.7 = (f32[5,8,128]{2,1,0:T(8,128)S(1)}, f32[5,8,128]{2,1,0:T(8,128)S(1)}, u32[]{:S(2)}, u32[]{:S(2)}) collective-permute-start(f32[5,8,128]{2,1,0:T(8,128)S(1)} %get-tuple-element.58), channel_id=1, source_target_pairs={{0,1},{1,0},{2,3},{3,2},{4,5},{5,4},{6,7},{7,6},{8,9},{9,8},{10,11... | collective-permute-start | bytes 61448 | tf_op jit(solution)/shard_map/ppermute | solution.py:27
  16.7 0.6 prepare.1
  17.4 0.7 %local_part.7.base_ref = f32[5,64,256]{2,1,0:T(8,128)S(1)} custom-call(f32[3,5,64,256]{3,2,1,0:T(8,128)S(1)} %get-tuple-element.48.refs_0_.state_ref, f32[5,64,256]{2,1,0:T(8,128)S(1)} %get-tuple-element.54.refs_1_.after_ref.refs_3_), custom_call_target="tpu_custom_call" | custom-call | flops 6553600 | bytes 983040 | tf_op jit(solution)/shard_map/local_part/pallas_call | solution.py:480
  18.1 1.1 %collective-permute-done.6.yb_ref = f32[5,8,128]{2,1,0:T(8,128)S(1)} collective-permute-done((f32[5,8,128]{2,1,0:T(8,128)S(1)}, f32[5,8,128]{2,1,0:T(8,128)S(1)}, u32[]{:S(2)}, u32[]{:S(2)}) %collective-permute-start.6) | collective-permute-done | bytes 20512 | tf_op jit(solution)/shard_map/ppermute | solution.py:27
  19.4 0.3 collective-permute-start.8
  19.7 2.0 %collective-permute-start.9 = (f32[5,16,256]{2,1,0:T(8,128)S(1)}, f32[5,16,256]{2,1,0:T(8,128)S(1)}, u32[]{:S(2)}, u32[]{:S(2)}) collective-permute-start(f32[5,16,256]{2,1,0:T(8,128)S(1)} %get-tuple-element.63), channel_id=1, source_target_pairs={{0,24},{8,16},{16,8},{24,0},{1,25},{9,17},{17,9},{25,1},{2,26},{10... | collective-permute-start | bytes 245768 | tf_op jit(solution)/shard_map/ppermute | solution.py:27
  21.9 1.4 %collective-permute-start.11 = (f32[5,8,128]{2,1,0:T(8,128)S(1)}, f32[5,8,128]{2,1,0:T(8,128)S(1)}, u32[]{:S(2)}, u32[]{:S(2)}) collective-permute-start(f32[5,8,128]{2,1,0:T(8,128)S(1)} %get-tuple-element.65), channel_id=1, source_target_pairs={{0,1},{1,0},{2,3},{3,2},{4,5},{5,4},{6,7},{7,6},{8,9},{9,8},{10,11... | collective-permute-start | bytes 61448 | tf_op jit(solution)/shard_map/ppermute | solution.py:27
  23.3 2.5 %local_part.8 = (f32[5,64,256]{2,1,0:T(8,128)S(1)}, f32[64,32,512]{2,1,0:T(8,128)S(1)}) custom-call(f32[3,5,64,256]{3,2,1,0:T(8,128)S(1)} %get-tuple-element.48.refs_0_.state_ref, f32[5,64,256]{2,1,0:T(8,128)S(1)} %get-tuple-element.60.refs_1_, f32[5,64,256]{2,1,0:T(8,128)S(1)} %get-tuple-element.49.refs_1_.refs_2_, ...), custom_call_target="tpu_custom_call" | custom-call | flops 6553600 | bytes 983040 | tf_op jit(solution)/shard_map/local_part/pallas_call | solution.py:480
  26.1 2.2 %project.2 = (f32[2,168,128]{2,1,0:T(8,128)S(1)}, f32[2,168,128]{2,1,0:T(8,128)S(1)}, f32[2,168,128]{2,1,0:T(8,128)S(1)}, f32[2,168,128]{2,1,0:T(8,128)S(1)}, f32[64,32,512]{2,1,0:T(8,128)S(1)}) custom-call(f32[5,64,256]{2,1,0:T(8,128)S(1)} %finish.8.refs_0_, f32[64,32,512]{2,1,0:T(8,128)S(1)} %get-tuple-element.66.refs_1_, ...), custom_call_target="tpu_custom_call" | custom-call | flops 4000000000 | bytes 20971520 | tf_op jit(solution)/shard_map/project/pallas_call | solution.py:603
  28.4 1.7 %collective-permute-start.16 = (f32[2,168,128]{2,1,0:T(8,128)S(1)}, f32[2,168,128]{2,1,0:T(8,128)S(1)}, u32[]{:S(2)}, u32[]{:S(2)}) collective-permute-start(f32[2,168,128]{2,1,0:T(8,128)S(1)} %get-tuple-element.75), channel_id=1, source_target_pairs={{0,2},{1,3},{2,0},{3,1},{4,6},{5,7},{6,4},{7,5},{8,10},{9,11},{10,... | collective-permute-start | bytes 516104 | tf_op jit(solution)/shard_map/ppermute | solution.py:691
  30.0 1.4 %collective-permute-start.17 = (f32[2,168,128]{2,1,0:T(8,128)S(1)}, f32[2,168,128]{2,1,0:T(8,128)S(1)}, u32[]{:S(2)}, u32[]{:S(2)}) collective-permute-start(f32[2,168,128]{2,1,0:T(8,128)S(1)} %get-tuple-element.76), channel_id=1, source_target_pairs={{0,4},{1,5},{2,6},{3,7},{4,0},{5,1},{6,2},{7,3},{8,12},{9,13},{10,... | collective-permute-start | bytes 516104 | tf_op jit(solution)/shard_map/ppermute | solution.py:691
  31.5 0.5 collective-permute-start.18
  31.9 2.2 %project.3 = (f32[2,168,128]{2,1,0:T(8,128)S(1)}, f32[2,168,128]{2,1,0:T(8,128)S(1)}, f32[2,168,128]{2,1,0:T(8,128)S(1)}, f32[2,168,128]{2,1,0:T(8,128)S(1)}, f32[5,64,256]{2,1,0:T(8,128)}) custom-call(f32[5,64,256]{2,1,0:T(8,128)S(1)} %finish.8.refs_0_, f32[64,32,512]{2,1,0:T(8,128)S(1)} %get-tuple-element.68.refs_1_, ...), custom_call_target="tpu_custom_call" | custom-call | flops 4000000000 | bytes 20971520 | tf_op jit(solution)/shard_map/project/pallas_call | solution.py:603
  34.1 1.7 %collective-permute-start.12 = (f32[2,168,128]{2,1,0:T(8,128)S(1)}, f32[2,168,128]{2,1,0:T(8,128)S(1)}, u32[]{:S(2)}, u32[]{:S(2)}) collective-permute-start(f32[2,168,128]{2,1,0:T(8,128)S(1)} %get-tuple-element.71), channel_id=1, source_target_pairs={{0,2},{1,3},{2,0},{3,1},{4,6},{5,7},{6,4},{7,5},{8,10},{9,11},{10,... | collective-permute-start | bytes 516104 | tf_op jit(solution)/shard_map/ppermute | solution.py:691
  35.8 1.4 %collective-permute-start.13 = (f32[2,168,128]{2,1,0:T(8,128)S(1)}, f32[2,168,128]{2,1,0:T(8,128)S(1)}, u32[]{:S(2)}, u32[]{:S(2)}) collective-permute-start(f32[2,168,128]{2,1,0:T(8,128)S(1)} %get-tuple-element.72), channel_id=1, source_target_pairs={{0,4},{1,5},{2,6},{3,7},{4,0},{5,1},{6,2},{7,3},{8,12},{9,13},{10,... | collective-permute-start | bytes 516104 | tf_op jit(solution)/shard_map/ppermute | solution.py:691
  37.2 1.2 %collective-permute-start.14 = (f32[2,168,128]{2,1,0:T(8,128)S(1)}, f32[2,168,128]{2,1,0:T(8,128)S(1)}, u32[]{:S(2)}, u32[]{:S(2)}) collective-permute-start(f32[2,168,128]{2,1,0:T(8,128)S(1)} %get-tuple-element.73), channel_id=1, source_target_pairs={{0,6},{1,7},{2,4},{3,5},{4,2},{5,3},{6,0},{7,1},{8,14},{9,15},{10,... | collective-permute-start | bytes 516104 | tf_op jit(solution)/shard_map/ppermute | solution.py:691
  38.5 2.4 %collective-permute-done.18.refs_3_ = f32[2,168,128]{2,1,0:T(8,128)S(1)} collective-permute-done((f32[2,168,128]{2,1,0:T(8,128)S(1)}, f32[2,168,128]{2,1,0:T(8,128)S(1)}, u32[]{:S(2)}, u32[]{:S(2)}) %collective-permute-start.18) | collective-permute-done | bytes 172064 | tf_op jit(solution)/shard_map/ppermute | solution.py:691
  41.0 2.2 %collective-permute-done.12.refs_1_ = f32[2,168,128]{2,1,0:T(8,128)S(1)} collective-permute-done((f32[2,168,128]{2,1,0:T(8,128)S(1)}, f32[2,168,128]{2,1,0:T(8,128)S(1)}, u32[]{:S(2)}, u32[]{:S(2)}) %collective-permute-start.12) | collective-permute-done | bytes 172064 | tf_op jit(solution)/shard_map/ppermute | solution.py:691
  43.2 1.5 %collective-permute-done.13.refs_2_ = f32[2,168,128]{2,1,0:T(8,128)S(1)} collective-permute-done((f32[2,168,128]{2,1,0:T(8,128)S(1)}, f32[2,168,128]{2,1,0:T(8,128)S(1)}, u32[]{:S(2)}, u32[]{:S(2)}) %collective-permute-start.13) | collective-permute-done | bytes 172064 | tf_op jit(solution)/shard_map/ppermute | solution.py:691
  44.7 2.1 %collective-permute-done.14.refs_3_ = f32[2,168,128]{2,1,0:T(8,128)S(1)} collective-permute-done((f32[2,168,128]{2,1,0:T(8,128)S(1)}, f32[2,168,128]{2,1,0:T(8,128)S(1)}, u32[]{:S(2)}, u32[]{:S(2)}) %collective-permute-start.14) | collective-permute-done | bytes 172064 | tf_op jit(solution)/shard_map/ppermute | solution.py:691
  46.9 0.5 receive.2
  47.5 1.1 %collective-permute-start.20 = (f32[5,16,256]{2,1,0:T(8,128)S(1)}, f32[5,16,256]{2,1,0:T(8,128)S(1)}, u32[]{:S(2)}, u32[]{:S(2)}) collective-permute-start(f32[5,16,256]{2,1,0:T(8,128)S(1)} %get-tuple-element.80), channel_id=1, source_target_pairs={{0,8},{8,0},{16,24},{24,16},{1,9},{9,1},{17,25},{25,17},{2,10},{10... | collective-permute-start | bytes 245768 | tf_op jit(solution)/shard_map/ppermute | solution.py:27
  48.6 1.5 %collective-permute-start.21 = (f32[5,16,256]{2,1,0:T(8,128)S(1)}, f32[5,16,256]{2,1,0:T(8,128)S(1)}, u32[]{:S(2)}, u32[]{:S(2)}) collective-permute-start(f32[5,16,256]{2,1,0:T(8,128)S(1)} %get-tuple-element.81), channel_id=1, source_target_pairs={{0,24},{8,16},{16,8},{24,0},{1,25},{9,17},{17,9},{25,1},{2,26},{10... | collective-permute-start | bytes 245768 | tf_op jit(solution)/shard_map/ppermute | solution.py:27
  50.1 0.6 receive.3
  50.7 1.3 %collective-permute-start.22 = (f32[5,8,128]{2,1,0:T(8,128)S(1)}, f32[5,8,128]{2,1,0:T(8,128)S(1)}, u32[]{:S(2)}, u32[]{:S(2)}) collective-permute-start(f32[5,8,128]{2,1,0:T(8,128)S(1)} %get-tuple-element.82), channel_id=1, source_target_pairs={{0,7},{1,2},{2,1},{3,4},{4,3},{5,6},{6,5},{7,0},{8,15},{9,10},{10,... | collective-permute-start | bytes 61448 | tf_op jit(solution)/shard_map/ppermute | solution.py:27
  51.9 0.6 collective-permute-start.23
  52.5 0.7 %local_part.9.base_ref = f32[5,64,256]{2,1,0:T(8,128)S(1)} custom-call(f32[3,5,64,256]{3,2,1,0:T(8,128)S(1)} %bitcast.4, f32[5,64,256]{2,1,0:T(8,128)S(1)} %get-tuple-element.79.refs_1_.refs_2_), custom_call_target="tpu_custom_call" | custom-call | flops 6553600 | bytes 983040 | tf_op jit(solution)/shard_map/local_part/pallas_call | solution.py:480
  53.2 1.6 %collective-permute-done.22.yb_ref = f32[5,8,128]{2,1,0:T(8,128)S(1)} collective-permute-done((f32[5,8,128]{2,1,0:T(8,128)S(1)}, f32[5,8,128]{2,1,0:T(8,128)S(1)}, u32[]{:S(2)}, u32[]{:S(2)}) %collective-permute-start.22) | collective-permute-done | bytes 20512 | tf_op jit(solution)/shard_map/ppermute | solution.py:27
  55.3 0.9 %collective-permute-start.24 = (f32[5,16,256]{2,1,0:T(8,128)S(1)}, f32[5,16,256]{2,1,0:T(8,128)S(1)}, u32[]{:S(2)}, u32[]{:S(2)}) collective-permute-start(f32[5,16,256]{2,1,0:T(8,128)S(1)} %get-tuple-element.85), channel_id=1, source_target_pairs={{0,8},{8,0},{16,24},{24,16},{1,9},{9,1},{17,25},{25,17},{2,10},{10... | collective-permute-start | bytes 245768 | tf_op jit(solution)/shard_map/ppermute | solution.py:27
  56.2 1.9 %collective-permute-start.25 = (f32[5,16,256]{2,1,0:T(8,128)S(1)}, f32[5,16,256]{2,1,0:T(8,128)S(1)}, u32[]{:S(2)}, u32[]{:S(2)}) collective-permute-start(f32[5,16,256]{2,1,0:T(8,128)S(1)} %get-tuple-element.86), channel_id=1, source_target_pairs={{0,24},{8,16},{16,8},{24,0},{1,25},{9,17},{17,9},{25,1},{2,26},{10... | collective-permute-start | bytes 245768 | tf_op jit(solution)/shard_map/ppermute | solution.py:27
  58.2 1.3 %collective-permute-start.27 = (f32[5,8,128]{2,1,0:T(8,128)S(1)}, f32[5,8,128]{2,1,0:T(8,128)S(1)}, u32[]{:S(2)}, u32[]{:S(2)}) collective-permute-start(f32[5,8,128]{2,1,0:T(8,128)S(1)} %get-tuple-element.88), channel_id=1, source_target_pairs={{0,1},{1,0},{2,3},{3,2},{4,5},{5,4},{6,7},{7,6},{8,9},{9,8},{10,11... | collective-permute-start | bytes 61448 | tf_op jit(solution)/shard_map/ppermute | solution.py:27
  59.5 0.7 %local_part.10.base_ref = f32[5,64,256]{2,1,0:T(8,128)S(1)} custom-call(f32[3,5,64,256]{3,2,1,0:T(8,128)S(1)} %bitcast.6, f32[5,64,256]{2,1,0:T(8,128)S(1)} %get-tuple-element.84.refs_1_.refs_3_), custom_call_target="tpu_custom_call" | custom-call | flops 6553600 | bytes 983040 | tf_op jit(solution)/shard_map/local_part/pallas_call | solution.py:480
  60.3 1.9 %collective-permute-done.26.yb_ref = f32[5,8,128]{2,1,0:T(8,128)S(1)} collective-permute-done((f32[5,8,128]{2,1,0:T(8,128)S(1)}, f32[5,8,128]{2,1,0:T(8,128)S(1)}, u32[]{:S(2)}, u32[]{:S(2)}) %collective-permute-start.26) | collective-permute-done | bytes 20512 | tf_op jit(solution)/shard_map/ppermute | solution.py:27
  62.6 0.4 collective-permute-start.28
  63.0 2.4 %collective-permute-start.29 = (f32[5,16,256]{2,1,0:T(8,128)S(1)}, f32[5,16,256]{2,1,0:T(8,128)S(1)}, u32[]{:S(2)}, u32[]{:S(2)}) collective-permute-start(f32[5,16,256]{2,1,0:T(8,128)S(1)} %get-tuple-element.91), channel_id=1, source_target_pairs={{0,24},{8,16},{16,8},{24,0},{1,25},{9,17},{17,9},{25,1},{2,26},{10... | collective-permute-start | bytes 245768 | tf_op jit(solution)/shard_map/ppermute | solution.py:27
  65.4 1.7 %collective-permute-start.31 = (f32[5,8,128]{2,1,0:T(8,128)S(1)}, f32[5,8,128]{2,1,0:T(8,128)S(1)}, u32[]{:S(2)}, u32[]{:S(2)}) collective-permute-start(f32[5,8,128]{2,1,0:T(8,128)S(1)} %get-tuple-element.93), channel_id=1, source_target_pairs={{0,1},{1,0},{2,3},{3,2},{4,5},{5,4},{6,7},{7,6},{8,9},{9,8},{10,11... | collective-permute-start | bytes 61448 | tf_op jit(solution)/shard_map/ppermute | solution.py:27
  67.1 0.8 %local_part.11.base_ref = f32[5,64,256]{2,1,0:T(8,128)S(1)} custom-call(f32[3,5,64,256]{3,2,1,0:T(8,128)S(1)} %bitcast.8, f32[5,64,256]{2,1,0:T(8,128)S(1)} %get-tuple-element.89.refs_1_, f32[5,64,256]{2,1,0:T(8,128)S(1)} %get-tuple-element.79.refs_1_.refs_2_, f32[5,64,256]{2,1,0:T(8,128)S(1)} %get-tuple-element.84.refs_1_.refs_3_), custom_call_target="tpu_custom_call" | custom-call | flops 6553600 | bytes 983040 | tf_op jit(solution)/shard_map/local_part/pallas_call | solution.py:480
  67.9 1.6 %collective-permute-done.30.yb_ref = f32[5,8,128]{2,1,0:T(8,128)S(1)} collective-permute-done((f32[5,8,128]{2,1,0:T(8,128)S(1)}, f32[5,8,128]{2,1,0:T(8,128)S(1)}, u32[]{:S(2)}, u32[]{:S(2)}) %collective-permute-start.30) | collective-permute-done | bytes 20512 | tf_op jit(solution)/shard_map/ppermute | solution.py:27
  69.5 0.9 %finish.11 = f32[5,64,256]{2,1,0:T(8,128)} custom-call(f32[3,5,64,256]{3,2,1,0:T(8,128)S(1)} %bitcast.9, f32[5,64,256]{2,1,0:T(8,128)S(1)} %local_part.11.base_ref, f32[5,16,256]{2,1,0:T(8,128)S(1)} %collective-permute-done.28.xa_ref, f32[5,16,256]{2,1,0:T(8,128)S(1)} %collective-permute-done.29.xb_ref, f32[5,8,128]{2,1,0:T(8,128)S(1)} %collective-permute-done.30.yb_ref, ...), custom_call_target="tpu_custom_call" | custom-call | tf_op jit(solution)/shard_map/finish/pallas_call | solution.py:493
  (50 shorter events, 2.4 us)
Async XLA Ops:
  0.6 16.1 %copy-start.2 = (s32[1,512]{1,0:T(1,128)S(1)}, s32[1,512]{1,0:T(1,128)}, u32[]{:S(2)}) copy-start(s32[1,512]{1,0:T(1,128)} %local_ref.1) | copy-start | bytes 6148
  0.6 16.1 %copy-start.1 = (s32[1,512,1]{1,2,0:T(1,128)S(1)}, s32[1,512,1]{1,2,0:T(1,128)}, u32[]{:S(2)}) copy-start(s32[1,512,1]{1,2,0:T(1,128)} %param.9) | copy-start | bytes 6148
  2.0 9.7 %collective-permute-start = (f32[5,16,256]{2,1,0:T(8,128)S(1)}, f32[5,16,256]{2,1,0:T(8,128)S(1)}, u32[]{:S(2)}, u32[]{:S(2)}) collective-permute-start(f32[5,16,256]{2,1,0:T(8,128)S(1)} %get-tuple-element.50), channel_id=1, source_target_pairs={{0,8},{8,0},{16,24},{24,16},{1,9},{9,1},{17,25},{25,17},{2,10},{10... | collective-permute-start | bytes 245768 | tf_op jit(solution)/shard_map/ppermute | solution.py:27
  5.1 6.6 %collective-permute-start.1 = (f32[5,16,256]{2,1,0:T(8,128)S(1)}, f32[5,16,256]{2,1,0:T(8,128)S(1)}, u32[]{:S(2)}, u32[]{:S(2)}) collective-permute-start(f32[5,16,256]{2,1,0:T(8,128)S(1)} %get-tuple-element.51), channel_id=1, source_target_pairs={{0,24},{8,16},{16,8},{24,0},{1,25},{9,17},{17,9},{25,1},{2,26},{10... | collective-permute-start | bytes 245768 | tf_op jit(solution)/shard_map/ppermute | solution.py:27
  7.6 4.1 %collective-permute-start.2 = (f32[5,8,128]{2,1,0:T(8,128)S(1)}, f32[5,8,128]{2,1,0:T(8,128)S(1)}, u32[]{:S(2)}, u32[]{:S(2)}) collective-permute-start(f32[5,8,128]{2,1,0:T(8,128)S(1)} %get-tuple-element.52), channel_id=1, source_target_pairs={{0,7},{1,2},{2,1},{3,4},{4,3},{5,6},{6,5},{7,0},{8,15},{9,10},{10,... | collective-permute-start | bytes 61448 | tf_op jit(solution)/shard_map/ppermute | solution.py:27
  8.9 2.8 %collective-permute-start.3 = (f32[5,8,128]{2,1,0:T(8,128)S(1)}, f32[5,8,128]{2,1,0:T(8,128)S(1)}, u32[]{:S(2)}, u32[]{:S(2)}) collective-permute-start(f32[5,8,128]{2,1,0:T(8,128)S(1)} %get-tuple-element.53), channel_id=1, source_target_pairs={{0,1},{1,0},{2,3},{3,2},{4,5},{5,4},{6,7},{7,6},{8,9},{9,8},{10,11... | collective-permute-start | bytes 61448 | tf_op jit(solution)/shard_map/ppermute | solution.py:27
  11.9 7.3 %collective-permute-start.4 = (f32[5,16,256]{2,1,0:T(8,128)S(1)}, f32[5,16,256]{2,1,0:T(8,128)S(1)}, u32[]{:S(2)}, u32[]{:S(2)}) collective-permute-start(f32[5,16,256]{2,1,0:T(8,128)S(1)} %get-tuple-element.55), channel_id=1, source_target_pairs={{0,8},{8,0},{16,24},{24,16},{1,9},{9,1},{17,25},{25,17},{2,10},{10... | collective-permute-start | bytes 245768 | tf_op jit(solution)/shard_map/ppermute | solution.py:27
  12.6 6.5 %collective-permute-start.5 = (f32[5,16,256]{2,1,0:T(8,128)S(1)}, f32[5,16,256]{2,1,0:T(8,128)S(1)}, u32[]{:S(2)}, u32[]{:S(2)}) collective-permute-start(f32[5,16,256]{2,1,0:T(8,128)S(1)} %get-tuple-element.56), channel_id=1, source_target_pairs={{0,24},{8,16},{16,8},{24,0},{1,25},{9,17},{17,9},{25,1},{2,26},{10... | collective-permute-start | bytes 245768 | tf_op jit(solution)/shard_map/ppermute | solution.py:27
  15.1 4.1 %collective-permute-start.6 = (f32[5,8,128]{2,1,0:T(8,128)S(1)}, f32[5,8,128]{2,1,0:T(8,128)S(1)}, u32[]{:S(2)}, u32[]{:S(2)}) collective-permute-start(f32[5,8,128]{2,1,0:T(8,128)S(1)} %get-tuple-element.57), channel_id=1, source_target_pairs={{0,7},{1,2},{2,1},{3,4},{4,3},{5,6},{6,5},{7,0},{8,15},{9,10},{10,... | collective-permute-start | bytes 61448 | tf_op jit(solution)/shard_map/ppermute | solution.py:27
  15.1 4.1 %collective-permute-start.7 = (f32[5,8,128]{2,1,0:T(8,128)S(1)}, f32[5,8,128]{2,1,0:T(8,128)S(1)}, u32[]{:S(2)}, u32[]{:S(2)}) collective-permute-start(f32[5,8,128]{2,1,0:T(8,128)S(1)} %get-tuple-element.58), channel_id=1, source_target_pairs={{0,1},{1,0},{2,3},{3,2},{4,5},{5,4},{6,7},{7,6},{8,9},{9,8},{10,11... | collective-permute-start | bytes 61448 | tf_op jit(solution)/shard_map/ppermute | solution.py:27
  19.4 6.4 %collective-permute-start.8 = (f32[5,16,256]{2,1,0:T(8,128)S(1)}, f32[5,16,256]{2,1,0:T(8,128)S(1)}, u32[]{:S(2)}, u32[]{:S(2)}) collective-permute-start(f32[5,16,256]{2,1,0:T(8,128)S(1)} %get-tuple-element.62), channel_id=1, source_target_pairs={{0,8},{8,0},{16,24},{24,16},{1,9},{9,1},{17,25},{25,17},{2,10},{10... | collective-permute-start | bytes 245768 | tf_op jit(solution)/shard_map/ppermute | solution.py:27
  19.7 6.3 %collective-permute-start.9 = (f32[5,16,256]{2,1,0:T(8,128)S(1)}, f32[5,16,256]{2,1,0:T(8,128)S(1)}, u32[]{:S(2)}, u32[]{:S(2)}) collective-permute-start(f32[5,16,256]{2,1,0:T(8,128)S(1)} %get-tuple-element.63), channel_id=1, source_target_pairs={{0,24},{8,16},{16,8},{24,0},{1,25},{9,17},{17,9},{25,1},{2,26},{10... | collective-permute-start | bytes 245768 | tf_op jit(solution)/shard_map/ppermute | solution.py:27
  21.7 4.1 %collective-permute-start.10 = (f32[5,8,128]{2,1,0:T(8,128)S(1)}, f32[5,8,128]{2,1,0:T(8,128)S(1)}, u32[]{:S(2)}, u32[]{:S(2)}) collective-permute-start(f32[5,8,128]{2,1,0:T(8,128)S(1)} %get-tuple-element.64), channel_id=1, source_target_pairs={{0,7},{1,2},{2,1},{3,4},{4,3},{5,6},{6,5},{7,0},{8,15},{9,10},{10,... | collective-permute-start | bytes 61448 | tf_op jit(solution)/shard_map/ppermute | solution.py:27
  21.9 3.9 %collective-permute-start.11 = (f32[5,8,128]{2,1,0:T(8,128)S(1)}, f32[5,8,128]{2,1,0:T(8,128)S(1)}, u32[]{:S(2)}, u32[]{:S(2)}) collective-permute-start(f32[5,8,128]{2,1,0:T(8,128)S(1)} %get-tuple-element.65), channel_id=1, source_target_pairs={{0,1},{1,0},{2,3},{3,2},{4,5},{5,4},{6,7},{7,6},{8,9},{9,8},{10,11... | collective-permute-start | bytes 61448 | tf_op jit(solution)/shard_map/ppermute | solution.py:27
  28.4 8.9 %collective-permute-start.16 = (f32[2,168,128]{2,1,0:T(8,128)S(1)}, f32[2,168,128]{2,1,0:T(8,128)S(1)}, u32[]{:S(2)}, u32[]{:S(2)}) collective-permute-start(f32[2,168,128]{2,1,0:T(8,128)S(1)} %get-tuple-element.75), channel_id=1, source_target_pairs={{0,2},{1,3},{2,0},{3,1},{4,6},{5,7},{6,4},{7,5},{8,10},{9,11},{10,... | collective-permute-start | bytes 516104 | tf_op jit(solution)/shard_map/ppermute | solution.py:691
  30.0 8.4 %collective-permute-start.17 = (f32[2,168,128]{2,1,0:T(8,128)S(1)}, f32[2,168,128]{2,1,0:T(8,128)S(1)}, u32[]{:S(2)}, u32[]{:S(2)}) collective-permute-start(f32[2,168,128]{2,1,0:T(8,128)S(1)} %get-tuple-element.76), channel_id=1, source_target_pairs={{0,4},{1,5},{2,6},{3,7},{4,0},{5,1},{6,2},{7,3},{8,12},{9,13},{10,... | collective-permute-start | bytes 516104 | tf_op jit(solution)/shard_map/ppermute | solution.py:691
  31.5 9.4 %collective-permute-start.18 = (f32[2,168,128]{2,1,0:T(8,128)S(1)}, f32[2,168,128]{2,1,0:T(8,128)S(1)}, u32[]{:S(2)}, u32[]{:S(2)}) collective-permute-start(f32[2,168,128]{2,1,0:T(8,128)S(1)} %get-tuple-element.77), channel_id=1, source_target_pairs={{0,6},{1,7},{2,4},{3,5},{4,2},{5,3},{6,0},{7,1},{8,14},{9,15},{10,... | collective-permute-start | bytes 516104 | tf_op jit(solution)/shard_map/ppermute | solution.py:691
  34.1 9.0 %collective-permute-start.12 = (f32[2,168,128]{2,1,0:T(8,128)S(1)}, f32[2,168,128]{2,1,0:T(8,128)S(1)}, u32[]{:S(2)}, u32[]{:S(2)}) collective-permute-start(f32[2,168,128]{2,1,0:T(8,128)S(1)} %get-tuple-element.71), channel_id=1, source_target_pairs={{0,2},{1,3},{2,0},{3,1},{4,6},{5,7},{6,4},{7,5},{8,10},{9,11},{10,... | collective-permute-start | bytes 516104 | tf_op jit(solution)/shard_map/ppermute | solution.py:691
  35.8 8.9 %collective-permute-start.13 = (f32[2,168,128]{2,1,0:T(8,128)S(1)}, f32[2,168,128]{2,1,0:T(8,128)S(1)}, u32[]{:S(2)}, u32[]{:S(2)}) collective-permute-start(f32[2,168,128]{2,1,0:T(8,128)S(1)} %get-tuple-element.72), channel_id=1, source_target_pairs={{0,4},{1,5},{2,6},{3,7},{4,0},{5,1},{6,2},{7,3},{8,12},{9,13},{10,... | collective-permute-start | bytes 516104 | tf_op jit(solution)/shard_map/ppermute | solution.py:691
  37.2 9.6 %collective-permute-start.14 = (f32[2,168,128]{2,1,0:T(8,128)S(1)}, f32[2,168,128]{2,1,0:T(8,128)S(1)}, u32[]{:S(2)}, u32[]{:S(2)}) collective-permute-start(f32[2,168,128]{2,1,0:T(8,128)S(1)} %get-tuple-element.73), channel_id=1, source_target_pairs={{0,6},{1,7},{2,4},{3,5},{4,2},{5,3},{6,0},{7,1},{8,14},{9,15},{10,... | collective-permute-start | bytes 516104 | tf_op jit(solution)/shard_map/ppermute | solution.py:691
  40.9 6.0 %collective-permute-start.19 = (f32[4,168,128]{2,1,0:T(8,128)S(1)}, f32[4,168,128]{2,1,0:T(8,128)S(1)}, u32[]{:S(2)}, u32[]{:S(2)}) collective-permute-start(f32[4,168,128]{2,1,0:T(8,128)S(1)} %pad_maximum_fusion.1), channel_id=1, source_target_pairs={{0,1},{1,0},{2,3},{3,2},{4,5},{5,4},{6,7},{7,6},{8,9},{9,8},{10,11... | collective-permute-start | bytes 1032200 | tf_op jit(solution)/shard_map/ppermute | solution.py:698
  43.2 9.3 %copy-start = (f32[1,3,5,64,256]{4,3,2,1,0:T(8,128)S(1)}, f32[1,3,5,64,256]{4,3,2,1,0:T(8,128)}, u32[]{:S(2)}) copy-start(f32[1,3,5,64,256]{4,3,2,1,0:T(8,128)} %param.8) | copy-start | bytes 2949124
  46.9 3.2 %collective-permute-start.15 = (f32[4,168,128]{2,1,0:T(8,128)S(1)}, f32[4,168,128]{2,1,0:T(8,128)S(1)}, u32[]{:S(2)}, u32[]{:S(2)}) collective-permute-start(f32[4,168,128]{2,1,0:T(8,128)S(1)} %pad_maximum_fusion), channel_id=1, source_target_pairs={{0,1},{1,0},{2,3},{3,2},{4,5},{5,4},{6,7},{7,6},{8,9},{9,8},{10,11... | collective-permute-start | bytes 1032200 | tf_op jit(solution)/shard_map/ppermute | solution.py:698
  47.5 7.4 %collective-permute-start.20 = (f32[5,16,256]{2,1,0:T(8,128)S(1)}, f32[5,16,256]{2,1,0:T(8,128)S(1)}, u32[]{:S(2)}, u32[]{:S(2)}) collective-permute-start(f32[5,16,256]{2,1,0:T(8,128)S(1)} %get-tuple-element.80), channel_id=1, source_target_pairs={{0,8},{8,0},{16,24},{24,16},{1,9},{9,1},{17,25},{25,17},{2,10},{10... | collective-permute-start | bytes 245768 | tf_op jit(solution)/shard_map/ppermute | solution.py:27
  48.6 6.5 %collective-permute-start.21 = (f32[5,16,256]{2,1,0:T(8,128)S(1)}, f32[5,16,256]{2,1,0:T(8,128)S(1)}, u32[]{:S(2)}, u32[]{:S(2)}) collective-permute-start(f32[5,16,256]{2,1,0:T(8,128)S(1)} %get-tuple-element.81), channel_id=1, source_target_pairs={{0,24},{8,16},{16,8},{24,0},{1,25},{9,17},{17,9},{25,1},{2,26},{10... | collective-permute-start | bytes 245768 | tf_op jit(solution)/shard_map/ppermute | solution.py:27
  50.7 4.2 %collective-permute-start.22 = (f32[5,8,128]{2,1,0:T(8,128)S(1)}, f32[5,8,128]{2,1,0:T(8,128)S(1)}, u32[]{:S(2)}, u32[]{:S(2)}) collective-permute-start(f32[5,8,128]{2,1,0:T(8,128)S(1)} %get-tuple-element.82), channel_id=1, source_target_pairs={{0,7},{1,2},{2,1},{3,4},{4,3},{5,6},{6,5},{7,0},{8,15},{9,10},{10,... | collective-permute-start | bytes 61448 | tf_op jit(solution)/shard_map/ppermute | solution.py:27
  51.9 2.9 %collective-permute-start.23 = (f32[5,8,128]{2,1,0:T(8,128)S(1)}, f32[5,8,128]{2,1,0:T(8,128)S(1)}, u32[]{:S(2)}, u32[]{:S(2)}) collective-permute-start(f32[5,8,128]{2,1,0:T(8,128)S(1)} %get-tuple-element.83), channel_id=1, source_target_pairs={{0,1},{1,0},{2,3},{3,2},{4,5},{5,4},{6,7},{7,6},{8,9},{9,8},{10,11... | collective-permute-start | bytes 61448 | tf_op jit(solution)/shard_map/ppermute | solution.py:27
  55.3 6.9 %collective-permute-start.24 = (f32[5,16,256]{2,1,0:T(8,128)S(1)}, f32[5,16,256]{2,1,0:T(8,128)S(1)}, u32[]{:S(2)}, u32[]{:S(2)}) collective-permute-start(f32[5,16,256]{2,1,0:T(8,128)S(1)} %get-tuple-element.85), channel_id=1, source_target_pairs={{0,8},{8,0},{16,24},{24,16},{1,9},{9,1},{17,25},{25,17},{2,10},{10... | collective-permute-start | bytes 245768 | tf_op jit(solution)/shard_map/ppermute | solution.py:27
  56.2 6.2 %collective-permute-start.25 = (f32[5,16,256]{2,1,0:T(8,128)S(1)}, f32[5,16,256]{2,1,0:T(8,128)S(1)}, u32[]{:S(2)}, u32[]{:S(2)}) collective-permute-start(f32[5,16,256]{2,1,0:T(8,128)S(1)} %get-tuple-element.86), channel_id=1, source_target_pairs={{0,24},{8,16},{16,8},{24,0},{1,25},{9,17},{17,9},{25,1},{2,26},{10... | collective-permute-start | bytes 245768 | tf_op jit(solution)/shard_map/ppermute | solution.py:27
  58.1 4.1 %collective-permute-start.26 = (f32[5,8,128]{2,1,0:T(8,128)S(1)}, f32[5,8,128]{2,1,0:T(8,128)S(1)}, u32[]{:S(2)}, u32[]{:S(2)}) collective-permute-start(f32[5,8,128]{2,1,0:T(8,128)S(1)} %get-tuple-element.87), channel_id=1, source_target_pairs={{0,7},{1,2},{2,1},{3,4},{4,3},{5,6},{6,5},{7,0},{8,15},{9,10},{10,... | collective-permute-start | bytes 61448 | tf_op jit(solution)/shard_map/ppermute | solution.py:27
  58.2 4.0 %collective-permute-start.27 = (f32[5,8,128]{2,1,0:T(8,128)S(1)}, f32[5,8,128]{2,1,0:T(8,128)S(1)}, u32[]{:S(2)}, u32[]{:S(2)}) collective-permute-start(f32[5,8,128]{2,1,0:T(8,128)S(1)} %get-tuple-element.88), channel_id=1, source_target_pairs={{0,1},{1,0},{2,3},{3,2},{4,5},{5,4},{6,7},{7,6},{8,9},{9,8},{10,11... | collective-permute-start | bytes 61448 | tf_op jit(solution)/shard_map/ppermute | solution.py:27
  62.6 6.9 %collective-permute-start.28 = (f32[5,16,256]{2,1,0:T(8,128)S(1)}, f32[5,16,256]{2,1,0:T(8,128)S(1)}, u32[]{:S(2)}, u32[]{:S(2)}) collective-permute-start(f32[5,16,256]{2,1,0:T(8,128)S(1)} %get-tuple-element.90), channel_id=1, source_target_pairs={{0,8},{8,0},{16,24},{24,16},{1,9},{9,1},{17,25},{25,17},{2,10},{10... | collective-permute-start | bytes 245768 | tf_op jit(solution)/shard_map/ppermute | solution.py:27
  63.0 6.5 %collective-permute-start.29 = (f32[5,16,256]{2,1,0:T(8,128)S(1)}, f32[5,16,256]{2,1,0:T(8,128)S(1)}, u32[]{:S(2)}, u32[]{:S(2)}) collective-permute-start(f32[5,16,256]{2,1,0:T(8,128)S(1)} %get-tuple-element.91), channel_id=1, source_target_pairs={{0,24},{8,16},{16,8},{24,0},{1,25},{9,17},{17,9},{25,1},{2,26},{10... | collective-permute-start | bytes 245768 | tf_op jit(solution)/shard_map/ppermute | solution.py:27
  65.4 4.1 %collective-permute-start.30 = (f32[5,8,128]{2,1,0:T(8,128)S(1)}, f32[5,8,128]{2,1,0:T(8,128)S(1)}, u32[]{:S(2)}, u32[]{:S(2)}) collective-permute-start(f32[5,8,128]{2,1,0:T(8,128)S(1)} %get-tuple-element.92), channel_id=1, source_target_pairs={{0,7},{1,2},{2,1},{3,4},{4,3},{5,6},{6,5},{7,0},{8,15},{9,10},{10,... | collective-permute-start | bytes 61448 | tf_op jit(solution)/shard_map/ppermute | solution.py:27
  65.4 4.1 %collective-permute-start.31 = (f32[5,8,128]{2,1,0:T(8,128)S(1)}, f32[5,8,128]{2,1,0:T(8,128)S(1)}, u32[]{:S(2)}, u32[]{:S(2)}) collective-permute-start(f32[5,8,128]{2,1,0:T(8,128)S(1)} %get-tuple-element.93), channel_id=1, source_target_pairs={{0,1},{1,0},{2,3},{3,2},{4,5},{5,4},{6,7},{7,6},{8,9},{9,8},{10,11... | collective-permute-start | bytes 61448 | tf_op jit(solution)/shard_map/ppermute | solution.py:27
